TPU v7x, 32 devices: a whole 2x2x4 slice. The times are simulated.
32 devices in a mesh: seq: 4 (over z), exp: 8 (over y, x, core).
Axes of the slice: x: 2, y: 2, z: 4, core: 2. Of those that a mesh axis runs over, the one named last changes fastest.
Arguments:
- layer_in: bfloat16 [2, 4096, 768], P(None, ('seq', 'exp')), may hold values from -6 to 6
- mixer_gain: float32 [768], replicated, may hold values from 0.5 to 1.5
- in_proj: bfloat16 [768, 3072], replicated, may hold values from -0.21875 to 0.21875
- conv_weight: float32 [4, 1536], replicated, may hold values from -3 to 3
- conv_bias: float32 [1536], replicated, may hold values from -3 to 3
- state_proj: bfloat16 [1536, 80], replicated, may hold values from -0.15625 to 0.15625
- delta_proj: bfloat16 [48, 1536], replicated, may hold values from -0.875 to 0.875
- delta_bias: float32 [1536], replicated, may hold values from -7 to -3
- decay_log: float32 [16, 1536], replicated, may hold values from -4 to 1.5
- skip_gain: float32 [1536], replicated, may hold values from 0.5 to 1.5
- out_proj: bfloat16 [1536, 768], replicated, may hold values from -0.3125 to 0.3125
- expert_norm: float32 [768], replicated, may hold values from 0.5 to 1.5
- router_weight: float32 [768, 8], replicated, may hold values from -0.15 to 0.15
- expert_up: bfloat16 [8, 768, 3072], P('exp', None, 'seq'), may hold values from -0.21875 to 0.21875
- expert_down: bfloat16 [8, 3072, 768], P('exp', 'seq'), may hold values from -6 to 6
- expert_ids: int32 [2, 4096], P(None, ('seq', 'exp')), may hold values from 0 to 7
- capacity_slot: int32 [2, 4096], P(None, ('seq', 'exp')), may hold values from 0 to 40, as said below
- out_grad: bfloat16 [2, 4096, 768], P(None, ('seq', 'exp')), may hold values from -6 to 6
Outputs:
- layer_out: bfloat16 [2, 4096, 768], P(None, ('seq', 'exp'))
- in_grad: float32 [2, 4096, 768], P(None, ('seq', 'exp'))
- grad_mixer_gain: float32 [768], replicated
- grad_in_proj: float32 [768, 3072], replicated
- grad_conv_weight: float32 [4, 1536], replicated
- grad_conv_bias: float32 [1536], replicated
- grad_state_proj: float32 [1536, 80], replicated
- grad_delta_proj: float32 [48, 1536], replicated
- grad_delta_bias: float32 [1536], replicated
- grad_decay_log: float32 [16, 1536], replicated
- grad_skip_gain: float32 [1536], replicated
- grad_out_proj: float32 [1536, 768], replicated
- grad_expert_norm: float32 [768], replicated
- grad_router: float32 [768, 8], replicated
- grad_expert_up: float32 [8, 768, 3072], P('exp', None, 'seq')
- grad_expert_down: float32 [8, 3072, 768], P('exp', 'seq')
Inputs may be any that keep to these rules, and one draw needn't show every extreme that they name: Each device holds the same 128 positions of every sequence; its 256 tokens are ordered by sequence, then position. capacity_slot is the number of earlier tokens of the same device with the same expert, or 40 where that number is 40 or more (such tokens are dropped).
All inputs are finite; a program needn't handle non-finite values.
Results may differ from a plain program's by a relative error of at most 0.011.
Values may be sent and summed in bfloat16 or wider, within the bound.
A program may use at most 256 MiB of HBM per device.

v0:
```python
import jax
import jax.numpy as jnp
from jax import lax
from jax.sharding import PartitionSpec as P

BLK = 16


EPSILON = 1e-05


def shifted(shard, axis, by):
    devices = lax.axis_size(axis)
    pairs = [(i, i + by) for i in range(devices) if 0 <= i + by < devices]
    return lax.ppermute(shard, axis, pairs)


def entering(shard, axis, combine, identity, reverse):
    devices, mine = (lax.axis_size(axis), lax.axis_index(axis))
    everything = jax.tree.map(lambda part: lax.all_gather(part, axis), shard)
    start = jax.tree.map(
        lambda part, zero: jnp.broadcast_to(jnp.asarray(zero, part.dtype), part.shape),
        shard,
        identity,
    )

    def lap(k, before):
        at = devices - 1 - k if reverse else k
        reached = at > mine if reverse else at < mine
        new = combine(before, jax.tree.map(lambda part: part[at], everything))
        return jax.tree.map(lambda a, b: jnp.where(reached, a, b), new, before)

    return lax.fori_loop(0, devices, lap, start)


def half_dot(left, right):
    return jnp.dot(left, right, preferred_element_type=jnp.float32)


def exact_dot(left, right):
    return jnp.dot(left, right, precision=lax.Precision.HIGHEST, preferred_element_type=jnp.float32)


def rows_dot(left, right, precision=None):
    return lax.dot_general(
        left,
        right,
        (((0,), (0,)), ((), ())),
        precision=precision,
        preferred_element_type=jnp.float32,
    )


def cols_dot(left, right, precision=None):
    return lax.dot_general(
        left,
        right,
        (((1,), (1,)), ((), ())),
        precision=precision,
        preferred_element_type=jnp.float32,
    )


def norm_forward(values, gain_vec):
    scaling = lax.rsqrt(jnp.mean(values * values, axis=-1, keepdims=True) + EPSILON)
    return (values * scaling * gain_vec, scaling)


def norm_backward(values, scaling, gain_vec, incoming):
    normal = values * scaling
    weighted = incoming * gain_vec
    grad_gain = jnp.sum(incoming * normal, axis=0)
    grad_values = scaling * (
        weighted - normal * jnp.mean(weighted * normal, axis=-1, keepdims=True)
    )
    return (grad_values, grad_gain)


def silu_slope(values):
    sigma = jax.nn.sigmoid(values)
    return sigma * (1.0 + values * (1.0 - sigma))


def exact_gelu(values):
    return jax.nn.gelu(values, approximate=False)


def affine_combine(earlier, later):
    return (later[0] * earlier[0], later[0] * earlier[1] + later[1])


def in_blocks(values, block_len):
    return values.reshape((values.shape[0] // block_len, block_len) + values.shape[1:])


def forward_states(
    initial, delta_time, drive_time, in_time, out_time, decay_rates, block_len, want_output
):

    def forward_one_block(state, pieces):
        delta_blk, drive_blk, in_blk, out_blk = pieces
        start_state = state
        outputs = []
        for inner_step in range(block_len):
            decay_now = jnp.exp(delta_blk[inner_step][:, None, :] * decay_rates[None])
            state = (
                decay_now * state
                + in_blk[inner_step][:, :, None] * drive_blk[inner_step][:, None, :]
            )
            if want_output:
                outputs.append(jnp.sum(out_blk[inner_step][:, :, None] * state, axis=1))
        if want_output:
            return (state, (jnp.stack(outputs), start_state))
        return (state, None)

    pieces = tuple(
        (in_blocks(values, block_len) for values in (delta_time, drive_time, in_time, out_time))
    )
    return lax.scan(forward_one_block, initial, pieces)


def gradient_summary(initial, delta_time, out_time, grad_time, decay_rates, block_len):

    def gradient_one_block(adjoint, pieces):
        delta_blk, out_blk, grad_blk = pieces
        for inner_step in reversed(range(block_len)):
            total_adj = adjoint + out_blk[inner_step][:, :, None] * grad_blk[inner_step][:, None, :]
            adjoint = jnp.exp(delta_blk[inner_step][:, None, :] * decay_rates[None]) * total_adj
        return (adjoint, None)

    pieces = tuple((in_blocks(values, block_len) for values in (delta_time, out_time, grad_time)))
    result, unused = lax.scan(gradient_one_block, initial, pieces, reverse=True)
    return result


def backward_states(
    incoming,
    starts,
    delta_time,
    drive_time,
    conv_time,
    in_time,
    out_time,
    grad_time,
    decay_rates,
    block_len,
):

    def backward_one_block(carried, pieces):
        adjoint, decay_acc = carried
        start_state, delta_blk, drive_blk, conv_blk, in_blk, out_blk, grad_blk = pieces
        decays = jnp.exp(delta_blk[:, :, None, :] * decay_rates[None, None])
        state = start_state
        earlier = []
        current = []
        for inner_step in range(block_len):
            earlier.append(state)
            state = (
                decays[inner_step] * state
                + in_blk[inner_step][:, :, None] * drive_blk[inner_step][:, None, :]
            )
            current.append(state)
        adjoints = [None] * block_len
        for inner_step in reversed(range(block_len)):
            total_adj = adjoint + out_blk[inner_step][:, :, None] * grad_blk[inner_step][:, None, :]
            adjoints[inner_step] = total_adj
            adjoint = decays[inner_step] * total_adj
        adj_stack = jnp.stack(adjoints)
        prev_stack = jnp.stack(earlier)
        state_stack = jnp.stack(current)
        exponent_grad = adj_stack * prev_stack * decays
        grad_delta = jnp.sum(
            exponent_grad * decay_rates[None, None]
            + adj_stack * in_blk[:, :, :, None] * conv_blk[:, :, None, :],
            axis=2,
        )
        grad_in = jnp.sum(adj_stack * drive_blk[:, :, None, :], axis=3)
        grad_out = jnp.sum(grad_blk[:, :, None, :] * state_stack, axis=3)
        grad_conv = jnp.sum(adj_stack * in_blk[:, :, :, None], axis=2) * delta_blk
        decay_acc = (
            decay_acc + jnp.sum(exponent_grad * delta_blk[:, :, None, :], axis=(0, 1)) * decay_rates
        )
        return ((adjoint, decay_acc), (grad_delta, grad_in, grad_out, grad_conv))

    pieces = (starts,) + tuple(
        (
            in_blocks(values, block_len)
            for values in (delta_time, drive_time, conv_time, in_time, out_time, grad_time)
        )
    )
    initial = (incoming, jnp.zeros(decay_rates.shape, jnp.float32))
    return lax.scan(backward_one_block, initial, pieces, reverse=True)


def on_device(
    layer_in,
    mixer_gain,
    in_proj,
    conv_weight,
    conv_bias,
    state_proj,
    delta_proj,
    delta_bias,
    decay_log,
    skip_gain,
    out_proj,
    expert_norm,
    router_weight,
    expert_up,
    expert_down,
    expert_ids,
    capacity_slot,
    out_grad,
):
    sequences, piece_len, width = layer_in.shape
    tokens = sequences * piece_len
    taps, inner_width = conv_weight.shape
    low_rank = delta_proj.shape[0]
    states = decay_log.shape[0]
    experts = router_weight.shape[1]
    senders = lax.axis_size("exp")
    capacity = (5 * tokens + 4 * experts - 1) // (4 * experts)
    block_len = BLK

    def time_major(values):
        return values.reshape(sequences, piece_len, values.shape[-1]).transpose(1, 0, 2)

    def token_major(values):
        return (
            values.reshape(piece_len, sequences, values.shape[-1])
            .transpose(1, 0, 2)
            .reshape(tokens, values.shape[-1])
        )

    flat_in = layer_in.reshape(tokens, width).astype(jnp.float32)
    normed_one, scaling_one = norm_forward(flat_in, mixer_gain)
    normed_half = normed_one.astype(jnp.bfloat16)
    projected = half_dot(normed_half, in_proj)
    inner = projected[:, :inner_width]
    gate_half = projected[:, inner_width:]
    inner_seq = inner.reshape(sequences, piece_len, inner_width)
    left_rim = shifted(inner_seq[:, piece_len - (taps - 1) :, :], ("seq", "exp"), 1)
    extended = jnp.concatenate([left_rim, inner_seq], axis=1)
    conv_pre = conv_bias + conv_weight[0] * extended[:, 0:piece_len, :]
    for tap in range(1, taps):
        conv_pre = conv_pre + conv_weight[tap] * extended[:, tap : tap + piece_len, :]
    conv_flat = jax.nn.silu(conv_pre).reshape(tokens, inner_width)
    projections = exact_dot(conv_flat, state_proj.astype(jnp.float32))
    delta_low = projections[:, :low_rank]
    in_coef = projections[:, low_rank : low_rank + states]
    out_coef = projections[:, low_rank + states :]
    delta_pre = exact_dot(delta_low, delta_proj.astype(jnp.float32)) + delta_bias
    delta = jax.nn.softplus(delta_pre)
    decay_rates = -jnp.exp(decay_log)
    delta_time = time_major(delta)
    conv_time = time_major(conv_flat)
    drive_time = delta_time * conv_time
    in_time = time_major(in_coef)
    out_time = time_major(out_coef)
    zeros_state = jnp.zeros((sequences, states, inner_width), jnp.float32)
    ones_state = jnp.ones((sequences, states, inner_width), jnp.float32)
    local_end, unused = forward_states(
        zeros_state, delta_time, drive_time, in_time, out_time, decay_rates, block_len, False
    )
    total_decay = jnp.exp(jnp.sum(delta_time, axis=0)[:, None, :] * decay_rates[None])
    carried = entering(
        (total_decay, local_end), ("seq", "exp"), affine_combine, (ones_state, zeros_state), False
    )
    unused_end, collected = forward_states(
        carried[1], delta_time, drive_time, in_time, out_time, decay_rates, block_len, True
    )
    scan_blocks, starts = collected
    scanned = token_major(scan_blocks.reshape(piece_len, sequences, inner_width))
    mixer_pre = scanned + skip_gain * conv_flat
    gate_act = jax.nn.silu(gate_half)
    mixed = (mixer_pre * gate_act).astype(jnp.bfloat16)
    resid = flat_in + half_dot(mixed, out_proj)
    normed_two, scaling_two = norm_forward(resid, expert_norm)
    routed = normed_two.astype(jnp.bfloat16)
    routed_wide = routed.astype(jnp.float32)
    shares = jax.nn.softmax(exact_dot(routed_wide, router_weight), axis=-1)
    flat_ids = expert_ids.reshape(tokens)
    flat_slot = capacity_slot.reshape(tokens)
    onehot = (flat_ids[:, None] == jnp.arange(experts, dtype=jnp.int32)[None, :]).astype(
        jnp.float32
    )
    gate_vals = jnp.sum(shares * onehot, axis=-1)
    kept = (flat_slot < capacity).astype(jnp.float32)
    target = jnp.where(flat_slot < capacity, flat_ids * capacity + flat_slot, experts * capacity)

    def to_slots(values):
        buffer = jnp.zeros((experts * capacity + 1, width), values.dtype).at[target].set(values)
        return buffer[:-1].reshape(experts, capacity, width)

    def from_slots(buffer):
        padded = jnp.concatenate(
            [buffer.reshape(experts * capacity, width), jnp.zeros((1, width), buffer.dtype)], axis=0
        )
        return padded[target]

    arrived = lax.all_to_all(to_slots(routed), "exp", split_axis=0, concat_axis=0, tiled=True)
    rows = arrived.reshape(senders * capacity, width)
    up_whole, down_whole = (
        lax.all_gather(expert_up, "seq", axis=2, tiled=True),
        lax.all_gather(expert_down, "seq", axis=1, tiled=True),
    )
    pre_act = half_dot(rows, up_whole[0])
    hidden_act, gelu_back = jax.vjp(exact_gelu, pre_act)
    hidden_half = hidden_act.astype(jnp.bfloat16)
    expert_out = half_dot(hidden_half, down_whole[0])
    returned = lax.all_to_all(
        expert_out.astype(jnp.bfloat16).reshape(senders, capacity, width),
        "exp",
        split_axis=0,
        concat_axis=0,
        tiled=True,
    )
    token_out = from_slots(returned).astype(jnp.float32)
    token_weight = kept * gate_vals
    layer_out = (
        (resid + token_weight[:, None] * token_out)
        .astype(jnp.bfloat16)
        .reshape(sequences, piece_len, width)
    )
    grad_top = out_grad.reshape(tokens, width).astype(jnp.float32)
    grad_sent = (token_weight[:, None] * grad_top).astype(jnp.bfloat16)
    grad_rows = lax.all_to_all(
        to_slots(grad_sent), "exp", split_axis=0, concat_axis=0, tiled=True
    ).reshape(senders * capacity, width)
    grad_gate = kept * jnp.sum(grad_top * token_out, axis=-1)
    grad_logits = (grad_gate * gate_vals)[:, None] * (onehot - shares)
    grad_router = rows_dot(routed_wide, grad_logits, lax.Precision.HIGHEST)
    grad_routed = cols_dot(grad_logits, router_weight, lax.Precision.HIGHEST)
    grad_down = rows_dot(hidden_half, grad_rows)
    grad_pre = gelu_back(cols_dot(grad_rows, down_whole[0]))[0].astype(jnp.bfloat16)
    grad_up = rows_dot(rows, grad_pre)
    grad_row_in = cols_dot(grad_pre, up_whole[0]).astype(jnp.bfloat16)
    grad_up_own, grad_down_own = (
        lax.psum_scatter(grad_up[None], "seq", scatter_dimension=2, tiled=True),
        lax.psum_scatter(grad_down[None], "seq", scatter_dimension=1, tiled=True),
    )
    back_rows = lax.all_to_all(
        grad_row_in.reshape(senders, capacity, width),
        "exp",
        split_axis=0,
        concat_axis=0,
        tiled=True,
    )
    grad_routed = grad_routed + from_slots(back_rows).astype(jnp.float32)
    grad_resid_norm, grad_expert_norm = norm_backward(resid, scaling_two, expert_norm, grad_routed)
    grad_resid = grad_top + grad_resid_norm
    grad_mixer = grad_resid.astype(jnp.bfloat16)
    grad_out_proj = rows_dot(mixed, grad_mixer)
    grad_mixed = cols_dot(grad_mixer, out_proj)
    grad_scan = grad_mixed * gate_act
    grad_gate_half = grad_mixed * mixer_pre * silu_slope(gate_half)
    grad_skip_gain = jnp.sum(grad_scan * conv_flat, axis=0)
    grad_time = time_major(grad_scan)
    gradient_first = gradient_summary(
        zeros_state, delta_time, out_time, grad_time, decay_rates, block_len
    )
    carried_back = entering(
        (total_decay, gradient_first),
        ("seq", "exp"),
        affine_combine,
        (ones_state, zeros_state),
        True,
    )
    final_carry, block_grads = backward_states(
        carried_back[1],
        starts,
        delta_time,
        drive_time,
        conv_time,
        in_time,
        out_time,
        grad_time,
        decay_rates,
        block_len,
    )
    grad_decay_log = final_carry[1]
    grad_delta_blocks, grad_in_blocks, grad_out_blocks, grad_conv_blocks = block_grads
    grad_delta = token_major(grad_delta_blocks.reshape(piece_len, sequences, inner_width))
    grad_in_coef = token_major(grad_in_blocks.reshape(piece_len, sequences, states))
    grad_out_coef = token_major(grad_out_blocks.reshape(piece_len, sequences, states))
    grad_conv_act = grad_scan * skip_gain + token_major(
        grad_conv_blocks.reshape(piece_len, sequences, inner_width)
    )
    grad_delta_pre = grad_delta * jax.nn.sigmoid(delta_pre)
    grad_delta_bias = jnp.sum(grad_delta_pre, axis=0)
    grad_delta_proj = rows_dot(delta_low, grad_delta_pre, lax.Precision.HIGHEST)
    grad_delta_low = cols_dot(grad_delta_pre, delta_proj.astype(jnp.float32), lax.Precision.HIGHEST)
    grad_projections = jnp.concatenate([grad_delta_low, grad_in_coef, grad_out_coef], axis=-1)
    grad_state_proj = rows_dot(conv_flat, grad_projections, lax.Precision.HIGHEST)
    grad_conv_act = grad_conv_act + cols_dot(
        grad_projections, state_proj.astype(jnp.float32), lax.Precision.HIGHEST
    )
    grad_conv_pre = grad_conv_act.reshape(sequences, piece_len, inner_width) * silu_slope(conv_pre)
    grad_conv_bias = jnp.sum(grad_conv_pre, axis=(0, 1))
    grad_conv_weight = jnp.stack(
        [
            jnp.sum(grad_conv_pre * extended[:, tap : tap + piece_len, :], axis=(0, 1))
            for tap in range(taps)
        ]
    )
    grad_extended = jnp.zeros_like(extended)
    for tap in range(taps):
        grad_extended = grad_extended.at[:, tap : tap + piece_len, :].add(
            conv_weight[tap] * grad_conv_pre
        )
    rim_back = shifted(
        grad_extended[:, : taps - 1, :].astype(jnp.bfloat16), ("seq", "exp"), -1
    ).astype(jnp.float32)
    grad_inner = grad_extended[:, taps - 1 :, :].at[:, piece_len - (taps - 1) :, :].add(rim_back)
    grad_projected = jnp.concatenate(
        [grad_inner.reshape(tokens, inner_width), grad_gate_half], axis=-1
    ).astype(jnp.bfloat16)
    grad_in_proj = rows_dot(normed_half, grad_projected)
    grad_normed_one = cols_dot(grad_projected, in_proj)
    grad_flat_in, grad_mixer_gain = norm_backward(flat_in, scaling_one, mixer_gain, grad_normed_one)
    in_grad = (grad_resid + grad_flat_in).reshape(sequences, piece_len, width)
    summed = lax.psum(
        (
            grad_mixer_gain,
            grad_in_proj,
            grad_conv_weight,
            grad_conv_bias,
            grad_state_proj,
            grad_delta_proj,
            grad_delta_bias,
            grad_decay_log,
            grad_skip_gain,
            grad_out_proj,
            grad_expert_norm,
            grad_router,
        ),
        ("seq", "exp"),
    )
    return (
        layer_out,
        in_grad,
        summed[0],
        summed[1],
        summed[2],
        summed[3],
        summed[4],
        summed[5],
        summed[6],
        summed[7],
        summed[8],
        summed[9],
        summed[10],
        summed[11],
        grad_up_own,
        grad_down_own,
    )


def solution(mesh):
    placed = (
        P(None, ("seq", "exp"), None),
        P(),
        P(),
        P(),
        P(),
        P(),
        P(),
        P(),
        P(),
        P(),
        P(),
        P(),
        P(),
        P("exp", None, "seq"),
        P("exp", "seq", None),
        P(None, ("seq", "exp")),
        P(None, ("seq", "exp")),
        P(None, ("seq", "exp"), None),
    )
    return jax.shard_map(
        on_device,
        mesh=mesh,
        in_specs=placed,
        out_specs=(
            P(None, ("seq", "exp"), None),
            P(None, ("seq", "exp"), None),
            P(),
            P(),
            P(),
            P(),
            P(),
            P(),
            P(),
            P(),
            P(),
            P(),
            P(),
            P(),
            P("exp", None, "seq"),
            P("exp", "seq", None),
        ),
        check_vma=False,
    )
```

profile of v0, /device:TPU:11, one launch (start us, length us, event | category | flops | bytes accessed | tf_op | source)
XLA Modules:
  0.0 1884.6 jit_solution(18023379698583756436)
XLA Ops:
  10.3 3.9 fusion.298
  15.6 3.7 collective-permute-start
  21.0 5.4 fusion.284
  28.0 2.0 bitcast_multiply_fusion.22
  31.9 2.4 copy.45
  34.3 2.4 copy.47
  37.5 23.4 %while.101 = (s32[]{:T(128)}, f32[2,16,1536]{2,1,0:T(8,128)S(1)}, f32[8,16,2,1536]{3,2,1,0:T(2,128)}, f32[16,1536]{1,0:T(8,128)S(1)}, f32[8,16,2,16]{3,2,1,0:T(2...) while((s32[]{:T(128)}, f32[2,16,1536]{2,1,0:T(8,128)S(1)}, ...), condition=%wide.region_3.4_spmd.clone, body=%wide.region_2.3_spmd.clone.sunk | while | flops 3194898 | bytes 1677835 | solution.py:119
  63.9 69.4 %all-gather.14.cloned.1.call-done = f32[64,16,1536]{2,1,0:T(8,128)} async-done(((f32[2,16,1536]{2,1,0:T(8,128)}), f32[64,16,1536]{2,1,0:T(8,128)}) %all-gather.14.cloned.1.call-update) | async-done | bytes 6291472 | tf_op jit(solution)/shard_map/all_gather | solution.py:20
  133.3 71.5 %all-gather.8.cloned.1.call-done = f32[32,2,16,1536]{3,2,1,0:T(8,128)} async-done(((f32[1,2,16,1536]{3,2,1,0:T(8,128)}), f32[32,2,16,1536]{3,2,1,0:T(8,128)}) %all-gather.8.cloned.1.call-update) | async-done | bytes 6291472 | tf_op jit(solution)/shard_map/all_gather | solution.py:20
  204.8 38.8 %while.102 = (s32[]{:T(128)}, f32[2,16,1536]{2,1,0:T(8,128)S(1)}, s32[]{:T(128)}, f32[32,2,16,1536]{3,2,1,0:T(8,128)}, f32[32,2,16,1536]{3,2,1,0:T(8,128)}, /*index=5*/s32[]{:T(128)}, s32[]{:T(128)}) while((s32[]{:T(128)}, f32[2,16,1536]{2,1,0:T(8,128)S(1)}, s32[]{:T(128)}, f32[32,2,16,1536]{3,2,1,0:T(8,128)}, ...), condition=%wide.region_5.6_spmd.clone, body=%wide.region_4.5_spmd.clone.sunk | while | flops 196612 | bytes 786533 | solution.py:33
  245.3 46.5 %while.100 = (s32[]{:T(128)}, f32[2,16,1536]{2,1,0:T(8,128)S(1)}, f32[8,16,2,1536]{3,2,1,0:T(2,128)}, f32[8,2,16,1536]{3,2,1,0:T(8,128)}, f32[8,16,2,1536]{3,2,1...) while((s32[]{:T(128)}, f32[2,16,1536]{2,1,0:T(8,128)S(1)}, ...), condition=%wide.region_23.24_spmd, body=%wide.region_6.23_spmd.sunk | while | flops 7028753 | bytes 5127193 | solution.py:119
  293.7 2.5 multiply_convert_fusion.2
  298.0 2.5 scatter_custom_fusion
  300.5 1.9 slice.2128
  302.4 5.0 all-to-all-start
  308.3 7.0 all-to-all-done
  315.3 13.4 multiply_convert_fusion
  328.7 52.0 %all-gather.12.cloned.1.call-done = bf16[1,3072,768]{2,1,0:T(8,128)(2,1)} async-done(((bf16[1,768,768]{2,1,0:T(8,128)(2,1)}), bf16[1,3072,768]{2,1,0:T(8,128)(2,1)}) %all-gather.12.cloned.1.call-update) | async-done | bytes 4718608 | tf_op jit(solution)/shard_map/all_gather | solution.py:305
  380.7 5.4 fusion.250
  386.1 4.7 all-to-all-start.1
  391.3 7.4 all-to-all-done.1
  399.8 1.9 gather_fusion
  405.0 2.2 scatter_custom_fusion.1
  407.2 12.1 all_to_all.20
  419.3 7.3 add_convert_fusion
  426.7 2.5 fusion.247
  429.3 5.1 all-to-all-start.3
  434.4 7.9 all-to-all-done.3
  444.1 1.9 gather_fusion.1
  446.0 3.1 multiply_reduce_fusion.25
  449.1 2.4 bitcast_add_fusion.4
  451.5 4.4 multiply_reduce_fusion.20
  455.9 2.4 copy.50
  458.3 18.0 while.103
  477.1 2.4 copy.51
  480.4 66.7 %all-gather.16.cloned.1.call-done = f32[64,16,1536]{2,1,0:T(8,128)} async-done(((f32[2,16,1536]{2,1,0:T(8,128)}), f32[64,16,1536]{2,1,0:T(8,128)}) %all-gather.16.cloned.1.call-update) | async-done | bytes 6291472 | tf_op jit(solution)/shard_map/all_gather | solution.py:20
  547.2 39.0 %while.104 = (s32[]{:T(128)}, f32[2,16,1536]{2,1,0:T(8,128)S(1)}, s32[]{:T(128)}, f32[32,2,16,1536]{3,2,1,0:T(8,128)}, f32[32,2,16,1536]{3,2,1,0:T(8,128)}, /*index=5*/s32[]{:T(128)}, s32[]{:T(128)}, s32[]{:T(128)}, s32[]{:T(128)}) while((s32[]{:T(128)}, f32[2,16,1536]{2,1,0:T(8,128)S(1)}, s32[]{:T(128)}, ...), condition=%wide.region_35.36_spmd.clone, body=%wide.region_34.35_spmd.clone.sunk | while | flops 196616 | bytes 786595 | solution.py:33
  590.8 216.9 %while.105 = (s32[]{:T(128)}, f32[2,16,1536]{2,1,0:T(8,128)S(1)}, f32[16,1536]{1,0:T(8,128)S(1)}, f32[8,16,2,1536]{3,2,1,0:T(2,128)}, f32[8,16,2,16]{3,2,1,0:T(2...) while((s32[]{:T(128)}, f32[2,16,1536]{2,1,0:T(8,128)S(1)}, ...), condition=%wide.region_42.43_spmd.clone, body=%wide.region_36.42_spmd.clone.sunk | while | flops 18676752 | bytes 72655952 | solution.py:192
  610.4 2.7 add_reduce_fusion.2
  637.5 2.7 add_reduce_fusion.2
  664.7 2.7 add_reduce_fusion.2
  691.8 2.7 add_reduce_fusion.2
  718.9 2.7 add_reduce_fusion.2
  746.0 2.7 add_reduce_fusion.2
  773.1 2.7 add_reduce_fusion.2
  800.3 2.7 add_reduce_fusion.2
  815.4 3.8 fusion.285
  822.8 5.0 scatter-add.15
  827.8 2.9 slice_add_fusion.1
  830.7 5.0 scatter-add.16
  838.6 2.1 collective-permute-start.1
  841.5 3.1 collective-permute-done.1
  848.1 5.8 multiply_reduce_fusion.26
  854.0 7.8 convolution_bitcast_fusion
  861.9 8.0 convolution_bitcast_fusion.1
  870.1 4.5 fusion.261
  876.4 1.9 fusion.266
  878.3 5.2 fusion.253
  886.0 89.9 %all-reduce.8.cloned.1.call-done = (f32[768]{0:T(1024)}, f32[4,1536]{1,0:T(4,128)}, f32[1536]{0:T(1024)}, f32[1536]{0:T(1024)}, f32[1536]{0:T(1024)}, /*index=5*/f32[768]{0:T(1024)}, f32[768,8]{0,1:T(8,128)}) async-done(((f32[768]{0:T(1024)}, f32[4,1536]{1,0:T(4,128)}, f32[1536]{0:T(1024)}, f32[1536]{0:T(1024)}, f32[1536]{0:T(1024)}, /*index=5*/f32[768]{0:T(1024)}, f32[768,8]{0,1:T(8,128)}), ...) | async-done | bytes 73744 | tf_op jit(solution)/shard_map/psum | solution.py:422
  975.9 166.1 %reduce-scatter.5.cloned.1.call-done = f32[1,768,768]{2,1,0:T(8,128)} async-done(((f32[1,3072,768]{2,1,0:T(8,128)}), f32[1,768,768]{2,1,0:T(8,128)}) %reduce-scatter.5.cloned.1.call-update) | async-done | bytes 2359312 | tf_op jit(solution)/shard_map/reduce_scatter | solution.py:340
  1142.0 165.2 %reduce-scatter.3.cloned.1.call-done = f32[1,768,768]{2,1,0:T(8,128)} async-done(((f32[1,768,3072]{2,1,0:T(8,128)}), f32[1,768,768]{2,1,0:T(8,128)}) %reduce-scatter.3.cloned.1.call-update) | async-done | bytes 2359312 | tf_op jit(solution)/shard_map/reduce_scatter | solution.py:339
  1307.2 552.2 %all-reduce.10.cloned.1.call-done = (f32[768,3072]{1,0:T(8,128)}, f32[1536,80]{0,1:T(8,128)}, f32[48,1536]{1,0:T(8,128)}, f32[16,1536]{1,0:T(8,128)}, f32[1536,768]{1,0:T(8,128)}) async-done(((f32[768,3072]{1,0:T(8,128)}, f32[1536,80]{0,1:T(8,128)}, f32[48,1536]{1,0:T(8,128)}, f32[16,1536]{1,0:T(8,128)}, f32[1536,768]{1,0:T(8,128)}), (f32[768,3072]{1,0:T(8,128)}, f32[1536,80]{0,1:T(8,128)}, ...) | async-done | bytes 15040528 | tf_op jit(solution)/shard_map/psum | solution.py:422
  1860.9 8.7 copy.200
  1874.2 2.2 copy.208
  (989 shorter events, 418.1 us)
Async XLA Ops:
  7.2 289.9 %copy-start = (bf16[1536,768]{1,0:T(8,128)(2,1)S(1)}, bf16[1536,768]{1,0:T(8,128)(2,1)}, u32[]{:S(2)}) copy-start(bf16[1536,768]{1,0:T(8,128)(2,1)} %param.50) | copy-start | bytes 7077892
  7.2 126.1 %all-gather.14.cloned.1.call-start = ((), (), s32[]{:S(2)}) async-start(), calls=%async_computation.11 | async-start | bytes 6488064 | tf_op jit(solution)/shard_map/all_gather | solution.py:20
  14.3 6.7 copy-start.91
  15.6 4.8 collective-permute-start
  19.4 7.5 copy-start.61
  19.4 7.5 copy-start.63
  19.4 7.5 copy-start.65
  19.4 7.5 copy-start.67
  21.0 5.9 copy-start.50
  37.5 26.2 %copy-start.83 = (s32[2,128]{1,0:T(2,128)S(1)}, s32[2,128]{1,0:T(2,128)}, u32[]{:S(2)}) copy-start(s32[2,128]{1,0:T(2,128)} %param.55) | copy-start | bytes 3076
  37.5 26.2 %copy-start.99 = (s32[2,128]{1,0:T(2,128)S(1)}, s32[2,128]{1,0:T(2,128)}, u32[]{:S(2)}) copy-start(s32[2,128]{1,0:T(2,128)} %param.56) | copy-start | bytes 3076
  61.5 143.3 %all-gather.8.cloned.1.call-start = ((), (), s32[]{:S(2)}) async-start(), calls=%async_computation.6 | async-start | bytes 6488064 | tf_op jit(solution)/shard_map/all_gather | solution.py:20
  62.3 246.0 %all-gather.10.cloned.1.call-start = ((), (), s32[]{:S(2)}) async-start(), calls=%async_computation.7 | async-start | bytes 5898240 | tf_op jit(solution)/shard_map/all_gather | solution.py:304
  63.1 317.6 %all-gather.12.cloned.1.call-start = ((), (), s32[]{:S(2)}) async-start(), calls=%async_computation.8 | async-start | bytes 5898240 | tf_op jit(solution)/shard_map/all_gather | solution.py:305
  298.0 30.7 %copy-start.9 = (f32[256,768]{1,0:T(8,128)}, f32[256,768]{1,0:T(8,128)S(1)}, u32[]{:S(2)}) copy-start(f32[256,768]{1,0:T(8,128)S(1)} %get-tuple-element.1456) | copy-start | bytes 2359300
  302.4 12.9 all-to-all-start
  380.7 10.1 copy-start.29
  380.7 10.1 copy-start.58
  386.1 12.6 all-to-all-start.1
  391.3 54.7 %copy-start.84 = (f32[256]{0:T(256)}, f32[256]{0:T(256)S(1)}, u32[]{:S(2)}) copy-start(f32[256]{0:T(256)S(1)} %fusion.271) | copy-start | bytes 3076
  403.1 42.9 %copy-start.86 = (f32[256]{0:T(256)}, f32[256]{0:T(256)S(1)}, u32[]{:S(2)}) copy-start(f32[256]{0:T(256)S(1)} %get-tuple-element.1452) | copy-start | bytes 3076
  407.2 19.5 %slice-start.2 = ((s8[4718592]{0:T(1024)(128)(4,1)}), s8[4194304]{0:T(1024)(128)(4,1)S(1)}, s32[]{:S(2)}) async-start(s8[4718592]{0:T(1024)(128)(4,1)} %bitcast.963), calls=%async_computation.17 | async-start | bytes 8388608
  419.3 7.4 copy-start.37
  419.3 7.4 slice-start.3
  429.3 12.9 all-to-all-start.3
  434.3 112.8 %all-gather.16.cloned.1.call-start = ((), (), s32[]{:S(2)}) async-start(), calls=%async_computation.12 | async-start | bytes 6488064 | tf_op jit(solution)/shard_map/all_gather | solution.py:20
  451.5 6.8 copy-start.10
  458.3 18.8 copy-start.21
  477.0 498.9 %all-reduce.8.cloned.1.call-start = ((), (), s32[]{:S(2)}) async-start(), calls=%async_computation.13 | async-start | bytes 163840 | tf_op jit(solution)/shard_map/psum | solution.py:422
  597.9 8.2 copy-start.3
  625.1 8.2 copy-start.3
  652.3 8.2 copy-start.3
  679.4 8.2 copy-start.3
  706.5 8.2 copy-start.3
  733.6 8.2 copy-start.3
  760.7 8.2 copy-start.3
  787.8 8.2 copy-start.3
  813.5 5.7 copy-start.69
  813.5 5.7 copy-start.71
  821.4 6.4 copy-start.64
  827.8 8.0 copy-start.62
  835.8 12.3 copy-start.28
  835.8 12.3 copy-start.81
  835.8 12.3 copy-start.89
  837.6 7.0 copy-start.14
  838.6 6.0 collective-permute-start.1
  848.0 5.9 copy-start.31
  848.1 5.9 copy-start.38
  854.0 288.0 %reduce-scatter.5.cloned.1.call-start = ((), (), s32[]{:S(2)}) async-start(), calls=%async_computation.10 | async-start | bytes 11796480 | tf_op jit(solution)/shard_map/reduce_scatter | solution.py:340
  861.9 445.3 %reduce-scatter.3.cloned.1.call-start = ((), (), s32[]{:S(2)}) async-start(), calls=%async_computation.9 | async-start | bytes 11796480 | tf_op jit(solution)/shard_map/reduce_scatter | solution.py:339
  870.0 6.4 copy-start.8
  870.0 6.4 copy-start.70
  870.0 989.4 %all-reduce.10.cloned.1.call-start = ((), (), s32[]{:S(2)}) async-start(), calls=%async_computation.14 | async-start | bytes 30081024 | tf_op jit(solution)/shard_map/psum | solution.py:422
  870.1 6.3 copy-start.52
  870.1 6.3 copy-start.72
  1859.4 14.8 slice-start
  1860.9 8.8 copy-start.80
  1860.9 9.4 copy-start.98
  1860.9 10.0 copy-start.46
  1860.9 10.8 copy-start.49
  1860.9 11.5 copy-start.97
  1860.9 12.1 copy-start.60
  1860.9 12.7 copy-start.96
  1860.9 13.3 slice-start.1
  (78 other events, 181.5 us)
Sparse Core Ops, SparseCore 0:
  61.7 71.6 all-gather.13
  136.8 68.0 all-gather.7
  206.4 84.9 all-gather.9
  292.8 87.8 all-gather.11
  477.1 69.9 all-gather.15
  854.1 121.7 all-reduce.7
  978.9 163.0 reduce-scatter.4
  1145.0 162.1 reduce-scatter.2
  1315.9 543.4 all-reduce.9
where the time goes:
time: 1900 us; the launch traced here: 1880 us
  waiting for transfers between devices  1260 us (66%)
  other arithmetic  280 us (15%)
  local copies, waits for them, and re-layouts  205 us (11%)
  matrix products  85.1 us (4%)
  starting transfers between devices  21.1 us (1%)
    psum x2, waiting for transfers between devices, on_device(): lax.psum((grad_mixer_gain, grad_in_proj, grad_conv_weight, grad_conv_bias...  642 us
    all_gather x3, waiting for transfers between devices, entering(): everything = jax.tree.map(lambda part: lax.all_gather(part, axis), shard)  208 us
    reduce_scatter x1, waiting for transfers between devices, on_device(): lax.psum_scatter(grad_down[None], 'seq', scatter_dimension=1, tiled=True)  166 us
    reduce_scatter x1, waiting for transfers between devices, on_device(): lax.psum_scatter(grad_up[None], 'seq', scatter_dimension=2, tiled=True)  165 us
    while x128, other arithmetic  86.4 us
    select_n x64, other arithmetic, lap(): return jax.tree.map(lambda a, b: jnp.where(reached, a, b), new, before)  76 us
    all_gather x1, waiting for transfers between devices, on_device(): lax.all_gather(expert_down, 'seq', axis=1, tiled=True)  52 us
  transfers between devices with their start and end apart: 14, of which 13 were waited for; matrix products, arithmetic and copies ran while one was open for 8% of the time, Pallas kernels for 0%

commit v1 on v0

v1 whole, which is shorter than its diff:
```python
import functools

import jax
import jax.numpy as jnp
from jax import lax
from jax.experimental import pallas as pl
from jax.experimental.pallas import tpu as pltpu
from jax.sharding import PartitionSpec as P

BLK = 16
LANES = 128
GROUP = 512
LOG2E = 1.4426950408889634
LN2 = 0.6931471805599453
VMEM_BYTES = 50 * 1024 * 1024


EPSILON = 1e-05


def shifted(shard, axis, by):
    devices = lax.axis_size(axis)
    pairs = [(i, i + by) for i in range(devices) if 0 <= i + by < devices]
    return lax.ppermute(shard, axis, pairs)


def half_dot(left, right):
    return jnp.dot(left, right, preferred_element_type=jnp.float32)


def exact_dot(left, right):
    return jnp.dot(left, right, precision=lax.Precision.HIGHEST, preferred_element_type=jnp.float32)


def rows_dot(left, right, precision=None):
    return lax.dot_general(
        left,
        right,
        (((0,), (0,)), ((), ())),
        precision=precision,
        preferred_element_type=jnp.float32,
    )


def cols_dot(left, right, precision=None):
    return lax.dot_general(
        left,
        right,
        (((1,), (1,)), ((), ())),
        precision=precision,
        preferred_element_type=jnp.float32,
    )


def norm_forward(values, gain_vec):
    scaling = lax.rsqrt(jnp.mean(values * values, axis=-1, keepdims=True) + EPSILON)
    return (values * scaling * gain_vec, scaling)


def norm_backward(values, scaling, gain_vec, incoming):
    normal = values * scaling
    weighted = incoming * gain_vec
    grad_gain = jnp.sum(incoming * normal, axis=0)
    grad_values = scaling * (
        weighted - normal * jnp.mean(weighted * normal, axis=-1, keepdims=True)
    )
    return (grad_values, grad_gain)


def silu_slope(values):
    sigma = jax.nn.sigmoid(values)
    return sigma * (1.0 + values * (1.0 - sigma))


def exact_gelu(values):
    return jax.nn.gelu(values, approximate=False)


def spread(coef, lanes):
    return jnp.broadcast_to(coef[:, :, None], coef.shape + (lanes,))


def diagonal(coef, block):
    tokens, states = coef.shape
    column = jnp.arange(block * states, dtype=jnp.int32)[None, :] // states
    row = jnp.arange(tokens, dtype=jnp.int32)[:, None] % block
    return jnp.where(column == row, jnp.tile(coef, (1, block)), 0.0).astype(jnp.bfloat16)


def undiagonal(product, block, states):
    tokens = product.shape[0]
    column = jnp.arange(block * states, dtype=jnp.int32)[None, :] // states
    row = jnp.arange(tokens, dtype=jnp.int32)[:, None] % block
    masked = jnp.where(column == row, product, 0.0)
    return jnp.sum(masked.reshape(tokens, block, states), axis=1)


def lane_parts(ref, k, states):
    width = ref.shape[-1]
    return [
        jnp.broadcast_to(ref[k : k + 1, at : at + LANES], (states, LANES))
        for at in range(0, width, LANES)
    ]


def block_of(ref, i):
    return ref.at[pl.ds(pl.multiple_of(i * BLK, BLK), BLK), :]


def rates_of(log_ref):
    rates = -jnp.exp(log_ref[...]) * LOG2E
    return [rates[:, at : at + LANES] for at in range(0, rates.shape[1], LANES)]


def first_pass_kernel(delta_ref, conv_ref, in_ref, log_ref, end_ref, drive):
    steps, width = delta_ref.shape
    states = log_ref.shape[0]
    rates = rates_of(log_ref)
    drive[...] = delta_ref[...] * conv_ref[...]

    def block(i, state):
        state = list(state)
        for k in range(BLK):
            t = i * BLK + k
            inward = in_ref[t]
            deltas = lane_parts(block_of(delta_ref, i), k, states)
            drives = lane_parts(block_of(drive, i), k, states)
            for j in range(width // LANES):
                state[j] = jnp.exp2(deltas[j] * rates[j]) * state[j] + inward * drives[j]
        return tuple(state)

    zero = tuple(jnp.zeros((states, LANES), jnp.float32) for _ in range(width // LANES))
    last = lax.fori_loop(0, steps // BLK, block, zero)
    for j in range(width // LANES):
        end_ref[0, :, j * LANES : (j + 1) * LANES] = last[j]


def second_pass_kernel(
    delta_ref, conv_ref, in_ref, log_ref, start_ref, out_ref, rest_ref, scanned_ref, drive, stack
):
    steps, width = delta_ref.shape
    states = log_ref.shape[0]
    rates = rates_of(log_ref)
    drive[...] = delta_ref[...] * conv_ref[...]

    def block(i, state):
        state = list(state)
        for k in range(BLK):
            t = i * BLK + k
            inward = in_ref[t]
            deltas = lane_parts(block_of(delta_ref, i), k, states)
            drives = lane_parts(block_of(drive, i), k, states)
            for j in range(width // LANES):
                state[j] = jnp.exp2(deltas[j] * rates[j]) * state[j] + inward * drives[j]
                stack[k * states : (k + 1) * states, j * LANES : (j + 1) * LANES] = state[j].astype(
                    jnp.bfloat16
                )
        rows = pl.ds(pl.multiple_of(i * BLK, BLK), BLK)
        both = jnp.concatenate([out_ref[rows, :], rest_ref[rows, :]], axis=0)
        product = jnp.dot(both, stack[...], preferred_element_type=jnp.float32)
        scanned_ref[rows, :] = product[:BLK] + product[BLK:]
        return tuple(state)

    begin = tuple(start_ref[0, :, j * LANES : (j + 1) * LANES] for j in range(width // LANES))
    lax.fori_loop(0, steps // BLK, block, begin)


def back_summary_kernel(delta_ref, grad_ref, out_ref, log_ref, end_ref):
    steps, width = delta_ref.shape
    states = log_ref.shape[0]
    rates = rates_of(log_ref)
    blocks = steps // BLK

    def block(i, state):
        state = list(state)
        for k in reversed(range(BLK)):
            t = (blocks - 1 - i) * BLK + k
            outward = out_ref[t]
            deltas = lane_parts(block_of(delta_ref, blocks - 1 - i), k, states)
            grads = lane_parts(block_of(grad_ref, blocks - 1 - i), k, states)
            for j in range(width // LANES):
                state[j] = jnp.exp2(deltas[j] * rates[j]) * (state[j] + outward * grads[j])
        return tuple(state)

    zero = tuple(jnp.zeros((states, LANES), jnp.float32) for _ in range(width // LANES))
    last = lax.fori_loop(0, blocks, block, zero)
    for j in range(width // LANES):
        end_ref[0, :, j * LANES : (j + 1) * LANES] = last[j]


def backward_kernel(
    delta_ref,
    conv_ref,
    grad_ref,
    in_ref,
    out_ref,
    in_diag_ref,
    log_ref,
    start_ref,
    finish_ref,
    grad_delta_ref,
    grad_conv_ref,
    grad_in_ref,
    grad_out_ref,
    grad_log_ref,
    drive,
    decays,
    carried,
    stack,
    slope,
):
    steps, width = delta_ref.shape
    states = log_ref.shape[0]
    parts = width // LANES
    rates = rates_of(log_ref)
    blocks = steps // BLK
    drive[...] = delta_ref[...] * conv_ref[...]
    first = pl.program_id(1) == 0

    def forward(i, state):
        state = list(state)
        for k in range(BLK):
            t = i * BLK + k
            inward = in_ref[t]
            deltas = lane_parts(block_of(delta_ref, i), k, states)
            drives = lane_parts(block_of(drive, i), k, states)
            for j in range(parts):
                at = slice(j * LANES, (j + 1) * LANES)
                decay = jnp.exp2(deltas[j] * rates[j])
                kept = decay * state[j]
                decays[t, :, at] = decay
                carried[t, :, at] = kept
                state[j] = kept + inward * drives[j]
                stack[k * states : (k + 1) * states, at] = state[j].astype(jnp.bfloat16)
        rows = pl.ds(pl.multiple_of(i * BLK, BLK), BLK)
        partial = cols_dot(grad_ref[rows, :].astype(jnp.bfloat16), stack[...])

        @pl.when(first)
        def _():
            grad_out_ref[rows, :] = partial

        @pl.when(jnp.logical_not(first))
        def _():
            grad_out_ref[rows, :] += partial

        return tuple(state)

    begin = tuple(start_ref[0, :, j * LANES : (j + 1) * LANES] for j in range(parts))
    lax.fori_loop(0, blocks, forward, begin)
    column = lax.broadcasted_iota(jnp.int32, (BLK, BLK * states), 1) // states
    row = lax.broadcasted_iota(jnp.int32, (BLK, BLK * states), 0)
    ones = jnp.where(column == row, 1.0, 0.0).astype(jnp.bfloat16)

    def backward(i, state):
        adjoint, gathered = list(state[:parts]), list(state[parts:])
        for k in reversed(range(BLK)):
            t = (blocks - 1 - i) * BLK + k
            outward = out_ref[t]
            deltas = lane_parts(block_of(delta_ref, blocks - 1 - i), k, states)
            grads = lane_parts(block_of(grad_ref, blocks - 1 - i), k, states)
            for j in range(parts):
                at = slice(j * LANES, (j + 1) * LANES)
                whole = adjoint[j] + outward * grads[j]
                exponent = whole * carried[t, :, at]
                gathered[j] = gathered[j] + exponent * deltas[j]
                slope[k * states : (k + 1) * states, at] = (exponent * rates[j]).astype(
                    jnp.bfloat16
                )
                stack[k * states : (k + 1) * states, at] = whole.astype(jnp.bfloat16)
                adjoint[j] = decays[t, :, at] * whole
        rows = pl.ds(pl.multiple_of((blocks - 1 - i) * BLK, BLK), BLK)
        driven = jnp.dot(in_diag_ref[rows, :], stack[...], preferred_element_type=jnp.float32)
        summed = jnp.dot(ones, slope[...], preferred_element_type=jnp.float32) * LN2
        grad_delta_ref[rows, :] = summed + driven * conv_ref[rows, :]
        grad_conv_ref[rows, :] = driven * delta_ref[rows, :]
        partial = cols_dot(drive[rows, :].astype(jnp.bfloat16), stack[...])

        @pl.when(first)
        def _():
            grad_in_ref[rows, :] = partial

        @pl.when(jnp.logical_not(first))
        def _():
            grad_in_ref[rows, :] += partial

        return tuple(adjoint + gathered)

    ends = tuple(finish_ref[0, :, j * LANES : (j + 1) * LANES] for j in range(parts))
    zero = tuple(jnp.zeros((states, LANES), jnp.float32) for _ in range(parts))
    last = lax.fori_loop(0, blocks, backward, ends + zero)
    for j in range(parts):
        grad_log_ref[0, :, j * LANES : (j + 1) * LANES] = last[parts + j] * rates[j] * LN2


def scan_call(kernel, name, sequences, states, operands, results, scratch):
    tokens, width = next(value.shape for kind, value in operands if kind == "wide")
    steps = tokens // sequences
    specs = {
        "wide": pl.BlockSpec((steps, GROUP), lambda q, j: (q, j)),
        "spread": pl.BlockSpec((steps, states, LANES), lambda q, j: (q, 0, 0)),
        "narrow": pl.BlockSpec((steps, BLK * states), lambda q, j: (q, 0)),
        "rates": pl.BlockSpec((states, GROUP), lambda q, j: (0, j)),
        "state": pl.BlockSpec((1, states, GROUP), lambda q, j: (q, 0, j)),
    }
    shapes = {
        "wide": (tokens, width),
        "narrow": (tokens, BLK * states),
        "state": (sequences, states, width),
    }
    return pl.pallas_call(
        kernel,
        name=name,
        grid=(sequences, width // GROUP),
        in_specs=[specs[kind] for kind, _ in operands],
        out_specs=[specs[kind] for kind in results],
        out_shape=[jax.ShapeDtypeStruct(shapes[kind], jnp.float32) for kind in results],
        scratch_shapes=scratch,
        compiler_params=pltpu.CompilerParams(
            dimension_semantics=("arbitrary", "arbitrary"), vmem_limit_bytes=VMEM_BYTES
        ),
        cost_estimate=pl.CostEstimate(
            flops=20 * tokens * states * width,
            transcendentals=tokens * states * width,
            bytes_accessed=16 * tokens * width,
        ),
    )(*(value for _, value in operands))


MESH = pl.DeviceIdType.MESH


def remote(src, dst, send, arrive, axis, peer):
    return pltpu.make_async_remote_copy(
        src_ref=src,
        dst_ref=dst,
        send_sem=send,
        recv_sem=arrive,
        device_id={axis: peer},
        device_id_type=MESH,
    )


def greet(axes):
    barrier = pltpu.get_barrier_semaphore()
    total = 0
    for axis, size in axes:
        mine = lax.axis_index(axis)
        for k in range(1, size):
            pl.semaphore_signal(
                barrier, inc=1, device_id={axis: lax.rem(mine + k, size)}, device_id_type=MESH
            )
        total += size - 1
    pl.semaphore_wait(barrier, total)


def exchange_kernel(
    reverse,
    planes,
    members,
    end_ref,
    sum_ref,
    rates_ref,
    carry_ref,
    packed,
    landed,
    summary,
    totals,
    starts,
    carries,
    send_one,
    recv_one,
    send_two,
    recv_two,
    send_three,
    recv_three,
):
    sequences, states, width = end_ref.shape
    rows = sequences * states // members
    plane, member = lax.axis_index("seq"), lax.axis_index("exp")
    rates = -jnp.exp(rates_ref[...])
    for i in range(members):
        q, n = (i * rows) // states, (i * rows) % states
        packed[i, :rows] = end_ref[q, n : n + rows]
        packed[i, rows:] = sum_ref[q : q + 1]
    greet((("seq", planes), ("exp", members)))
    for k in range(1, members):
        other = lax.rem(member + k, members)
        remote(
            packed.at[other],
            landed.at[member],
            send_one.at[k],
            recv_one.at[member],
            "exp",
            other,
        ).start()
    landed[member] = packed[member]
    for k in range(1, members):
        other = lax.rem(member + k, members)
        remote(
            packed.at[other], landed.at[other], send_one.at[k], recv_one.at[other], "exp", other
        ).wait()
    order = range(members)[::-1] if reverse else range(members)
    plane_order = range(planes)[::-1] if reverse else range(planes)

    def through(piece, before):
        return jnp.exp(piece[rows:] * rates) * before + piece[:rows]

    state = jnp.zeros((rows, width), jnp.float32)
    total = jnp.zeros((1, width), jnp.float32)
    for i in order:
        piece = landed[i]
        state = through(piece, state)
        total = total + piece[rows:]
    summary[:rows] = state
    summary[rows:] = total
    for k in range(1, planes):
        other = lax.rem(plane + k, planes)
        remote(
            summary, totals.at[plane], send_two.at[k], recv_two.at[plane], "seq", other
        ).start()
    totals[plane] = summary[...]
    for k in range(1, planes):
        other = lax.rem(plane + k, planes)
        remote(summary, totals.at[other], send_two.at[k], recv_two.at[other], "seq", other).wait()
    state = jnp.zeros((rows, width), jnp.float32)
    for s in plane_order:
        reached = plane < s if reverse else plane > s
        state = jnp.where(reached, through(totals[s], state), state)
    for i in order:
        starts[i] = state
        state = through(landed[i], state)
    for k in range(1, members):
        other = lax.rem(member + k, members)
        remote(
            starts.at[other],
            carries.at[member],
            send_three.at[k],
            recv_three.at[member],
            "exp",
            other,
        ).start()
    carries[member] = starts[member]
    for k in range(1, members):
        other = lax.rem(member + k, members)
        remote(
            starts.at[other],
            carries.at[other],
            send_three.at[k],
            recv_three.at[other],
            "exp",
            other,
        ).wait()
    for i in range(members):
        q, n = (i * rows) // states, (i * rows) % states
        carry_ref[q, n : n + rows] = carries[i]


def exchange(local_end, delta_sum, decay_log, reverse):
    sequences, states, width = local_end.shape
    planes, members = lax.axis_size("seq"), lax.axis_size("exp")
    rows = sequences * states // members
    first_row = lax.rem(lax.axis_index("exp") * rows, states)
    own_rates = lax.dynamic_slice(decay_log, (first_row, 0), (rows, width))
    vmem = pl.BlockSpec(memory_space=pltpu.VMEM)
    piece = (rows + 1, width)
    return pl.pallas_call(
        functools.partial(exchange_kernel, reverse, planes, members),
        name="state_exchange_back" if reverse else "state_exchange",
        in_specs=[vmem] * 3,
        out_specs=vmem,
        out_shape=jax.ShapeDtypeStruct(local_end.shape, jnp.float32),
        scratch_shapes=[
            pltpu.VMEM((members,) + piece, jnp.float32),
            pltpu.VMEM((members,) + piece, jnp.float32),
            pltpu.VMEM(piece, jnp.float32),
            pltpu.VMEM((planes,) + piece, jnp.float32),
            pltpu.VMEM((members, rows, width), jnp.float32),
            pltpu.VMEM((members, rows, width), jnp.float32),
            pltpu.SemaphoreType.DMA((members,)),
            pltpu.SemaphoreType.DMA((members,)),
            pltpu.SemaphoreType.DMA((planes,)),
            pltpu.SemaphoreType.DMA((planes,)),
            pltpu.SemaphoreType.DMA((members,)),
            pltpu.SemaphoreType.DMA((members,)),
        ],
        compiler_params=pltpu.CompilerParams(
            collective_id=2 if reverse else 1,
            has_side_effects=True,
            vmem_limit_bytes=VMEM_BYTES,
        ),
        cost_estimate=pl.CostEstimate(flops=10**6, transcendentals=10**5, bytes_accessed=2 * 10**7),
    )(local_end, delta_sum, own_rates)


def total_kernel(planes, chips, count, *refs):
    given, results = refs[:count], refs[count : 2 * count]
    halves, slots, sums, finals = (refs[(2 + i) * count : (3 + i) * count] for i in range(4))
    sends, arrivals = refs[6 * count : 6 * count + 6], refs[6 * count + 6 :]
    plane, member = lax.axis_index("seq"), lax.axis_index("exp")
    chip, core = member // 2, lax.rem(member, 2)
    partner = member + 1 - 2 * core
    barrier = pltpu.get_barrier_semaphore()
    pl.semaphore_signal(barrier, inc=1, device_id={"exp": partner}, device_id_type=MESH)

    def chip_peer(k):
        other = lax.rem(chip + k, chips)
        return other, other * 2 + core

    def plane_peer(k):
        return lax.rem(plane + k, planes)

    for k in range(1, chips):
        pl.semaphore_signal(
            barrier, inc=1, device_id={"exp": chip_peer(k)[1]}, device_id_type=MESH
        )
    for k in range(1, planes):
        pl.semaphore_signal(
            barrier, inc=1, device_id={"seq": plane_peer(k)}, device_id_type=MESH
        )
    pl.semaphore_wait(barrier, chips + planes - 1)

    def pair_half(i):
        return remote(
            given[i].at[1 - core], halves[i], sends[0].at[i], arrivals[0].at[i], "exp", partner
        )

    def scatter_chip(i, k, arriving):
        other, device = chip_peer(k)
        slot = other if arriving else chip
        return remote(
            halves[i].at[other],
            slots[i].at[slot],
            sends[1].at[i, k],
            arrivals[1].at[i, slot],
            "exp",
            device,
        )

    def scatter_plane(i, k, arriving):
        other = plane_peer(k)
        slot = other if arriving else plane
        return remote(
            sums[i].at[other],
            finals[i].at[slot],
            sends[2].at[i, k],
            arrivals[2].at[i, slot],
            "seq",
            other,
        )

    def gather_plane(i, k, arriving):
        other = plane_peer(k)
        slot = other if arriving else plane
        return remote(
            results[i].at[core, chip, plane],
            results[i].at[core, chip, slot],
            sends[3].at[i, k],
            arrivals[3].at[i, slot],
            "seq",
            other,
        )

    def gather_chip(i, k, arriving):
        other, device = chip_peer(k)
        slot = other if arriving else chip
        return remote(
            results[i].at[core, chip],
            results[i].at[core, slot],
            sends[4].at[i, k],
            arrivals[4].at[i, slot],
            "exp",
            device,
        )

    def pair_gather(i, k, arriving):
        other = lax.rem(chip + k, chips)
        half = 1 - core if arriving else core
        return remote(
            results[i].at[core, other],
            results[i].at[half, other],
            sends[5].at[i, k],
            arrivals[5].at[i, other],
            "exp",
            partner,
        )

    wide, half = jnp.float32, jnp.bfloat16
    for i in range(count):
        pair_half(i).start()
    for i in range(count):
        pair_half(i).wait()
        halves[i][...] = (given[i][core].astype(wide) + halves[i][...].astype(wide)).astype(half)
        for k in range(1, chips):
            scatter_chip(i, k, False).start()
        slots[i][chip] = halves[i][chip]
    for i in range(count):
        for k in range(1, chips):
            scatter_chip(i, k, True).wait_recv()
        added = slots[i][0].astype(wide)
        for k in range(1, chips):
            added = added + slots[i][k].astype(wide)
        sums[i][...] = added.astype(half)
        for k in range(1, planes):
            scatter_plane(i, k, False).start()
        finals[i][plane] = sums[i][plane]
    for i in range(count):
        for k in range(1, planes):
            scatter_plane(i, k, True).wait_recv()
        added = finals[i][0].astype(wide)
        for k in range(1, planes):
            added = added + finals[i][k].astype(wide)
        results[i][core, chip, plane] = added.astype(half)
        for k in range(1, planes):
            gather_plane(i, k, False).start()
    for i in range(count):
        for k in range(1, planes):
            gather_plane(i, k, True).wait_recv()
        for k in range(1, chips):
            gather_chip(i, k, False).start()
        pair_gather(i, 0, False).start()
    for i in range(count):
        for k in range(1, chips):
            gather_chip(i, k, True).wait_recv()
            pair_gather(i, k, False).start()
    for i in range(count):
        for k in range(chips):
            pair_gather(i, k, True).wait_recv()
            pair_gather(i, k, False).wait_send()
        for k in range(1, chips):
            scatter_chip(i, k, False).wait_send()
            gather_chip(i, k, False).wait_send()
        for k in range(1, planes):
            scatter_plane(i, k, False).wait_send()
            gather_plane(i, k, False).wait_send()


def total(arrays, collective_id, name):
    planes, members = lax.axis_size("seq"), lax.axis_size("exp")
    chips, count = members // 2, len(arrays)
    shaped = [
        value.reshape((2, chips, planes, value.shape[0] // (members * planes), value.shape[1]))
        for value in arrays
    ]
    tails = [value.shape[3:] for value in shaped]
    vmem = pl.BlockSpec(memory_space=pltpu.VMEM)

    def scratch(*lead):
        return [pltpu.VMEM(lead + tail, jnp.bfloat16) for tail in tails]

    semaphores = [
        pltpu.SemaphoreType.DMA((count,)),
        pltpu.SemaphoreType.DMA((count, chips)),
        pltpu.SemaphoreType.DMA((count, planes)),
        pltpu.SemaphoreType.DMA((count, planes)),
        pltpu.SemaphoreType.DMA((count, chips)),
        pltpu.SemaphoreType.DMA((count, chips)),
    ]
    results = pl.pallas_call(
        functools.partial(total_kernel, planes, chips, count),
        name=name,
        in_specs=[vmem] * count,
        out_specs=[vmem] * count,
        out_shape=[jax.ShapeDtypeStruct(value.shape, jnp.bfloat16) for value in shaped],
        scratch_shapes=scratch(chips, planes)
        + scratch(chips, planes)
        + scratch(planes)
        + scratch(planes)
        + semaphores
        + semaphores,
        compiler_params=pltpu.CompilerParams(
            collective_id=collective_id, has_side_effects=True, vmem_limit_bytes=VMEM_BYTES
        ),
        cost_estimate=pl.CostEstimate(flops=10**7, transcendentals=0, bytes_accessed=10**8),
    )(*shaped)
    return [result.reshape(value.shape) for result, value in zip(results, arrays)]


def on_device(
    layer_in,
    mixer_gain,
    in_proj,
    conv_weight,
    conv_bias,
    state_proj,
    delta_proj,
    delta_bias,
    decay_log,
    skip_gain,
    out_proj,
    expert_norm,
    router_weight,
    expert_up,
    expert_down,
    expert_ids,
    capacity_slot,
    out_grad,
):
    sequences, piece_len, width = layer_in.shape
    tokens = sequences * piece_len
    taps, inner_width = conv_weight.shape
    low_rank = delta_proj.shape[0]
    states = decay_log.shape[0]
    experts = router_weight.shape[1]
    senders = lax.axis_size("exp")
    capacity = (5 * tokens + 4 * experts - 1) // (4 * experts)
    flat_in = layer_in.reshape(tokens, width).astype(jnp.float32)
    normed_one, scaling_one = norm_forward(flat_in, mixer_gain)
    normed_half = normed_one.astype(jnp.bfloat16)
    projected = half_dot(normed_half, in_proj)
    inner = projected[:, :inner_width]
    gate_half = projected[:, inner_width:]
    inner_seq = inner.reshape(sequences, piece_len, inner_width)
    left_rim = shifted(inner_seq[:, piece_len - (taps - 1) :, :], ("seq", "exp"), 1)
    extended = jnp.concatenate([left_rim, inner_seq], axis=1)
    conv_pre = conv_bias + conv_weight[0] * extended[:, 0:piece_len, :]
    for tap in range(1, taps):
        conv_pre = conv_pre + conv_weight[tap] * extended[:, tap : tap + piece_len, :]
    conv_flat = jax.nn.silu(conv_pre).reshape(tokens, inner_width)
    projections = exact_dot(conv_flat, state_proj.astype(jnp.float32))
    delta_low = projections[:, :low_rank]
    in_coef = projections[:, low_rank : low_rank + states]
    out_coef = projections[:, low_rank + states :]
    delta_pre = exact_dot(delta_low, delta_proj.astype(jnp.float32)) + delta_bias
    delta = jax.nn.softplus(delta_pre)
    steps_by = (piece_len, GROUP)
    in_spread, out_spread = spread(in_coef, LANES), spread(out_coef, LANES)
    in_diag, out_diag = diagonal(in_coef, BLK), diagonal(out_coef, BLK)
    out_rest = diagonal(out_coef - lax.reduce_precision(out_coef, 8, 7), BLK)
    float_steps = pltpu.VMEM(steps_by, jnp.float32)
    stack_of = pltpu.VMEM((BLK * states, GROUP), jnp.bfloat16)
    (local_end,) = scan_call(
        first_pass_kernel,
        "first_pass",
        sequences,
        states,
        [("wide", delta), ("wide", conv_flat), ("spread", in_spread), ("rates", decay_log)],
        ["state"],
        [float_steps],
    )
    delta_sum = jnp.sum(delta.reshape(sequences, piece_len, inner_width), axis=1)
    carried = exchange(local_end, delta_sum, decay_log, False)
    (scanned,) = scan_call(
        second_pass_kernel,
        "second_pass",
        sequences,
        states,
        [
            ("wide", delta),
            ("wide", conv_flat),
            ("spread", in_spread),
            ("rates", decay_log),
            ("state", carried),
            ("narrow", out_diag),
            ("narrow", out_rest),
        ],
        ["wide"],
        [float_steps, stack_of],
    )
    mixer_pre = scanned + skip_gain * conv_flat
    gate_act = jax.nn.silu(gate_half)
    mixed = (mixer_pre * gate_act).astype(jnp.bfloat16)
    resid = flat_in + half_dot(mixed, out_proj)
    normed_two, scaling_two = norm_forward(resid, expert_norm)
    routed = normed_two.astype(jnp.bfloat16)
    flat_ids = expert_ids.reshape(tokens)
    flat_slot = capacity_slot.reshape(tokens)
    target = jnp.where(flat_slot < capacity, flat_ids * capacity + flat_slot, experts * capacity)
    slot_rows = jnp.arange(experts * capacity, dtype=jnp.int32)
    picks = (slot_rows[:, None] == target[None, :]).astype(jnp.bfloat16)
    group = lax.axis_size("seq")
    expert = lax.axis_index("exp")

    def to_experts(values):
        buffer = half_dot(picks, values).astype(jnp.bfloat16)
        arrived = lax.all_to_all(
            buffer.reshape(experts, capacity, width), "exp", split_axis=0, concat_axis=0, tiled=True
        )
        return lax.all_gather(arrived.reshape(senders * capacity, width), "seq", axis=0, tiled=True)

    def to_tokens(partial):
        mine = lax.psum_scatter(partial, "seq", scatter_dimension=0, tiled=True)
        back = lax.all_to_all(
            mine.reshape(senders, capacity, width), "exp", split_axis=0, concat_axis=0, tiled=True
        )
        return rows_dot(picks, back.reshape(experts * capacity, width))

    grad_rows = to_experts(out_grad.reshape(tokens, width)).astype(jnp.float32)
    rows = to_experts(routed)
    rows_wide = rows.astype(jnp.float32)
    shares = jax.nn.softmax(exact_dot(rows_wide, router_weight), axis=-1)
    chosen = (jnp.arange(experts, dtype=jnp.int32) == expert).astype(jnp.float32)[None, :]
    gate = jnp.sum(shares * chosen, axis=-1, keepdims=True)
    up, down = expert_up[0], expert_down[0]
    pre_act = half_dot(rows, up)
    hidden_act, gelu_back = jax.vjp(exact_gelu, pre_act)
    hidden_half = hidden_act.astype(jnp.bfloat16)
    expert_out = half_dot(hidden_half, down)
    grad_sent = (gate * grad_rows).astype(jnp.bfloat16)
    grad_gate = jnp.sum(grad_rows * expert_out, axis=-1, keepdims=True)
    grad_logits = grad_gate * gate * (chosen - shares)
    grad_router = rows_dot(rows_wide, grad_logits, lax.Precision.HIGHEST)
    grad_down = rows_dot(hidden_half, grad_sent)
    grad_pre = gelu_back(cols_dot(grad_sent, down))[0].astype(jnp.bfloat16)
    grad_up = rows_dot(rows, grad_pre)
    grad_row_in = cols_dot(grad_pre, up) + cols_dot(
        grad_logits, router_weight, lax.Precision.HIGHEST
    )
    grad_routed = to_tokens(grad_row_in.astype(jnp.bfloat16))
    layer_out = (
        (resid + to_tokens((gate * expert_out).astype(jnp.bfloat16)))
        .astype(jnp.bfloat16)
        .reshape(sequences, piece_len, width)
    )
    grad_top = out_grad.reshape(tokens, width).astype(jnp.float32)
    grad_up_own, grad_down_own = grad_up[None], grad_down[None]
    grad_resid_norm, grad_expert_norm = norm_backward(resid, scaling_two, expert_norm, grad_routed)
    grad_resid = grad_top + grad_resid_norm
    grad_mixer = grad_resid.astype(jnp.bfloat16)
    grad_out_proj = rows_dot(mixed, grad_mixer)
    grad_mixed = cols_dot(grad_mixer, out_proj)
    grad_scan = grad_mixed * gate_act
    grad_gate_half = grad_mixed * mixer_pre * silu_slope(gate_half)
    grad_gate_half = grad_gate_half.astype(jnp.bfloat16)
    grad_in_gate = rows_dot(normed_half, grad_gate_half)
    grad_normed_gate = cols_dot(grad_gate_half, in_proj[:, inner_width:])
    grad_skip_gain = jnp.sum(grad_scan * conv_flat, axis=0)
    (gradient_first,) = scan_call(
        back_summary_kernel,
        "back_summary",
        sequences,
        states,
        [("wide", delta), ("wide", grad_scan), ("spread", out_spread), ("rates", decay_log)],
        ["state"],
        [],
    )
    carried_back = exchange(gradient_first, delta_sum, decay_log, True)
    full_steps = pltpu.VMEM((piece_len, states, GROUP), jnp.float32)
    grad_delta, grad_conv_scan, grad_in_wide, grad_out_wide, grad_log_parts = scan_call(
        backward_kernel,
        "backward_scan",
        sequences,
        states,
        [
            ("wide", delta),
            ("wide", conv_flat),
            ("wide", grad_scan),
            ("spread", in_spread),
            ("spread", out_spread),
            ("narrow", in_diag),
            ("rates", decay_log),
            ("state", carried),
            ("state", carried_back),
        ],
        ["wide", "wide", "narrow", "narrow", "state"],
        [float_steps, full_steps, full_steps, stack_of, stack_of],
    )
    grad_decay_log = jnp.sum(grad_log_parts, axis=0)
    grad_in_coef = undiagonal(grad_in_wide, BLK, states)
    grad_out_coef = undiagonal(grad_out_wide, BLK, states)
    grad_conv_act = grad_scan * skip_gain + grad_conv_scan
    grad_delta_pre = grad_delta * jax.nn.sigmoid(delta_pre)
    grad_delta_bias = jnp.sum(grad_delta_pre, axis=0)
    grad_delta_proj = rows_dot(delta_low, grad_delta_pre, lax.Precision.HIGHEST)
    grad_delta_low = cols_dot(grad_delta_pre, delta_proj.astype(jnp.float32), lax.Precision.HIGHEST)
    grad_projections = jnp.concatenate([grad_delta_low, grad_in_coef, grad_out_coef], axis=-1)
    grad_state_proj = rows_dot(conv_flat, grad_projections, lax.Precision.HIGHEST)
    grad_conv_act = grad_conv_act + cols_dot(
        grad_projections, state_proj.astype(jnp.float32), lax.Precision.HIGHEST
    )
    grad_conv_pre = grad_conv_act.reshape(sequences, piece_len, inner_width) * silu_slope(conv_pre)
    grad_conv_bias = jnp.sum(grad_conv_pre, axis=(0, 1))
    grad_conv_weight = jnp.stack(
        [
            jnp.sum(grad_conv_pre * extended[:, tap : tap + piece_len, :], axis=(0, 1))
            for tap in range(taps)
        ]
    )
    grad_extended = jnp.zeros_like(extended)
    for tap in range(taps):
        grad_extended = grad_extended.at[:, tap : tap + piece_len, :].add(
            conv_weight[tap] * grad_conv_pre
        )
    rim_back = shifted(
        grad_extended[:, : taps - 1, :].astype(jnp.bfloat16), ("seq", "exp"), -1
    ).astype(jnp.float32)
    grad_inner = grad_extended[:, taps - 1 :, :].at[:, piece_len - (taps - 1) :, :].add(rim_back)
    grad_inner = grad_inner.reshape(tokens, inner_width).astype(jnp.bfloat16)
    grad_in_inner = rows_dot(normed_half, grad_inner)
    grad_normed_one = grad_normed_gate + cols_dot(grad_inner, in_proj[:, :inner_width])
    grad_flat_in, grad_mixer_gain = norm_backward(flat_in, scaling_one, mixer_gain, grad_normed_one)
    in_grad = (grad_resid + grad_flat_in).reshape(sequences, piece_len, width)
    def as_rows(values):
        blocks = values.shape[1] // width
        return jnp.concatenate(
            [values[:, at * width : (at + 1) * width] for at in range(blocks)], axis=0
        ).astype(jnp.bfloat16)

    def as_columns(values):
        return jnp.concatenate(
            [values[at : at + width] for at in range(0, values.shape[0], width)], axis=1
        ).astype(jnp.float32)

    small = [
        grad_state_proj.T,
        grad_delta_proj,
        grad_decay_log,
        grad_conv_weight,
        grad_conv_bias[None],
        grad_delta_bias[None],
        grad_skip_gain[None],
        jnp.concatenate([grad_mixer_gain, grad_expert_norm])[None],
        grad_router.T.reshape(experts * width // inner_width, inner_width),
    ]
    heights = [value.shape[0] for value in small]
    devices = lax.axis_size("seq") * senders
    spare = -sum(heights) % (devices // 2)
    packed = as_rows(
        jnp.concatenate(small + [jnp.zeros((spare, inner_width), jnp.float32)], axis=0)
    )
    sum_out, sum_gate, sum_inner, sum_small = total(
        [grad_out_proj.astype(jnp.bfloat16), as_rows(grad_in_gate), as_rows(grad_in_inner), packed],
        3,
        "grad_total",
    )
    grad_in_proj = jnp.concatenate([as_columns(sum_inner), as_columns(sum_gate)], axis=1)
    half_height = sum_small.shape[0] // 2
    small_wide = jnp.concatenate([sum_small[:half_height], sum_small[half_height:]], axis=1).astype(
        jnp.float32
    )
    offsets = [sum(heights[:at]) for at in range(len(heights) + 1)]
    pieces = [small_wide[offsets[at] : offsets[at + 1]] for at in range(len(heights))]
    summed = (
        pieces[7][0, :width],
        grad_in_proj,
        pieces[3],
        pieces[4][0],
        pieces[0].T,
        pieces[1],
        pieces[5][0],
        pieces[2],
        pieces[6][0],
        sum_out.astype(jnp.float32),
        pieces[7][0, width:],
        pieces[8].reshape(experts, width).T,
    )
    return (
        layer_out,
        in_grad,
        summed[0],
        summed[1],
        summed[2],
        summed[3],
        summed[4],
        summed[5],
        summed[6],
        summed[7],
        summed[8],
        summed[9],
        summed[10],
        summed[11],
        grad_up_own,
        grad_down_own,
    )


def solution(mesh):
    placed = (
        P(None, ("seq", "exp"), None),
        P(),
        P(),
        P(),
        P(),
        P(),
        P(),
        P(),
        P(),
        P(),
        P(),
        P(),
        P(),
        P("exp", None, "seq"),
        P("exp", "seq", None),
        P(None, ("seq", "exp")),
        P(None, ("seq", "exp")),
        P(None, ("seq", "exp"), None),
    )
    return jax.shard_map(
        on_device,
        mesh=mesh,
        in_specs=placed,
        out_specs=(
            P(None, ("seq", "exp"), None),
            P(None, ("seq", "exp"), None),
            P(),
            P(),
            P(),
            P(),
            P(),
            P(),
            P(),
            P(),
            P(),
            P(),
            P(),
            P(),
            P("exp", None, "seq"),
            P("exp", "seq", None),
        ),
        check_vma=False,
    )
```

time: 1900 us -> 585 us (0.31)
  waiting for transfers between devices: 1260 us -> 98.1 us
  other arithmetic: 280 us -> 46 us
  Pallas kernels: 0 us -> 231 us
  local copies, waits for them, and re-layouts: 205 us -> 55.6 us
    psum x2 -> x0, waiting for transfers between devices: 642 us -> none  [on_device(): lax.psum((grad_mixer_gain, grad_in_proj, grad_conv_weight, grad_conv_bias...]
    reduce_scatter x2, waiting for transfers between devices: 331 us -> 59.9 us  [to_tokens(): mine = lax.psum_scatter(partial, 'seq', scatter_dimension=0, tiled=True)]
    pallas_call x0 -> x7, Pallas kernels: none -> 231 us  [the longest x1 122 us: total(): pl.pallas_call(functools.partial(total_kernel, planes, chips, count), nam...]
    all_gather x5 -> x2, waiting for transfers between devices: 260 us -> 38.1 us  [to_experts(): lax.all_gather(arrived.reshape(senders * capacity, width), 'seq', axis=0,...]
    mul x121 -> x0, local copies, waits for them, and re-layouts: 111 us -> none  [the longest x24 23.6 us: forward_one_block(): in_blk[inner_step][:, :, None] * drive_blk[inner_step][:, None, :]]
    while x128 -> x0, other arithmetic: 86.4 us -> none
    select_n x66 -> x2, other arithmetic: 76.8 us -> 0.9 us  [the longest x1 0.89 us: undiagonal(): masked = jnp.where(column == row, product, 0.0)]
    reduce_sum x59 -> x7, other arithmetic: 42.9 us -> 3.37 us  [the longest x1 1.35 us: on_device(): grad_conv_bias = jnp.sum(grad_conv_pre, axis=(0, 1))]
  transfers between devices with their start and end apart: 14 -> 9, of which waited for: 13 -> 3; matrix products, arithmetic and copies ran while one was open for 8% -> 15% of each run, Pallas kernels for 0% -> 19%
where the time goes in v1:
time: 585 us; the launch traced here: 576 us
  Pallas kernels  231 us (39%)
  waiting for transfers between devices  98.1 us (17%)
  matrix products  96.5 us (16%)
  local copies, waits for them, and re-layouts  55.6 us (10%)
  other arithmetic  46 us (8%)
  starting transfers between devices  21.6 us (4%)
  between operations  15.6 us (3%)
  blocking collectives  11.1 us (2%)
    pallas_call x1, Pallas kernels, total(): pl.pallas_call(functools.partial(total_kernel, planes, chips, count), nam...  122 us
    pallas_call x4, Pallas kernels, scan_call(): pl.pallas_call(kernel, name=name, grid=(sequences, width // GROUP), in_sp...  65.2 us
    reduce_scatter x2, waiting for transfers between devices, to_tokens(): mine = lax.psum_scatter(partial, 'seq', scatter_dimension=0, tiled=True)  59.9 us
    pallas_call x2, Pallas kernels, exchange(): pl.pallas_call(functools.partial(exchange_kernel, reverse, planes, member...  44.7 us
    all_gather x2, waiting for transfers between devices, to_experts(): lax.all_gather(arrived.reshape(senders * capacity, width), 'seq', axis=0,...  38.1 us
    dot_general x8, matrix products, cols_dot(): lax.dot_general(left, right, (((1,), (1,)), ((), ())), precision=precisio...  32.7 us
    dot_general x6, matrix products, half_dot(): return jnp.dot(left, right, preferred_element_type=jnp.float32)  32.3 us
    dot_general x10, matrix products, rows_dot(): lax.dot_general(left, right, (((0,), (0,)), ((), ())), precision=precisio...  25.5 us
  transfers between devices with their start and end apart: 9, of which 3 were waited for; matrix products, arithmetic and copies ran while one was open for 15% of the time, Pallas kernels for 19%

profile of v1, /device:TPU:11, one launch (start us, length us, event | category | flops | bytes accessed | tf_op | source)
XLA Modules:
  0.0 576.0 jit_solution(10327701609429356780)
XLA Ops:
  7.2 1.3 multiply_reduce_fusion.10
  9.1 1.2 multiply_convert_fusion.6
  10.3 3.9 fusion.84
  15.6 3.7 collective-permute-start
  20.4 4.0 all-to-all-start.2
  24.7 5.4 fusion.25
  31.1 1.2 copy-done.1
  33.7 1.6 compare_select_fusion
  35.4 1.9 broadcast_in_dim.30.in_ref
  37.9 6.6 %first_pass.1.end_ref = f32[2,16,1536]{2,1,0:T(8,128)S(1)} custom-call(f32[256,1536]{1,0:T(8,128)S(1)} %get-tuple-element.150.delta_ref, f32[256,1536]{1,0:T(8,128)S(1)} %bitcast.112, f32[256,16,128]{2,1,0:T(8,128)} %broadcast_in_dim.30.in_ref, f32[16,1536]{1,0:T(8,128)S(1)} %copy-done.13), custom_call_target="tpu_custom_call" | custom-call | flops 125829120 | bytes 6291456 | tf_op jit(solution)/shard_map/first_pass/pallas_call | solution.py:310
  45.5 25.2 %state_exchange.1.start_ref = f32[2,16,1536]{2,1,0:T(8,128)S(1)} custom-call(f32[2,16,1536]{2,1,0:T(8,128)S(1)} %first_pass.1.end_ref, f32[2,1536]{1,0:T(2,128)S(1)} %bitcast_reduce_fusion.sum_ref, f32[4,1536]{1,0:T(4,128)S(1)} %constant_dynamic-slice_fusion.rates_ref), custom_call_target="tpu_custom_call" | custom-call | flops 1000000 | bytes 20000000 | tf_op jit(solution)/shard_map/state_exchange/pallas_call | solution.py:466
  70.9 15.4 %second_pass.1 = f32[256,1536]{1,0:T(8,128)S(1)} custom-call(f32[256,1536]{1,0:T(8,128)S(1)} %get-tuple-element.150.delta_ref, f32[256,1536]{1,0:T(8,128)} %bitcast.110, f32[256,16,128]{2,1,0:T(8,128)} %broadcast_in_dim.30.in_ref, f32[16,1536]{1,0:T(8,128)S(1)} %copy-done.13, f32[2,16,1536]{2,1,0:T(8,128)S(1)} %state_exchange.1.start_ref, ...), custom_call_target="tpu_custom_call" | custom-call | flops 125829120 | bytes 6291456 | tf_op jit(solution)/shard_map/second_pass/pallas_call | solution.py:310
  89.8 11.1 %all_to_all.20 = bf16[8,40,768]{2,1,0:T(8,128)(2,1)} all-to-all(bf16[8,40,768]{2,1,0:T(8,128)(2,1)S(1)} %bitcast.128), channel_id=1, replica_groups=mesh['seq'=4,'exp'=8] {'exp'}, dimensions={0} | all-to-all | bytes 983040 | tf_op jit(solution)/shard_map/all_to_all | solution.py:775
  101.3 4.0 copy.55
  105.3 38.1 %all-gather.3.cloned.1.call-done = bf16[1280,768]{1,0:T(8,128)(2,1)} async-done(((bf16[320,768]{1,0:T(8,128)(2,1)}), bf16[1280,768]{1,0:T(8,128)(2,1)}) %all-gather.3.cloned.1.call-update) | async-done | bytes 1966096 | tf_op jit(solution)/shard_map/all_gather | solution.py:778
  143.4 3.4 fusion.83
  147.0 22.7 %multiply_convert_fusion.1 = (bf16[1280,768]{1,0:T(8,128)(2,1)S(1)}, f32[1280,768]{1,0:T(8,128)S(1)}, f32[1280,768]{1,0:T(8,128)S(1)}) fusion(bf16[1280,768]{1,0:T(8,128)(2,1)S(1)} %copy-done.17, bf16[1,768,768]{2,1,0:T(8,128)(2,1)} %param.41), kind=kOutput, calls=%fused_computation.12 | convolution fusion | flops 1573847040 | bytes 12976128 | tf_op jit(solution)/shard_map/dot_general | solution.py:28
  169.7 3.3 fusion.1
  173.0 2.9 add_convert_fusion
  176.0 1.8 fusion.33
  177.8 15.9 %fusion.8 = bf16[1280,768]{1,0:T(8,128)(2,1)} fusion(f32[1280,768]{1,0:T(8,128)S(1)} %fusion.33, f32[768,8]{0,1:T(8,128)S(1)} %copy-done.57, f32[1280]{0:T(1024)S(1)} %mul.368, f32[8]{0:T(128)S(1)} %compare_convert_fusion, f32[1280,8]{0,1:T(8,128)S(1)} %get-tuple-element.156, f32[1280]{0:T(1024)S(1)} %fusion.58, f32[1280]{0:T(1024)S(1)} %get-tuple-element.155), kind=kOutput, calls=%fused_computation.26 | convolution fusion | flops 96378880 | bytes 5979168 | tf_op jit(solution)/shard_map/dot_general | solution.py:46
  193.8 4.0 copy.62
  198.6 2.5 fusion.59
  201.1 5.3 fusion.19
  206.4 27.3 %reduce-scatter.5.cloned.1.call-done = bf16[320,768]{1,0:T(8,128)(2,1)} async-done(((bf16[1280,768]{1,0:T(8,128)(2,1)}), bf16[320,768]{1,0:T(8,128)(2,1)}) %reduce-scatter.5.cloned.1.call-update) | async-done | bytes 491536 | tf_op jit(solution)/shard_map/reduce_scatter | solution.py:781
  233.8 6.1 %all-to-all-start.3 = ((bf16[8,40,768]{2,1,0:T(8,128)(2,1)}), bf16[8,40,768]{2,1,0:T(8,128)(2,1)}, u32[]{:S(2)}, u32[]{:S(2)}) async-start(bf16[8,40,768]{2,1,0:T(8,128)(2,1)} %bitcast.137), calls=%async_computation.4 | async-start | bytes 983040 | tf_op jit(solution)/shard_map/all_to_all | solution.py:782
  239.8 5.3 convolution_bitcast_fusion
  245.1 32.6 %reduce-scatter.7.cloned.1.call-done = bf16[320,768]{1,0:T(8,128)(2,1)} async-done(((bf16[1280,768]{1,0:T(8,128)(2,1)}), bf16[320,768]{1,0:T(8,128)(2,1)}) %reduce-scatter.7.cloned.1.call-update) | async-done | bytes 491536 | tf_op jit(solution)/shard_map/reduce_scatter | solution.py:781
  277.7 4.9 all-to-all-start.1
  282.7 2.6 multiply_reduce_fusion.5
  286.5 4.2 multiply_reduce_fusion
  290.8 1.9 broadcast_in_dim.33.out_ref
  293.3 6.5 %back_summary.1.end_ref = f32[2,16,1536]{2,1,0:T(8,128)S(1)} custom-call(f32[256,1536]{1,0:T(8,128)S(1)} %copy-done.15, f32[256,1536]{1,0:T(8,128)S(1)} %get-tuple-element.116.grad_ref, f32[256,16,128]{2,1,0:T(8,128)} %broadcast_in_dim.33.out_ref, f32[16,1536]{1,0:T(8,128)S(1)} %copy-done.13), custom_call_target="tpu_custom_call" | custom-call | flops 125829120 | bytes 6291456 | tf_op jit(solution)/shard_map/back_summary/pallas_call | solution.py:310
  299.9 19.5 %state_exchange_back.1.finish_ref = f32[2,16,1536]{2,1,0:T(8,128)S(1)} custom-call(f32[2,16,1536]{2,1,0:T(8,128)S(1)} %back_summary.1.end_ref, f32[2,1536]{1,0:T(2,128)S(1)} %bitcast_reduce_fusion.sum_ref, f32[4,1536]{1,0:T(4,128)S(1)} %constant_dynamic-slice_fusion.rates_ref), custom_call_target="tpu_custom_call" | custom-call | flops 1000000 | bytes 20000000 | tf_op jit(solution)/shard_map/state_exchange_back/pallas_call | solution.py:466
  319.4 36.6 %backward_scan.1 = (f32[256,1536]{1,0:T(8,128)S(1)}, f32[256,1536]{1,0:T(8,128)}, f32[256,256]{1,0:T(8,128)S(1)}, f32[256,256]{1,0:T(8,128)S(1)}, f32[2,16,1536]{2,1,0:T(8,128)S(1)}) custom-call(f32[256,1536]{1,0:T(8,128)} %copy-done.14, f32[256,1536]{1,0:T(8,128)} %bitcast.111, f32[256,1536]{1,0:T(8,128)} %copy-done.8, ...), custom_call_target="tpu_custom_call" | custom-call | flops 125829120 | bytes 6291456 | tf_op jit(solution)/shard_map/backward_scan/pallas_call | solution.py:310
  359.1 1.8 copy.58
  362.0 2.5 fusion.74
  368.8 1.3 fusion.72
  370.4 1.5 scatter-add.14
  371.8 1.5 multiply_add_fusion
  373.3 5.1 scatter-add.15
  378.4 3.4 slice_add_fusion.1
  381.7 5.1 scatter-add.16
  386.8 3.5 slice_add_fusion
  391.3 1.8 fusion.53
  393.1 2.5 collective-permute-start.1
  396.6 1.6 pad_maximum_fusion
  398.7 1.7 fusion.54
  400.5 2.2 convolution_convert_fusion.1
  402.7 2.5 fusion.29
  406.2 1.6 scatter-add.19
  407.8 1.5 convert_element_type.143
  409.3 2.5 fusion.9
  411.9 3.4 multiply_reduce_fusion.6
  416.3 1.6 fusion.78
  419.1 1.2 convert_element_type.149.refs_3_
  420.3 3.2 pad_maximum_fusion.1
  423.5 121.5 %grad_total.1 = (bf16[2,4,4,48,768]{4,3,2,1,0:T(8,128)(2,1)S(1)}, bf16[2,4,4,48,768]{4,3,2,1,0:T(8,128)(2,1)}, bf16[2,4,4,48,768]{4,3,2,1,0:T(8,128)(2,1)}, bf16[2,4,4,10,768]{4,3,2,1,0:T(8,128)(2,1)S(1)}) custom-call(bf16[2,4,4,48,768]{4,3,2,1,0:T(8,128)(2,1)} %bitcast.119, bf16[2,4,4,48,768]{4,3,2,1,0:T(8,128)(2,1)} %bitcast.117, ...), custom_call_target="tpu_custom_call" | custom-call | flops 10000000 | bytes 100000000 | tf_op jit(solution)/shard_map/grad_total/pallas_call | solution.py:658
  545.1 1.4 copy-done.6
  552.7 1.6 fusion.77
  555.2 1.5 fusion.76
  557.7 2.7 bitcast_convert_fusion.1
  561.0 2.5 multiply_add_fusion.3
  563.5 5.6 maximum_convert_fusion
  (274 shorter events, 36.7 us)
Async XLA Ops:
  7.2 80.4 %copy-start = (bf16[1536,768]{1,0:T(8,128)(2,1)S(1)}, bf16[1536,768]{1,0:T(8,128)(2,1)}, u32[]{:S(2)}) copy-start(bf16[1536,768]{1,0:T(8,128)(2,1)} %param.38) | copy-start | bytes 7077892
  10.3 4.0 copy-start.45
  14.2 6.2 %copy-start.24 = (f32[256,3072]{1,0:T(8,128)}, f32[256,3072]{1,0:T(8,128)S(1)}, u32[]{:S(2)}) copy-start(f32[256,3072]{1,0:T(8,128)S(1)} %fusion.84) | copy-start | bytes 9437188
  14.3 5.1 copy-start.90
  14.3 5.0 copy-start.91
  14.3 5.1 copy-start.43
  14.3 10.2 %copy-start.77 = (f32[4,1536]{1,0:T(4,128)S(1)}, f32[4,1536]{1,0:T(4,128)}, u32[]{:S(2)}) copy-start(f32[4,1536]{1,0:T(4,128)} %param.31) | copy-start | bytes 73732
  14.3 10.3 %copy-start.13 = (f32[16,1536]{1,0:T(8,128)S(1)}, f32[16,1536]{1,0:T(8,128)}, u32[]{:S(2)}) copy-start(f32[16,1536]{1,0:T(8,128)} %log_ref.7) | copy-start | bytes 294916
  14.3 10.3 %copy-start.86 = (f32[1536]{0:T(1024)S(1)}, f32[1536]{0:T(1024)}, u32[]{:S(2)}) copy-start(f32[1536]{0:T(1024)} %param.32) | copy-start | bytes 18436
  15.6 9.0 %collective-permute-start = (f32[2,3,1536]{2,1,0:T(4,128)S(1)}, f32[2,3,1536]{2,1,0:T(4,128)S(1)}, u32[]{:S(2)}, u32[]{:S(2)}) collective-permute-start(f32[2,3,1536]{2,1,0:T(4,128)S(1)} %slice.316), channel_id=1, source_target_pairs={{0,1},{1,2},{2,3},{3,4},{4,5},{5,6},{6,7},{7,8},{8,9},{9,10},{10,1... | collective-permute-start | bytes 110600 | tf_op jit(solution)/shard_map/ppermute | solution.py:24
  19.3 69.3 %copy-start.74 = (s32[256]{0:T(256)}, s32[256]{0:T(256)S(1)}, u32[]{:S(2)}) copy-start(s32[256]{0:T(256)S(1)} %fusion.66) | copy-start | bytes 3076
  20.4 11.9 %all-to-all-start.2 = ((bf16[8,40,768]{2,1,0:T(8,128)(2,1)}), bf16[8,40,768]{2,1,0:T(8,128)(2,1)S(1)}, u32[]{:S(2)}, u32[]{:S(2)}) async-start(bf16[8,40,768]{2,1,0:T(8,128)(2,1)} %bitcast.16), calls=%async_computation.2 | async-start | bytes 983040 | tf_op jit(solution)/shard_map/all_to_all | solution.py:775
  24.4 76.9 %all-gather.5.cloned.1.call-start = ((), (), s32[]{:S(2)}) async-start(), calls=%async_computation.7 | async-start | bytes 2457600 | tf_op jit(solution)/shard_map/all_gather | solution.py:778
  24.5 5.5 copy-start.58
  24.5 5.5 copy-start.60
  24.6 5.5 copy-start.62
  24.6 5.5 copy-start.64
  24.6 46.1 %copy-start.82 = (s32[256]{0:T(256)}, s32[256]{0:T(256)S(1)}, u32[]{:S(2)}) copy-start(s32[256]{0:T(256)S(1)} %get-tuple-element.159) | copy-start | bytes 3076
  24.6 46.1 %copy-start.84 = (s32[256]{0:T(256)}, s32[256]{0:T(256)S(1)}, u32[]{:S(2)}) copy-start(s32[256]{0:T(256)S(1)} %get-tuple-element.160) | copy-start | bytes 3076
  24.7 5.4 copy-start.47
  30.1 3.6 copy-start.53
  30.1 3.6 copy-start.94
  33.1 110.3 %all-gather.3.cloned.1.call-start = ((), (), s32[]{:S(2)}) async-start(), calls=%async_computation.6 | async-start | bytes 2457600 | tf_op jit(solution)/shard_map/all_gather | solution.py:778
  35.3 9.2 %copy-start.32 = (f32[256,1536]{1,0:T(8,128)}, f32[256,1536]{1,0:T(8,128)S(1)}, u32[]{:S(2)}) copy-start(f32[256,1536]{1,0:T(8,128)S(1)} %get-tuple-element.151) | copy-start | bytes 4718596
  35.3 35.5 %copy-start.14 = (f32[256,1536]{1,0:T(8,128)}, f32[256,1536]{1,0:T(8,128)S(1)}, u32[]{:S(2)}) copy-start(f32[256,1536]{1,0:T(8,128)S(1)} %get-tuple-element.150.delta_ref) | copy-start | bytes 4718596
  70.9 15.5 %copy-start.3 = (f32[2,128,1536]{2,1,0:T(8,128)S(1)}, f32[2,128,1536]{2,1,0:T(8,128)}, u32[]{:S(2)}) copy-start(f32[2,128,1536]{2,1,0:T(8,128)} %copy-done.1) | copy-start | bytes 4718596
  70.9 15.5 %copy-start.25 = (f32[256,3072]{1,0:T(8,128)S(1)}, f32[256,3072]{1,0:T(8,128)}, u32[]{:S(2)}) copy-start(f32[256,3072]{1,0:T(8,128)} %copy-done.24) | copy-start | bytes 9437188
  70.9 15.5 %copy-start.70 = (f32[1536]{0:T(1024)S(1)}, f32[1536]{0:T(1024)}, u32[]{:S(2)}) copy-start(f32[1536]{0:T(1024)} %param.37) | copy-start | bytes 18436
  88.6 16.7 %copy-start.78 = (f32[256]{0:T(256)}, f32[256]{0:T(256)S(1)}, u32[]{:S(2)}) copy-start(f32[256]{0:T(256)S(1)} %add_rsqrt_fusion) | copy-start | bytes 3076
  101.0 132.8 %reduce-scatter.5.cloned.1.call-start = ((), (), s32[]{:S(2)}) async-start(), calls=%async_computation.8 | async-start | bytes 2457600 | tf_op jit(solution)/shard_map/reduce_scatter | solution.py:781
  101.3 42.1 %copy-start.57 = (f32[768,8]{0,1:T(8,128)S(1)}, f32[768,8]{0,1:T(8,128)}, u32[]{:S(2)}) copy-start(f32[768,8]{0,1:T(8,128)} %param.40) | copy-start | bytes 73732
  143.4 3.5 copy-start.17
  146.9 30.8 %copy-start.73 = (f32[1280]{0:T(1024)}, f32[1280]{0:T(1024)S(1)}, u32[]{:S(2)}) copy-start(f32[1280]{0:T(1024)S(1)} %multiply_reduce_fusion.11) | copy-start | bytes 15364
  146.9 22.7 %copy-start.39 = (bf16[1280,768]{0,1:T(8,128)(2,1)S(1)}, bf16[1280,768]{0,1:T(8,128)(2,1)}, u32[]{:S(2)}) copy-start(bf16[1280,768]{0,1:T(8,128)(2,1)} %copy.55) | copy-start | bytes 5898244
  146.9 22.7 %copy-start.92 = (bf16[1,768,768]{2,1,0:T(8,128)(2,1)S(1)}, bf16[1,768,768]{2,1,0:T(8,128)(2,1)}, u32[]{:S(2)}) copy-start(bf16[1,768,768]{2,1,0:T(8,128)(2,1)} %param.42) | copy-start | bytes 3538948
  169.7 3.4 copy-start.95
  173.0 2.9 copy-start.93
  177.8 16.0 %copy-start.66 = (f32[1280]{0:T(1024)}, f32[1280]{0:T(1024)S(1)}, u32[]{:S(2)}) copy-start(f32[1280]{0:T(1024)S(1)} %mul.368) | copy-start | bytes 15364
  193.7 84.0 %reduce-scatter.7.cloned.1.call-start = ((), (), s32[]{:S(2)}) async-start(), calls=%async_computation.9 | async-start | bytes 2457600 | tf_op jit(solution)/shard_map/reduce_scatter | solution.py:781
  233.8 44.0 %all-to-all-start.3 = ((bf16[8,40,768]{2,1,0:T(8,128)(2,1)}), bf16[8,40,768]{2,1,0:T(8,128)(2,1)}, u32[]{:S(2)}, u32[]{:S(2)}) async-start(bf16[8,40,768]{2,1,0:T(8,128)(2,1)} %bitcast.137), calls=%async_computation.4 | async-start | bytes 983040 | tf_op jit(solution)/shard_map/all_to_all | solution.py:782
  239.8 42.9 %copy-start.68 = (f32[768]{0:T(1024)S(1)}, f32[768]{0:T(1024)}, u32[]{:S(2)}) copy-start(f32[768]{0:T(1024)} %param.39) | copy-start | bytes 9220
  239.8 42.9 %copy-start.75 = (s32[256]{0:T(256)S(1)}, s32[256]{0:T(256)}, u32[]{:S(2)}) copy-start(s32[256]{0:T(256)} %copy-done.74) | copy-start | bytes 3076
  239.8 42.9 %copy-start.79 = (f32[256]{0:T(256)S(1)}, f32[256]{0:T(256)}, u32[]{:S(2)}) copy-start(f32[256]{0:T(256)} %copy-done.78) | copy-start | bytes 3076
  277.7 124.9 %all-to-all-start.1 = ((bf16[8,40,768]{2,1,0:T(8,128)(2,1)}), bf16[8,40,768]{2,1,0:T(8,128)(2,1)}, u32[]{:S(2)}, u32[]{:S(2)}) async-start(bf16[8,40,768]{2,1,0:T(8,128)(2,1)} %bitcast.136), calls=%async_computation.1 | async-start | bytes 983040 | tf_op jit(solution)/shard_map/all_to_all | solution.py:782
  282.7 3.8 copy-start.4
  282.7 3.8 copy-start.11
  282.7 3.8 copy-start.71
  290.8 9.1 %copy-start.8 = (f32[256,1536]{1,0:T(8,128)}, f32[256,1536]{1,0:T(8,128)S(1)}, u32[]{:S(2)}) copy-start(f32[256,1536]{1,0:T(8,128)S(1)} %get-tuple-element.116.grad_ref) | copy-start | bytes 4718596
  319.3 37.8 %copy-start.83 = (s32[256]{0:T(256)S(1)}, s32[256]{0:T(256)}, u32[]{:S(2)}) copy-start(s32[256]{0:T(256)} %copy-done.82) | copy-start | bytes 3076
  319.4 37.8 %copy-start.85 = (s32[256]{0:T(256)S(1)}, s32[256]{0:T(256)}, u32[]{:S(2)}) copy-start(s32[256]{0:T(256)} %copy-done.84) | copy-start | bytes 3076
  361.9 3.4 copy-start.42
  361.9 3.4 copy-start.48
  362.0 3.4 copy-start.72
  362.0 5.5 copy-start.30
  364.4 3.0 copy-start.20
  373.3 5.1 copy-start.61
  381.7 5.1 copy-start.59
  386.8 4.5 copy-start.5
  390.3 5.3 copy-start.46
  390.3 5.3 copy-start.50
  393.1 12.2 %collective-permute-start.1 = (bf16[2,3,1536]{2,1,0:T(4,128)(2,1)S(1)}, bf16[2,3,1536]{2,1,0:T(4,128)(2,1)S(1)}, u32[]{:S(2)}, u32[]{:S(2)}) collective-permute-start(bf16[2,3,1536]{2,1,0:T(4,128)(2,1)S(1)} %slice.393), channel_id=1, source_target_pairs={{1,0},{2,1},{3,2},{4,3},{5,4},{6,5},{7,6},{8,7},{9,8},{10,9},{11,1... | collective-permute-start | bytes 55304 | tf_op jit(solution)/shard_map/ppermute | solution.py:24
  411.9 3.5 copy-start.88
  549.7 3.0 copy-start.38
  557.7 3.3 copy-start.29
  (41 other events, 74.9 us)
Sparse Core Ops, SparseCore 0:
  33.2 44.9 all-gather.4
  101.1 42.2 all-gather.2
  193.9 39.8 reduce-scatter.4
  235.9 41.7 reduce-scatter.6

commit v2 on v1

--- a/solution.py
+++ b/solution.py
@@ -1,4 +1,5 @@
 import functools
+import math
 
 import jax
 import jax.numpy as jnp
@@ -189,6 +190,7 @@
 
 
 def backward_kernel(
+    middle,
     delta_ref,
     conv_ref,
     grad_ref,
@@ -247,6 +249,7 @@
 
     begin = tuple(start_ref[0, :, j * LANES : (j + 1) * LANES] for j in range(parts))
     lax.fori_loop(0, blocks, forward, begin)
+    middle()
     column = lax.broadcasted_iota(jnp.int32, (BLK, BLK * states), 1) // states
     row = lax.broadcasted_iota(jnp.int32, (BLK, BLK * states), 0)
     ones = jnp.where(column == row, 1.0, 0.0).astype(jnp.bfloat16)
@@ -292,7 +295,7 @@
         grad_log_ref[0, :, j * LANES : (j + 1) * LANES] = last[parts + j] * rates[j] * LN2
 
 
-def scan_call(kernel, name, sequences, states, operands, results, scratch):
+def scan_call(kernel, name, sequences, states, operands, results, scratch, early=None):
     tokens, width = next(value.shape for kind, value in operands if kind == "wide")
     steps = tokens // sequences
     specs = {
@@ -307,16 +310,38 @@
         "narrow": (tokens, BLK * states),
         "state": (sequences, states, width),
     }
+    in_specs = [specs[kind] for kind, _ in operands]
+    out_specs = [specs[kind] for kind in results]
+    out_shape = [jax.ShapeDtypeStruct(shapes[kind], jnp.float32) for kind in results]
+    sending = {}
+    if early:
+        planes, side, *moving = early
+        tails = [value.shape[4:] for value in moving[:2]]
+        kernel = functools.partial(kernel, planes, side)
+        whole, anywhere = (pl.BlockSpec(memory_space=space) for space in (pltpu.VMEM, pl.ANY))
+        in_specs += [whole, whole, anywhere]
+        out_specs += [whole, whole, anywhere]
+        out_shape += [jax.ShapeDtypeStruct((planes,) + tail, jnp.bfloat16) for tail in tails]
+        out_shape.append(jax.ShapeDtypeStruct(moving[2].shape, jnp.bfloat16))
+        operands = operands + [("early", value) for value in moving]
+        semaphores = stage_semaphores(2, planes, side)[:5]
+        scratch = scratch + scatter_buffers(tails, planes, side)
+        scratch = scratch + [pltpu.VMEM((planes,) + tail, jnp.bfloat16) for tail in tails]
+        scratch = scratch + semaphores + semaphores
+        scratch = scratch + [pltpu.SemaphoreType.DMA, pltpu.SemaphoreType.DMA]
+        sending = dict(collective_id=6, has_side_effects=True)
     return pl.pallas_call(
         kernel,
         name=name,
         grid=(sequences, width // GROUP),
-        in_specs=[specs[kind] for kind, _ in operands],
-        out_specs=[specs[kind] for kind in results],
-        out_shape=[jax.ShapeDtypeStruct(shapes[kind], jnp.float32) for kind in results],
+        in_specs=in_specs,
+        out_specs=out_specs,
+        out_shape=out_shape,
         scratch_shapes=scratch,
         compiler_params=pltpu.CompilerParams(
-            dimension_semantics=("arbitrary", "arbitrary"), vmem_limit_bytes=VMEM_BYTES
+            dimension_semantics=("arbitrary", "arbitrary"),
+            vmem_limit_bytes=VMEM_BYTES,
+            **sending,
         ),
         cost_estimate=pl.CostEstimate(
             flops=20 * tokens * states * width,
@@ -492,187 +517,802 @@
     )(local_end, delta_sum, own_rates)
 
 
-def total_kernel(planes, chips, count, *refs):
-    given, results = refs[:count], refs[count : 2 * count]
-    halves, slots, sums, finals = (refs[(2 + i) * count : (3 + i) * count] for i in range(4))
-    sends, arrivals = refs[6 * count : 6 * count + 6], refs[6 * count + 6 :]
-    plane, member = lax.axis_index("seq"), lax.axis_index("exp")
-    chip, core = member // 2, lax.rem(member, 2)
-    partner = member + 1 - 2 * core
+class Sums:
+    def __init__(self, planes, side, sends, arrivals):
+        self.planes, self.side = planes, side
+        self.plane, self.member = lax.axis_index("seq"), lax.axis_index("exp")
+        chip, self.core = self.member // 2, lax.rem(self.member, 2)
+        high, low = chip // side, lax.rem(chip, side)
+        self.first = low + (high - low) * self.core
+        self.second = high + (low - high) * self.core
+        self.partner = self.member + 1 - 2 * self.core
+        self.sends, self.arrivals = sends, arrivals
+
+    def chip_at(self, first, second):
+        low = first + (second - first) * self.core
+        high = second + (first - second) * self.core
+        return (high * self.side + low) * 2 + self.core
+
+    def first_peer(self, k):
+        other = lax.rem(self.first + k, self.side)
+        return other, self.chip_at(other, self.second)
+
+    def second_peer(self, k):
+        other = lax.rem(self.second + k, self.side)
+        return other, self.chip_at(self.first, other)
+
+    def plane_peer(self, k):
+        return lax.rem(self.plane + k, self.planes)
+
+    def signal_peers(self, barrier):
+        peers = [{"exp": self.partner}]
+        peers += [{"exp": self.first_peer(k)[1]} for k in range(1, self.side)]
+        peers += [{"exp": self.second_peer(k)[1]} for k in range(1, self.side)]
+        peers += [{"seq": self.plane_peer(k)} for k in range(1, self.planes)]
+        for peer in peers:
+            pl.semaphore_signal(barrier, inc=1, device_id=peer, device_id_type=MESH)
+        return len(peers)
+
+    def move(self, stage, at, slot, src, dst, axis, peer):
+        return remote(
+            src, dst, self.sends[stage].at[at], self.arrivals[stage].at[slot], axis, peer
+        )
+
+    def pair_half(self, i, given, half):
+        return self.move(0, i, i, given.at[1 - self.core], half, "exp", self.partner)
+
+    def scatter_first(self, i, k, half, slots, arriving):
+        other, device = self.first_peer(k)
+        slot = other if arriving else self.first
+        return self.move(1, (i, k), (i, slot), half.at[other], slots.at[slot], "exp", device)
+
+    def scatter_second(self, i, k, quarter, slots, arriving):
+        other, device = self.second_peer(k)
+        slot = other if arriving else self.second
+        return self.move(2, (i, k), (i, slot), quarter.at[other], slots.at[slot], "exp", device)
+
+    def scatter_plane(self, i, k, eighth, slots, arriving):
+        other = self.plane_peer(k)
+        slot = other if arriving else self.plane
+        return self.move(3, (i, k), (i, slot), eighth.at[other], slots.at[slot], "seq", other)
+
+    def gather_plane(self, i, k, block, arriving):
+        other = self.plane_peer(k)
+        slot = other if arriving else self.plane
+        return self.move(
+            4, (i, k), (i, slot), block.at[self.plane], block.at[slot], "seq", other
+        )
+
+    def gather_second(self, i, k, result, arriving):
+        other, device = self.second_peer(k)
+        slot = other if arriving else self.second
+        row = result.at[self.core, self.first]
+        return self.move(5, (i, k), (i, slot), row.at[self.second], row.at[slot], "exp", device)
+
+    def gather_first(self, i, k, result, arriving):
+        other, device = self.first_peer(k)
+        slot = other if arriving else self.first
+        own = result.at[self.core]
+        return self.move(6, (i, k), (i, slot), own.at[self.first], own.at[slot], "exp", device)
+
+    def pair_gather(self, i, k, result, arriving):
+        other = lax.rem(self.first + k, self.side)
+        low = lax.rem(self.partner // 2, self.side)
+        theirs = low + (self.partner // (2 * self.side) - low) * (1 - self.core)
+        other = lax.rem(theirs + k, self.side) if arriving else other
+        half = 1 - self.core if arriving else self.core
+        mine = result.at[self.core, lax.rem(self.first + k, self.side)]
+        return self.move(7, (i, k), (i, k), mine, result.at[half, other], "exp", self.partner)
+
+    def after_pair(self, i, given, half, slots):
+        self.pair_half(i, given, half).wait()
+        own = self.core
+        for at in range(self.side):
+            for to in range(self.side):
+                both = given[own, at, to].astype(jnp.float32) + half[at, to].astype(jnp.float32)
+                half[at, to] = both.astype(jnp.bfloat16)
+        for k in range(1, self.side):
+            self.scatter_first(i, k, half, slots, False).start()
+        slots[self.first] = half[self.first]
+
+    def after_first(self, i, half, slots, quarter, slots_two):
+        for k in range(1, self.side):
+            self.scatter_first(i, k, half, slots, True).wait_recv()
+        for at in range(self.side):
+            added = slots[0, at].astype(jnp.float32)
+            for k in range(1, self.side):
+                added = added + slots[k, at].astype(jnp.float32)
+            quarter[at] = added.astype(jnp.bfloat16)
+        for k in range(1, self.side):
+            self.scatter_second(i, k, quarter, slots_two, False).start()
+        slots_two[self.second] = quarter[self.second]
+
+    def after_second(self, i, quarter, slots_two, eighth, slots_three):
+        for k in range(1, self.side):
+            self.scatter_second(i, k, quarter, slots_two, True).wait_recv()
+        added = slots_two[0].astype(jnp.float32)
+        for k in range(1, self.side):
+            added = added + slots_two[k].astype(jnp.float32)
+        eighth[...] = added.astype(jnp.bfloat16)
+        for k in range(1, self.planes):
+            self.scatter_plane(i, k, eighth, slots_three, False).start()
+        slots_three[self.plane] = eighth[self.plane]
+
+    def after_planes(self, i, eighth, slots_three, block):
+        for k in range(1, self.planes):
+            self.scatter_plane(i, k, eighth, slots_three, True).wait_recv()
+        added = slots_three[0].astype(jnp.float32)
+        for k in range(1, self.planes):
+            added = added + slots_three[k].astype(jnp.float32)
+        block[self.plane] = added.astype(jnp.bfloat16)
+        for k in range(1, self.planes):
+            self.gather_plane(i, k, block, False).start()
+
+    def planes_gathered(self, i, block):
+        for k in range(1, self.planes):
+            self.gather_plane(i, k, block, True).wait_recv()
+
+    def scatter_sent(self, i, half, slots, quarter, slots_two, eighth, slots_three, block):
+        for k in range(1, self.side):
+            self.scatter_first(i, k, half, slots, False).wait_send()
+            self.scatter_second(i, k, quarter, slots_two, False).wait_send()
+        for k in range(1, self.planes):
+            self.scatter_plane(i, k, eighth, slots_three, False).wait_send()
+            self.gather_plane(i, k, block, False).wait_send()
+
+    def gather_start(self, i, block, result):
+        result[self.core, self.first, self.second] = block[...]
+        for k in range(1, self.side):
+            self.gather_second(i, k, result, False).start()
+
+    def gather_across(self, i, result):
+        for k in range(1, self.side):
+            self.gather_second(i, k, result, True).wait_recv()
+        for k in range(1, self.side):
+            self.gather_first(i, k, result, False).start()
+        self.pair_gather(i, 0, result, False).start()
+
+    def gather_pass(self, i, result):
+        for k in range(1, self.side):
+            self.gather_first(i, k, result, True).wait_recv()
+            self.pair_gather(i, k, result, False).start()
+
+    def gather_end(self, i, result):
+        for k in range(self.side):
+            self.pair_gather(i, k, result, True).wait_recv()
+            self.pair_gather(i, k, result, False).wait_send()
+        for k in range(1, self.side):
+            self.gather_first(i, k, result, False).wait_send()
+            self.gather_second(i, k, result, False).wait_send()
+
+
+def stage_semaphores(count, planes, side):
+    each = [(count,)] + [(count, size) for size in (side, side, planes, planes, side, side, side)]
+    return [pltpu.SemaphoreType.DMA(shape) for shape in each]
+
+
+def scatter_buffers(tails, planes, side):
+    leads = [(side, side, planes), (side, side, planes), (side, planes), (side, planes)]
+    leads += [(planes,), (planes,)]
+    return [pltpu.VMEM(lead + tail, jnp.bfloat16) for lead in leads for tail in tails]
+
+
+def neighbour_plane():
+    plane = lax.axis_index("seq")
+    return {"seq": plane + 1 - 2 * lax.rem(plane, 2)}
+
+
+def swapped(src, dst, send, arrive):
+    return pltpu.make_async_remote_copy(
+        src_ref=src,
+        dst_ref=dst,
+        send_sem=send,
+        recv_sem=arrive,
+        device_id=neighbour_plane(),
+        device_id_type=MESH,
+    )
+
+
+class Routes:
+    def __init__(self, planes, members, sends, arrivals, local):
+        self.planes, self.members = planes, members
+        self.plane, self.member = lax.axis_index("seq"), lax.axis_index("exp")
+        self.hops = planes // 2
+        self.sends, self.arrivals, self.local = sends, arrivals, local
+        self.pairs = [
+            (hop, k) for hop in reversed(range(self.hops)) for k in range(members) if hop or k
+        ]
+
+    def device(self, hop, k):
+        return {
+            "seq": lax.rem(self.plane + 2 * hop, self.planes),
+            "exp": lax.rem(self.member + k, self.members),
+        }
+
+    def signal_peers(self, barrier):
+        for hop, k in self.pairs:
+            pl.semaphore_signal(
+                barrier, inc=1, device_id=self.device(hop, k), device_id_type=MESH
+            )
+        return len(self.pairs)
+
+    def moved(self, given, landed, returning, hop, k, arriving):
+        device = self.device(hop, k)
+        other = device["exp"]
+        slot = hop if arriving else (-hop) % self.hops
+        sender = other if arriving else self.member
+        return pltpu.make_async_remote_copy(
+            src_ref=given.at[hop, other] if returning else given.at[other],
+            dst_ref=landed.at[slot, sender],
+            send_sem=self.sends.at[hop, k],
+            recv_sem=self.arrivals.at[slot, sender],
+            device_id=device,
+            device_id_type=MESH,
+        )
+
+    def own(self, given, landed, returning):
+        src = given.at[0, self.member] if returning else given.at[self.member]
+        return pltpu.make_async_copy(src, landed.at[0, self.member], self.local)
+
+    def start(self, given, landed, returning):
+        for hop, k in self.pairs:
+            self.moved(given, landed, returning, hop, k, False).start()
+        self.own(given, landed, returning).start()
+
+    def wait(self, given, landed, returning):
+        for hop, k in self.pairs:
+            self.moved(given, landed, returning, hop, k, True).wait_recv()
+        self.own(given, landed, returning).wait()
+        for hop, k in self.pairs:
+            self.moved(given, landed, returning, hop, k, False).wait_send()
+
+
+def route_semaphores(planes, members):
+    shape = (planes // 2, members)
+    return [
+        pltpu.SemaphoreType.DMA(shape),
+        pltpu.SemaphoreType.DMA(shape),
+        pltpu.SemaphoreType.DMA,
+    ]
+
+
+def two_part(left, right, dims):
+    high = left.astype(jnp.bfloat16)
+    rest = (left - high.astype(jnp.float32)).astype(jnp.bfloat16)
+    numbers = (dims, ((), ()))
+    wide = jnp.float32
+    return lax.dot_general(high, right, numbers, preferred_element_type=wide) + lax.dot_general(
+        rest, right, numbers, preferred_element_type=wide
+    )
+
+
+def finish_kernel(
+    planes,
+    side,
+    grad_delta_ref,
+    grad_conv_ref,
+    grad_in_ref,
+    grad_out_ref,
+    grad_log_ref,
+    grad_scan_ref,
+    delta_pre_ref,
+    delta_low_ref,
+    conv_ref,
+    conv_pre_ref,
+    extended_ref,
+    normed_ref,
+    normed_gate_ref,
+    layer_ref,
+    grad_resid_ref,
+    delta_proj_ref,
+    state_proj_ref,
+    in_proj_ref,
+    conv_weight_ref,
+    skip_ref,
+    mixer_gain_ref,
+    skip_grad_ref,
+    norm_grad_ref,
+    router_grad_ref,
+    early_out_ref,
+    early_gate_ref,
+    returned_ref,
+    far_ref,
+    in_grad_ref,
+    total_out_ref,
+    total_gate_ref,
+    total_left_ref,
+    total_right_ref,
+    total_small_ref,
+    landed_ref,
+    near_ref,
+    slopes,
+    low_grads,
+    padded,
+    grad_inner,
+    small,
+    rim_out,
+    rim_in,
+    *rest,
+):
+    givens, buffers, (rim_sent, rim_landed) = rest[:3], rest[3:21], rest[21:23]
+    semaphores = rest[23:]
+    routes = Routes(planes, 2 * side * side, *semaphores[16:19])
+    cut_rows = far_ref.shape[1] // 2
+    swaps = [
+        swapped(far_ref.at[:, at], near_ref.at[:, at], semaphores[19].at[i], semaphores[20].at[i])
+        for i, at in enumerate((pl.ds(0, cut_rows), pl.ds(cut_rows, cut_rows)))
+    ]
+    totals = (total_left_ref, total_right_ref, total_small_ref)
+    tail = [tuple(buffers[3 * stage + i] for stage in range(6)) for i in range(3)]
+    chips = side * side
+    tokens, inner_width = grad_delta_ref.shape
+    width = layer_ref.shape[1]
+    low_rank = delta_low_ref.shape[1]
+    taps = conv_weight_ref.shape[0]
+    sequences = extended_ref.shape[0]
+    piece = tokens // sequences
+    states = grad_log_ref.shape[1]
+    wide, half = jnp.float32, jnp.bfloat16
+    sums = Sums(planes, side, semaphores[:8], semaphores[8:16])
+    place = sums.plane * (2 * chips) + sums.member
+    devices = 2 * chips * planes
+    before, after = lax.rem(place + devices - 1, devices), lax.rem(place + 1, devices)
+
+    def device(at):
+        return {"seq": at // (2 * chips), "exp": lax.rem(at, 2 * chips)}
+
     barrier = pltpu.get_barrier_semaphore()
-    pl.semaphore_signal(barrier, inc=1, device_id={"exp": partner}, device_id_type=MESH)
-
-    def chip_peer(k):
-        other = lax.rem(chip + k, chips)
-        return other, other * 2 + core
-
-    def plane_peer(k):
-        return lax.rem(plane + k, planes)
-
-    for k in range(1, chips):
-        pl.semaphore_signal(
-            barrier, inc=1, device_id={"exp": chip_peer(k)[1]}, device_id_type=MESH
-        )
-    for k in range(1, planes):
-        pl.semaphore_signal(
-            barrier, inc=1, device_id={"seq": plane_peer(k)}, device_id_type=MESH
-        )
-    pl.semaphore_wait(barrier, chips + planes - 1)
-
-    def pair_half(i):
-        return remote(
-            given[i].at[1 - core], halves[i], sends[0].at[i], arrivals[0].at[i], "exp", partner
-        )
-
-    def scatter_chip(i, k, arriving):
-        other, device = chip_peer(k)
-        slot = other if arriving else chip
-        return remote(
-            halves[i].at[other],
-            slots[i].at[slot],
-            sends[1].at[i, k],
-            arrivals[1].at[i, slot],
-            "exp",
-            device,
-        )
-
-    def scatter_plane(i, k, arriving):
-        other = plane_peer(k)
-        slot = other if arriving else plane
-        return remote(
-            sums[i].at[other],
-            finals[i].at[slot],
-            sends[2].at[i, k],
-            arrivals[2].at[i, slot],
-            "seq",
-            other,
-        )
-
-    def gather_plane(i, k, arriving):
-        other = plane_peer(k)
-        slot = other if arriving else plane
-        return remote(
-            results[i].at[core, chip, plane],
-            results[i].at[core, chip, slot],
-            sends[3].at[i, k],
-            arrivals[3].at[i, slot],
-            "seq",
-            other,
-        )
-
-    def gather_chip(i, k, arriving):
-        other, device = chip_peer(k)
-        slot = other if arriving else chip
-        return remote(
-            results[i].at[core, chip],
-            results[i].at[core, slot],
-            sends[4].at[i, k],
-            arrivals[4].at[i, slot],
-            "exp",
-            device,
-        )
-
-    def pair_gather(i, k, arriving):
-        other = lax.rem(chip + k, chips)
-        half = 1 - core if arriving else core
-        return remote(
-            results[i].at[core, other],
-            results[i].at[half, other],
-            sends[5].at[i, k],
-            arrivals[5].at[i, other],
-            "exp",
-            partner,
-        )
-
+    for peer in (before, after):
+        pl.semaphore_signal(barrier, inc=1, device_id=device(peer), device_id_type=MESH)
+    pl.semaphore_signal(barrier, inc=1, device_id=neighbour_plane(), device_id_type=MESH)
+    greeted = 3 + sums.signal_peers(barrier) + routes.signal_peers(barrier)
+    pl.semaphore_wait(barrier, greeted)
+    early = [(total_out_ref, early_out_ref), (total_gate_ref, early_gate_ref)]
+    for i, (result, own) in enumerate(early):
+        sums.gather_start(i, own, result)
+    swaps[0].start()
+
+    unit = 256
+    count = inner_width // unit
+    low_grads[...] = jnp.zeros(low_grads.shape, wide)
+    small[...] = jnp.zeros(small.shape, wide)
+
+    def lanes(j):
+        return pl.ds(pl.multiple_of(j * unit, unit), unit)
+
+    at_delta = low_rank + 2 * states
+    at_log = at_delta + low_rank
+    at_conv = at_log + states
+
+    def first(j, carry):
+        at = lanes(j)
+        slope = grad_delta_ref[:, at] * jax.nn.sigmoid(delta_pre_ref[:, at])
+        small[at_conv + taps + 1 : at_conv + taps + 2, at] = jnp.sum(slope, axis=0, keepdims=True)
+        small[at_delta:at_log, at] = rows_dot(delta_low_ref[...], slope, lax.Precision.HIGHEST)
+        low_grads[...] += two_part(slope, delta_proj_ref[:, at], ((1,), (1,)))
+        return carry
+
+    lax.fori_loop(0, count, first, 0)
+    for i, (result, _) in enumerate(early):
+        sums.gather_across(i, result)
+    block = grad_in_ref.shape[1] // states
+    column = lax.broadcasted_iota(jnp.int32, grad_in_ref.shape, 1) // states
+    row = lax.rem(lax.broadcasted_iota(jnp.int32, grad_in_ref.shape, 0), block)
+    fold = jnp.where(
+        lax.rem(lax.broadcasted_iota(jnp.int32, (grad_in_ref.shape[1], states), 0), states)
+        == lax.broadcasted_iota(jnp.int32, (grad_in_ref.shape[1], states), 1),
+        1.0,
+        0.0,
+    ).astype(half)
+
+    def folded(ref):
+        return two_part(jnp.where(column == row, ref[...], 0.0), fold, ((1,), (0,)))
+
+    coefs = jnp.concatenate([low_grads[...], folded(grad_in_ref), folded(grad_out_ref)], axis=1)
+    rim_out[...] = jnp.zeros(rim_out.shape, half)
+
+    def second(j, carry):
+        at = lanes(j)
+        small[:at_delta, at] = rows_dot(coefs, conv_ref[:, at], lax.Precision.HIGHEST)
+        through = two_part(coefs, state_proj_ref[:, at], ((1,), (0,)))
+        through = through + grad_scan_ref[:, at] * skip_ref[:, at] + grad_conv_ref[:, at]
+        pre = conv_pre_ref[:, at]
+        sigma = jax.nn.sigmoid(pre)
+        through = through * (sigma * (1.0 + pre * (1.0 - sigma)))
+        small[at_conv + taps : at_conv + taps + 1, at] = jnp.sum(through, axis=0, keepdims=True)
+        for q in range(sequences):
+            padded[q, :8] = jnp.zeros((8, unit), wide)
+            padded[q, 8 + piece :] = jnp.zeros((8, unit), wide)
+            padded[q, 8 : 8 + piece] = through[q * piece : (q + 1) * piece]
+            result = jnp.zeros((piece, unit), wide)
+            rim = jnp.zeros((8, unit), wide)
+            for tap in range(taps):
+                weight = conv_weight_ref[tap : tap + 1, at]
+                shift = taps - 1 - tap
+                result = result + weight * padded[q, 8 + shift : 8 + shift + piece]
+                rim = rim + weight * padded[q, 8 - tap : 16 - tap]
+            grad_inner[q * piece : (q + 1) * piece, at] = result
+            rim_out[q, 8 - (taps - 1) :, at] = rim[: taps - 1].astype(half)
+        for tap in range(taps):
+            start = 8 - (taps - 1) + tap
+            product = jnp.zeros((1, unit), wide)
+            for q in range(sequences):
+                product = product + jnp.sum(
+                    padded[q, 8 : 8 + piece] * extended_ref[q, start : start + piece, at],
+                    axis=0,
+                    keepdims=True,
+                )
+            small[at_conv + tap : at_conv + tap + 1, at] = product
+        return carry
+
+    lax.fori_loop(0, count, second, 0)
+    rim_copy = pltpu.make_async_remote_copy(
+        src_ref=rim_out,
+        dst_ref=rim_in,
+        send_sem=rim_sent,
+        recv_sem=rim_landed,
+        device_id=device(before),
+        device_id_type=MESH,
+    )
+    rim_copy.start()
+    routes.start(returned_ref, landed_ref, True)
+    swaps[1].start()
+    for i, (result, _) in enumerate(early):
+        sums.gather_pass(i, result)
+    at_end = at_conv + taps + 2
+    log_total = grad_log_ref[0]
+    for q in range(1, sequences):
+        log_total = log_total + grad_log_ref[q]
+    small[at_log:at_conv] = log_total
+    small[at_end : at_end + 1] = skip_grad_ref[...]
+    small[at_end + 1 : at_end + 2, width:] = norm_grad_ref[...]
+    for k in range(router_grad_ref.shape[0]):
+        line = at_end + 2 + k // 2
+        small[line : line + 1, (k % 2) * width : (k % 2 + 1) * width] = router_grad_ref[k : k + 1]
+    rim_copy.wait()
+    keep = jnp.where(place < devices - 1, 1.0, 0.0)
+    for q in range(sequences):
+        rows = slice((q + 1) * piece - 8, (q + 1) * piece)
+        grad_inner[rows, :] += keep * rim_in[q].astype(wide)
+    slopes[...] = grad_inner[...].astype(half)
+    tall = width // chips
+    size = tall // planes
+    cut = size // 2
+    for c in range(2):
+        for m in range(chips):
+            product = rows_dot(
+                normed_ref[:, m * tall : (m + 1) * tall], slopes[:, c * width : (c + 1) * width]
+            ).astype(half)
+            for z in range(planes):
+                givens[0][c, m // side, m % side, z] = product[z * size : z * size + cut]
+                givens[1][c, m // side, m % side, z] = product[z * size + cut : (z + 1) * size]
+    for i in range(2):
+        sums.pair_half(i, givens[i], tail[i][0]).start()
+    normed_grad = normed_gate_ref[...] + cols_dot(slopes[...], in_proj_ref[...])
+    layer = layer_ref[...].astype(wide)
+    scaling = lax.rsqrt(jnp.mean(layer * layer, axis=-1, keepdims=True) + EPSILON)
+    normal = layer * scaling
+    small[at_end + 1 : at_end + 2, :width] = jnp.sum(normed_grad * normal, axis=0, keepdims=True)
+    low = givens[2].shape[4]
+    for c in range(2):
+        for m in range(chips):
+            for z in range(planes):
+                line = (m * planes + z) * low
+                givens[2][c, m // side, m % side, z] = small[
+                    line : line + low, c * width : (c + 1) * width
+                ].astype(half)
+    sums.pair_half(2, givens[2], tail[2][0]).start()
+    every = range(3)
+    for i in every:
+        sums.after_pair(i, givens[i], *tail[i][:2])
+    weighted = normed_grad * mixer_gain_ref[...]
+    in_grad_ref[...] = grad_resid_ref[...] + scaling * (
+        weighted - normal * jnp.mean(weighted * normal, axis=-1, keepdims=True)
+    )
+    for i in every:
+        sums.after_first(i, *tail[i][:4])
+    for i in every:
+        sums.after_second(i, *tail[i][2:6])
+    blocks = [total.at[sums.core, sums.first, sums.second] for total in totals]
+    for i in every:
+        sums.after_planes(i, *tail[i][4:6], blocks[i])
+    for i in every:
+        sums.planes_gathered(i, blocks[i])
+        for k in range(1, side):
+            sums.gather_second(2 + i, k, totals[i], False).start()
+    for i in every:
+        sums.gather_across(2 + i, totals[i])
+    for i in every:
+        sums.gather_pass(2 + i, totals[i])
+    for i, (result, _) in enumerate(early):
+        sums.gather_end(i, result)
+    routes.wait(returned_ref, landed_ref, True)
+    for swap in swaps:
+        swap.wait()
+    for i in every:
+        sums.scatter_sent(i, *tail[i], blocks[i])
+        sums.gather_end(2 + i, totals[i])
+
+
+def finish(operands, small_height, side):
+    planes = lax.axis_size("seq")
+    tokens, inner_width = operands[0].shape
+    layer = operands[13]
+    width = layer.shape[1]
+    sequences = operands[4].shape[0]
+    low = -(-small_height // (side * side * planes))
+    lead = (2, side, side, planes)
+    big = lead + operands[24].shape[1:]
+    split = lead + (big[4] // 2, width)
+    little = lead + (low, width)
+    tails = [split[4:], split[4:], little[4:]]
+    vmem, anywhere = (pl.BlockSpec(memory_space=space) for space in (pltpu.VMEM, pl.ANY))
+    half, wide = jnp.bfloat16, jnp.float32
+    moved = [jax.ShapeDtypeStruct(value.shape, half) for value in operands[-2:]]
+    return pl.pallas_call(
+        functools.partial(finish_kernel, planes, side),
+        name="finish_gradients",
+        in_specs=[vmem] * (len(operands) - 2) + [anywhere] * 2,
+        out_specs=[vmem] * 6 + [anywhere] * 2,
+        out_shape=[jax.ShapeDtypeStruct((tokens, width), wide)]
+        + [jax.ShapeDtypeStruct(shape, half) for shape in (big, big, split, split, little)]
+        + moved,
+        scratch_shapes=[
+            pltpu.VMEM((tokens, inner_width), half),
+            pltpu.VMEM((tokens, operands[7].shape[1]), wide),
+            pltpu.VMEM((sequences, tokens // sequences + 16, 256), wide),
+            pltpu.VMEM((tokens, inner_width), wide),
+            pltpu.VMEM((low * side * side * planes, inner_width), wide),
+            pltpu.VMEM((sequences, 8, inner_width), half),
+            pltpu.VMEM((sequences, 8, inner_width), half),
+            pltpu.VMEM(split, half),
+            pltpu.VMEM(split, half),
+            pltpu.VMEM(little, half),
+        ]
+        + scatter_buffers(tails, planes, side)
+        + [pltpu.SemaphoreType.DMA, pltpu.SemaphoreType.DMA]
+        + stage_semaphores(5, planes, side)
+        + stage_semaphores(5, planes, side)
+        + route_semaphores(planes, 2 * side * side)
+        + [pltpu.SemaphoreType.DMA((2,)), pltpu.SemaphoreType.DMA((2,))],
+        compiler_params=pltpu.CompilerParams(
+            collective_id=3, has_side_effects=True, vmem_limit_bytes=60 * 1024 * 1024
+        ),
+        cost_estimate=pl.CostEstimate(flops=10**8, transcendentals=0, bytes_accessed=2 * 10**8),
+    )(*operands)
+
+
+def backward_sum_kernel(planes, side, *refs):
+    inputs, given, far_ref, results, owns = refs[:9], refs[9:11], refs[11], refs[12:17], refs[17:19]
+    near_ref, scratch, buffers, semaphores = refs[19], refs[20:25], refs[25:37], refs[39:]
+    blocks = refs[37:39]
+    halves, slots, quarters, slots_two, eighths, slots_three = (
+        buffers[2 * i : 2 * i + 2] for i in range(6)
+    )
+    sums = Sums(planes, side, semaphores[:5], semaphores[5:10])
+    swap = swapped(far_ref, near_ref, *semaphores[10:])
+    step = pl.program_id(0) * pl.num_programs(1) + pl.program_id(1)
+    last = pl.num_programs(0) * pl.num_programs(1) - 1
+
+    def begin(_):
+        barrier = pltpu.get_barrier_semaphore()
+        pl.semaphore_signal(barrier, inc=1, device_id=neighbour_plane(), device_id_type=MESH)
+        pl.semaphore_wait(barrier, sums.signal_peers(barrier) + 1)
+        for i in range(2):
+            sums.pair_half(i, given[i], halves[i]).start()
+        swap.start()
+
+    def pairs(i):
+        sums.after_pair(i, given[i], halves[i], slots[i])
+
+    def firsts(i):
+        sums.after_first(i, halves[i], slots[i], quarters[i], slots_two[i])
+
+    def seconds(i):
+        sums.after_second(i, quarters[i], slots_two[i], eighths[i], slots_three[i])
+
+    def across(i):
+        sums.after_planes(i, eighths[i], slots_three[i], blocks[i])
+
+    def at(point, stage, which):
+        @pl.when(step == point)
+        def _():
+            for i in which:
+                stage(i)
+
+    at(0, begin, [0])
+    at(1, pairs, [0, 1])
+    at(3, firsts, [0])
+    at(4, seconds, [0])
+    at(last, across, [0])
+
+    def middle():
+        at(3, firsts, [1])
+        at(4, seconds, [1])
+        at(last, across, [1])
+
+    backward_kernel(middle, *inputs, *results, *scratch)
+
+    @pl.when(step == last)
+    def _():
+        for i in range(2):
+            sums.planes_gathered(i, blocks[i])
+            owns[i][...] = blocks[i][...]
+            parts = (halves, slots, quarters, slots_two, eighths, slots_three, blocks)
+            sums.scatter_sent(i, *(part[i] for part in parts))
+        swap.wait()
+
+
+def dispatch_kernel(planes, members, returning, given, landed, *semaphores):
+    routes = Routes(planes, members, *semaphores)
+    barrier = pltpu.get_barrier_semaphore()
+    pl.semaphore_wait(barrier, routes.signal_peers(barrier))
+    routes.start(given, landed, returning)
+    routes.wait(given, landed, returning)
+
+
+def dispatch(values, returning, collective_id, name):
+    planes, members = lax.axis_size("seq"), lax.axis_size("exp")
+    anywhere = pl.BlockSpec(memory_space=pl.ANY)
+    shape = (planes // 2, members) + values.shape[-2:]
+    return pl.pallas_call(
+        functools.partial(dispatch_kernel, planes, members, returning),
+        name=name,
+        in_specs=[anywhere],
+        out_specs=anywhere,
+        out_shape=jax.ShapeDtypeStruct(shape, jnp.bfloat16),
+        scratch_shapes=route_semaphores(planes, members),
+        compiler_params=pltpu.CompilerParams(collective_id=collective_id, has_side_effects=True),
+        cost_estimate=pl.CostEstimate(flops=10**6, transcendentals=0, bytes_accessed=5 * 10**7),
+    )(values)
+
+
+def expert_kernel(
+    rows_ref,
+    grads_ref,
+    up_ref,
+    down_ref,
+    near_up_ref,
+    near_down_ref,
+    router_ref,
+    chosen_ref,
+    out_ref,
+    grad_row_ref,
+    grad_up_ref,
+    grad_down_ref,
+    far_up_ref,
+    far_down_ref,
+    grad_router_ref,
+    sent,
+    out_sum,
+    row_sum,
+    hidden,
+    grad_pre,
+    shares_kept,
+):
+    count = rows_ref.shape[0]
+    step = pl.program_id(0)
+    chunk = count // 4
     wide, half = jnp.float32, jnp.bfloat16
-    for i in range(count):
-        pair_half(i).start()
-    for i in range(count):
-        pair_half(i).wait()
-        halves[i][...] = (given[i][core].astype(wide) + halves[i][...].astype(wide)).astype(half)
-        for k in range(1, chips):
-            scatter_chip(i, k, False).start()
-        slots[i][chip] = halves[i][chip]
-    for i in range(count):
-        for k in range(1, chips):
-            scatter_chip(i, k, True).wait_recv()
-        added = slots[i][0].astype(wide)
-        for k in range(1, chips):
-            added = added + slots[i][k].astype(wide)
-        sums[i][...] = added.astype(half)
-        for k in range(1, planes):
-            scatter_plane(i, k, False).start()
-        finals[i][plane] = sums[i][plane]
-    for i in range(count):
-        for k in range(1, planes):
-            scatter_plane(i, k, True).wait_recv()
-        added = finals[i][0].astype(wide)
-        for k in range(1, planes):
-            added = added + finals[i][k].astype(wide)
-        results[i][core, chip, plane] = added.astype(half)
-        for k in range(1, planes):
-            gather_plane(i, k, False).start()
-    for i in range(count):
-        for k in range(1, planes):
-            gather_plane(i, k, True).wait_recv()
-        for k in range(1, chips):
-            gather_chip(i, k, False).start()
-        pair_gather(i, 0, False).start()
-    for i in range(count):
-        for k in range(1, chips):
-            gather_chip(i, k, True).wait_recv()
-            pair_gather(i, k, False).start()
-    for i in range(count):
-        for k in range(chips):
-            pair_gather(i, k, True).wait_recv()
-            pair_gather(i, k, False).wait_send()
-        for k in range(1, chips):
-            scatter_chip(i, k, False).wait_send()
-            gather_chip(i, k, False).wait_send()
-        for k in range(1, planes):
-            scatter_plane(i, k, False).wait_send()
-            gather_plane(i, k, False).wait_send()
-
-
-def total(arrays, collective_id, name):
-    planes, members = lax.axis_size("seq"), lax.axis_size("exp")
-    chips, count = members // 2, len(arrays)
-    shaped = [
-        value.reshape((2, chips, planes, value.shape[0] // (members * planes), value.shape[1]))
-        for value in arrays
-    ]
-    tails = [value.shape[3:] for value in shaped]
-    vmem = pl.BlockSpec(memory_space=pltpu.VMEM)
-
-    def scratch(*lead):
-        return [pltpu.VMEM(lead + tail, jnp.bfloat16) for tail in tails]
-
-    semaphores = [
-        pltpu.SemaphoreType.DMA((count,)),
-        pltpu.SemaphoreType.DMA((count, chips)),
-        pltpu.SemaphoreType.DMA((count, planes)),
-        pltpu.SemaphoreType.DMA((count, planes)),
-        pltpu.SemaphoreType.DMA((count, chips)),
-        pltpu.SemaphoreType.DMA((count, chips)),
-    ]
-    results = pl.pallas_call(
-        functools.partial(total_kernel, planes, chips, count),
-        name=name,
-        in_specs=[vmem] * count,
-        out_specs=[vmem] * count,
-        out_shape=[jax.ShapeDtypeStruct(value.shape, jnp.bfloat16) for value in shaped],
-        scratch_shapes=scratch(chips, planes)
-        + scratch(chips, planes)
-        + scratch(planes)
-        + scratch(planes)
-        + semaphores
-        + semaphores,
+
+    def chunks(body):
+        def run(i, carry):
+            body(pl.ds(pl.multiple_of(i * chunk, chunk), chunk))
+            return carry
+
+        lax.fori_loop(0, count // chunk, run, 0)
+
+    @pl.when(step == 0)
+    def _():
+        def prepare(at):
+            logits = lax.dot_general(
+                rows_ref[at, :].astype(wide),
+                router_ref[...],
+                (((1,), (1,)), ((), ())),
+                precision=lax.Precision.HIGHEST,
+                preferred_element_type=wide,
+            )
+            raised = jnp.exp(logits - jnp.max(logits, axis=-1, keepdims=True))
+            shares = raised / jnp.sum(raised, axis=-1, keepdims=True)
+            gate = jnp.sum(shares * chosen_ref[...], axis=-1, keepdims=True)
+            shares_kept[at, :] = shares
+            sent[at, :] = (gate * grads_ref[at, :].astype(wide)).astype(half)
+            out_sum[at, :] = jnp.zeros((chunk, out_sum.shape[1]), wide)
+            row_sum[at, :] = jnp.zeros((chunk, row_sum.shape[1]), wide)
+
+        chunks(prepare)
+
+    def apply(up, down, at):
+        pre = half_dot(rows_ref[at, :], up)
+        phi = 0.5 * (1.0 + lax.erf(pre * 0.7071067811865476))
+        slope = phi + pre * (jnp.exp(-0.5 * pre * pre) * 0.3989422804014327)
+        active = (pre * phi).astype(half)
+        hidden[at, :] = active
+        out_sum[at, :] += half_dot(active, down)
+        back = (slope * cols_dot(sent[at, :], down)).astype(half)
+        grad_pre[at, :] = back
+        row_sum[at, :] += cols_dot(back, up)
+
+    chunks(functools.partial(apply, up_ref[0], down_ref[0]))
+    grad_up_ref[0] = rows_dot(rows_ref[...], grad_pre[...])
+    grad_down_ref[0] = rows_dot(hidden[...], sent[...])
+    chunks(functools.partial(apply, near_up_ref[0], near_down_ref[0]))
+    far_up_ref[0] = rows_dot(rows_ref[...], grad_pre[...]).astype(half)
+    far_down_ref[0] = rows_dot(hidden[...], sent[...]).astype(half)
+
+    @pl.when(step == pl.num_programs(0) - 1)
+    def _():
+        grad_router_ref[...] = jnp.zeros(grad_router_ref.shape, wide)
+
+        def finish(at):
+            shares = shares_kept[at, :]
+            chosen = chosen_ref[...]
+            gate = jnp.sum(shares * chosen, axis=-1, keepdims=True)
+            grad_gate = jnp.sum(
+                grads_ref[at, :].astype(wide) * out_sum[at, :], axis=-1, keepdims=True
+            )
+            grad_logits = grad_gate * gate * (chosen - shares)
+            out_ref[at, :] = (gate * out_sum[at, :]).astype(half)
+            grad_row_ref[at, :] = (
+                row_sum[at, :]
+                + jnp.dot(
+                    grad_logits,
+                    router_ref[...],
+                    precision=lax.Precision.HIGHEST,
+                    preferred_element_type=wide,
+                )
+            ).astype(half)
+            grad_router_ref[...] += rows_dot(
+                grad_logits, rows_ref[at, :].astype(wide), lax.Precision.HIGHEST
+            )
+
+        chunks(finish)
+
+
+def expert_apply(rows, grads, weights, router, chosen):
+    count, width = rows.shape
+    experts = router.shape[0]
+    up, down = weights[:2]
+    unit = 256
+    whole = pl.BlockSpec((count, width), lambda h: (0, 0))
+    up_block = pl.BlockSpec((1, width, unit), lambda h: (0, 0, h))
+    down_block = pl.BlockSpec((1, unit, width), lambda h: (0, h, 0))
+    router_block = pl.BlockSpec((experts, width), lambda h: (0, 0))
+    chosen_block = pl.BlockSpec((1, experts), lambda h: (0, 0))
+    both = [up_block, down_block]
+    half, wide = jnp.bfloat16, jnp.float32
+    return pl.pallas_call(
+        expert_kernel,
+        name="expert_apply",
+        grid=(up.shape[2] // unit,),
+        in_specs=[whole, whole] + both + both + [router_block, chosen_block],
+        out_specs=[whole, whole] + both + both + [router_block],
+        out_shape=[
+            jax.ShapeDtypeStruct((count, width), half),
+            jax.ShapeDtypeStruct((count, width), half),
+            jax.ShapeDtypeStruct(up.shape, wide),
+            jax.ShapeDtypeStruct(down.shape, wide),
+            jax.ShapeDtypeStruct(up.shape, half),
+            jax.ShapeDtypeStruct(down.shape, half),
+            jax.ShapeDtypeStruct(router.shape, wide),
+        ],
+        scratch_shapes=[
+            pltpu.VMEM((count, width), half),
+            pltpu.VMEM((count, width), wide),
+            pltpu.VMEM((count, width), wide),
+            pltpu.VMEM((count, unit), half),
+            pltpu.VMEM((count, unit), half),
+            pltpu.VMEM((count, experts), wide),
+        ],
         compiler_params=pltpu.CompilerParams(
-            collective_id=collective_id, has_side_effects=True, vmem_limit_bytes=VMEM_BYTES
+            dimension_semantics=("arbitrary",), vmem_limit_bytes=VMEM_BYTES
         ),
-        cost_estimate=pl.CostEstimate(flops=10**7, transcendentals=0, bytes_accessed=10**8),
-    )(*shaped)
-    return [result.reshape(value.shape) for result, value in zip(results, arrays)]
+        cost_estimate=pl.CostEstimate(
+            flops=24 * count * width * up.shape[2],
+            transcendentals=4 * count * up.shape[2],
+            bytes_accessed=3 * 10**7,
+        ),
+    )(rows, grads, *weights, router, chosen)
 
 
 def on_device(
@@ -711,10 +1351,12 @@
     gate_half = projected[:, inner_width:]
     inner_seq = inner.reshape(sequences, piece_len, inner_width)
     left_rim = shifted(inner_seq[:, piece_len - (taps - 1) :, :], ("seq", "exp"), 1)
-    extended = jnp.concatenate([left_rim, inner_seq], axis=1)
-    conv_pre = conv_bias + conv_weight[0] * extended[:, 0:piece_len, :]
+    lead = 8 - (taps - 1)
+    blank = jnp.zeros((sequences, lead, inner_width), jnp.float32)
+    extended = jnp.concatenate([blank, left_rim, inner_seq], axis=1)
+    conv_pre = conv_bias + conv_weight[0] * extended[:, lead : lead + piece_len, :]
     for tap in range(1, taps):
-        conv_pre = conv_pre + conv_weight[tap] * extended[:, tap : tap + piece_len, :]
+        conv_pre = conv_pre + conv_weight[tap] * extended[:, lead + tap : lead + tap + piece_len, :]
     conv_flat = jax.nn.silu(conv_pre).reshape(tokens, inner_width)
     projections = exact_dot(conv_flat, state_proj.astype(jnp.float32))
     delta_low = projections[:, :low_rank]
@@ -767,52 +1409,46 @@
     target = jnp.where(flat_slot < capacity, flat_ids * capacity + flat_slot, experts * capacity)
     slot_rows = jnp.arange(experts * capacity, dtype=jnp.int32)
     picks = (slot_rows[:, None] == target[None, :]).astype(jnp.bfloat16)
-    group = lax.axis_size("seq")
-    expert = lax.axis_index("exp")
-
-    def to_experts(values):
+    planes = lax.axis_size("seq")
+    hops = planes // 2
+
+    def along_planes(values, by):
+        pairs = [(at, (at + by) % planes) for at in range(planes)]
+        return lax.ppermute(values, "seq", pairs)
+
+    def with_neighbour(values):
+        pairs = [(at, at ^ 1) for at in range(planes)]
+        return lax.ppermute(values, "seq", pairs)
+
+    def swapped(values):
+        return lax.all_to_all(values, "exp", split_axis=0, concat_axis=0, tiled=True)
+
+    def to_slots(values):
         buffer = half_dot(picks, values).astype(jnp.bfloat16)
-        arrived = lax.all_to_all(
-            buffer.reshape(experts, capacity, width), "exp", split_axis=0, concat_axis=0, tiled=True
-        )
-        return lax.all_gather(arrived.reshape(senders * capacity, width), "seq", axis=0, tiled=True)
-
-    def to_tokens(partial):
-        mine = lax.psum_scatter(partial, "seq", scatter_dimension=0, tiled=True)
-        back = lax.all_to_all(
-            mine.reshape(senders, capacity, width), "exp", split_axis=0, concat_axis=0, tiled=True
-        )
-        return rows_dot(picks, back.reshape(experts * capacity, width))
-
-    grad_rows = to_experts(out_grad.reshape(tokens, width)).astype(jnp.float32)
-    rows = to_experts(routed)
-    rows_wide = rows.astype(jnp.float32)
-    shares = jax.nn.softmax(exact_dot(rows_wide, router_weight), axis=-1)
-    chosen = (jnp.arange(experts, dtype=jnp.int32) == expert).astype(jnp.float32)[None, :]
-    gate = jnp.sum(shares * chosen, axis=-1, keepdims=True)
-    up, down = expert_up[0], expert_down[0]
-    pre_act = half_dot(rows, up)
-    hidden_act, gelu_back = jax.vjp(exact_gelu, pre_act)
-    hidden_half = hidden_act.astype(jnp.bfloat16)
-    expert_out = half_dot(hidden_half, down)
-    grad_sent = (gate * grad_rows).astype(jnp.bfloat16)
-    grad_gate = jnp.sum(grad_rows * expert_out, axis=-1, keepdims=True)
-    grad_logits = grad_gate * gate * (chosen - shares)
-    grad_router = rows_dot(rows_wide, grad_logits, lax.Precision.HIGHEST)
-    grad_down = rows_dot(hidden_half, grad_sent)
-    grad_pre = gelu_back(cols_dot(grad_sent, down))[0].astype(jnp.bfloat16)
-    grad_up = rows_dot(rows, grad_pre)
-    grad_row_in = cols_dot(grad_pre, up) + cols_dot(
-        grad_logits, router_weight, lax.Precision.HIGHEST
-    )
-    grad_routed = to_tokens(grad_row_in.astype(jnp.bfloat16))
-    layer_out = (
-        (resid + to_tokens((gate * expert_out).astype(jnp.bfloat16)))
-        .astype(jnp.bfloat16)
-        .reshape(sequences, piece_len, width)
+        return buffer.reshape(experts, capacity, width)
+
+    weights = [expert_up, expert_down, with_neighbour(expert_up), with_neighbour(expert_down)]
+    near_grads = swapped(to_slots(out_grad.reshape(tokens, width)))
+    grad_rows = jnp.stack(
+        [near_grads] + [along_planes(near_grads, -2 * hop) for hop in range(1, hops)]
+    )
+    rows = dispatch(to_slots(routed), False, 4, "send_rows")
+    chosen = (
+        jnp.arange(experts, dtype=jnp.int32) == lax.axis_index("exp")
+    ).astype(jnp.float32)[None, :]
+    expert_out, grad_row_in, grad_up, grad_down, far_up, far_down, grad_router = expert_apply(
+        rows.reshape(hops * senders * capacity, width),
+        grad_rows.reshape(hops * senders * capacity, width),
+        weights,
+        router_weight.T,
+        chosen,
+    )
+    slotted = (hops, senders, capacity, width)
+    back_rows = dispatch(grad_row_in.reshape(slotted), True, 5, "return_rows")
+    grad_routed = rows_dot(
+        jnp.concatenate([picks] * hops, axis=0), back_rows.reshape(hops * senders * capacity, width)
     )
     grad_top = out_grad.reshape(tokens, width).astype(jnp.float32)
-    grad_up_own, grad_down_own = grad_up[None], grad_down[None]
     grad_resid_norm, grad_expert_norm = norm_backward(resid, scaling_two, expert_norm, grad_routed)
     grad_resid = grad_top + grad_resid_norm
     grad_mixer = grad_resid.astype(jnp.bfloat16)
@@ -835,8 +1471,26 @@
     )
     carried_back = exchange(gradient_first, delta_sum, decay_log, True)
     full_steps = pltpu.VMEM((piece_len, states, GROUP), jnp.float32)
-    grad_delta, grad_conv_scan, grad_in_wide, grad_out_wide, grad_log_parts = scan_call(
-        backward_kernel,
+    side = math.isqrt(senders // 2)
+    big = (2, side, side, planes, inner_width // (senders * planes), width)
+
+    def as_rows(values):
+        blocks = values.shape[1] // width
+        return jnp.concatenate(
+            [values[:, at * width : (at + 1) * width] for at in range(blocks)], axis=0
+        ).astype(jnp.bfloat16)
+
+    def as_columns(values):
+        return jnp.concatenate(
+            [values[at : at + width] for at in range(0, values.shape[0], width)], axis=1
+        ).astype(jnp.float32)
+
+    early = [
+        grad_out_proj.astype(jnp.bfloat16).reshape(big),
+        as_rows(grad_in_gate).reshape(big),
+    ]
+    *block_grads, own_out, own_gate, near_up = scan_call(
+        backward_sum_kernel,
         "backward_scan",
         sequences,
         states,
@@ -853,80 +1507,58 @@
         ],
         ["wide", "wide", "narrow", "narrow", "state"],
         [float_steps, full_steps, full_steps, stack_of, stack_of],
-    )
-    grad_decay_log = jnp.sum(grad_log_parts, axis=0)
-    grad_in_coef = undiagonal(grad_in_wide, BLK, states)
-    grad_out_coef = undiagonal(grad_out_wide, BLK, states)
-    grad_conv_act = grad_scan * skip_gain + grad_conv_scan
-    grad_delta_pre = grad_delta * jax.nn.sigmoid(delta_pre)
-    grad_delta_bias = jnp.sum(grad_delta_pre, axis=0)
-    grad_delta_proj = rows_dot(delta_low, grad_delta_pre, lax.Precision.HIGHEST)
-    grad_delta_low = cols_dot(grad_delta_pre, delta_proj.astype(jnp.float32), lax.Precision.HIGHEST)
-    grad_projections = jnp.concatenate([grad_delta_low, grad_in_coef, grad_out_coef], axis=-1)
-    grad_state_proj = rows_dot(conv_flat, grad_projections, lax.Precision.HIGHEST)
-    grad_conv_act = grad_conv_act + cols_dot(
-        grad_projections, state_proj.astype(jnp.float32), lax.Precision.HIGHEST
-    )
-    grad_conv_pre = grad_conv_act.reshape(sequences, piece_len, inner_width) * silu_slope(conv_pre)
-    grad_conv_bias = jnp.sum(grad_conv_pre, axis=(0, 1))
-    grad_conv_weight = jnp.stack(
+        [planes, side] + early + [far_up],
+    )
+    grad_delta, grad_conv_scan, grad_in_wide, grad_out_wide, grad_log_parts = block_grads
+    heights = [low_rank + 2 * states, low_rank, states, taps, 1, 1, 1, 1, experts // 2]
+    in_grad, sum_out, sum_gate, sum_left, sum_right, sum_small, back_out, near_down = finish(
         [
-            jnp.sum(grad_conv_pre * extended[:, tap : tap + piece_len, :], axis=(0, 1))
-            for tap in range(taps)
-        ]
-    )
-    grad_extended = jnp.zeros_like(extended)
-    for tap in range(taps):
-        grad_extended = grad_extended.at[:, tap : tap + piece_len, :].add(
-            conv_weight[tap] * grad_conv_pre
-        )
-    rim_back = shifted(
-        grad_extended[:, : taps - 1, :].astype(jnp.bfloat16), ("seq", "exp"), -1
-    ).astype(jnp.float32)
-    grad_inner = grad_extended[:, taps - 1 :, :].at[:, piece_len - (taps - 1) :, :].add(rim_back)
-    grad_inner = grad_inner.reshape(tokens, inner_width).astype(jnp.bfloat16)
-    grad_in_inner = rows_dot(normed_half, grad_inner)
-    grad_normed_one = grad_normed_gate + cols_dot(grad_inner, in_proj[:, :inner_width])
-    grad_flat_in, grad_mixer_gain = norm_backward(flat_in, scaling_one, mixer_gain, grad_normed_one)
-    in_grad = (grad_resid + grad_flat_in).reshape(sequences, piece_len, width)
-    def as_rows(values):
-        blocks = values.shape[1] // width
-        return jnp.concatenate(
-            [values[:, at * width : (at + 1) * width] for at in range(blocks)], axis=0
-        ).astype(jnp.bfloat16)
-
-    def as_columns(values):
-        return jnp.concatenate(
-            [values[at : at + width] for at in range(0, values.shape[0], width)], axis=1
-        ).astype(jnp.float32)
-
-    small = [
-        grad_state_proj.T,
-        grad_delta_proj,
-        grad_decay_log,
-        grad_conv_weight,
-        grad_conv_bias[None],
-        grad_delta_bias[None],
-        grad_skip_gain[None],
-        jnp.concatenate([grad_mixer_gain, grad_expert_norm])[None],
-        grad_router.T.reshape(experts * width // inner_width, inner_width),
-    ]
-    heights = [value.shape[0] for value in small]
-    devices = lax.axis_size("seq") * senders
-    spare = -sum(heights) % (devices // 2)
-    packed = as_rows(
-        jnp.concatenate(small + [jnp.zeros((spare, inner_width), jnp.float32)], axis=0)
-    )
-    sum_out, sum_gate, sum_inner, sum_small = total(
-        [grad_out_proj.astype(jnp.bfloat16), as_rows(grad_in_gate), as_rows(grad_in_inner), packed],
-        3,
-        "grad_total",
-    )
-    grad_in_proj = jnp.concatenate([as_columns(sum_inner), as_columns(sum_gate)], axis=1)
-    half_height = sum_small.shape[0] // 2
-    small_wide = jnp.concatenate([sum_small[:half_height], sum_small[half_height:]], axis=1).astype(
-        jnp.float32
-    )
+            grad_delta,
+            grad_conv_scan,
+            grad_in_wide,
+            grad_out_wide,
+            grad_log_parts,
+            grad_scan,
+            delta_pre,
+            delta_low,
+            conv_flat,
+            conv_pre.reshape(tokens, inner_width),
+            extended,
+            normed_half,
+            grad_normed_gate,
+            layer_in.reshape(tokens, width),
+            grad_resid,
+            delta_proj,
+            state_proj.T,
+            in_proj[:, :inner_width],
+            conv_weight,
+            skip_gain[None],
+            mixer_gain[None],
+            grad_skip_gain[None],
+            grad_expert_norm[None],
+            grad_router,
+            own_out,
+            own_gate,
+            expert_out.reshape(slotted),
+            far_down,
+        ],
+        sum(heights),
+        side,
+    )
+    grad_up_own = grad_up + near_up.astype(jnp.float32)
+    grad_down_own = grad_down + near_down.astype(jnp.float32)
+    token_out = rows_dot(
+        jnp.concatenate([picks] * hops, axis=0), back_out.reshape(hops * senders * capacity, width)
+    )
+    layer_out = (resid + token_out).astype(jnp.bfloat16).reshape(sequences, piece_len, width)
+    sum_inner = jnp.concatenate([sum_left, sum_right], axis=4)
+    in_grad = in_grad.reshape(sequences, piece_len, width)
+    rows_of = (inner_width, width)
+    grad_in_proj = jnp.concatenate(
+        [as_columns(sum_inner.reshape(rows_of)), as_columns(sum_gate.reshape(rows_of))], axis=1
+    )
+    small_halves = sum_small.reshape(2, -1, width)
+    small_wide = jnp.concatenate([small_halves[0], small_halves[1]], axis=1).astype(jnp.float32)
     offsets = [sum(heights[:at]) for at in range(len(heights) + 1)]
     pieces = [small_wide[offsets[at] : offsets[at + 1]] for at in range(len(heights))]
     summed = (
@@ -939,7 +1571,7 @@
         pieces[5][0],
         pieces[2],
         pieces[6][0],
-        sum_out.astype(jnp.float32),
+        sum_out.reshape(rows_of).astype(jnp.float32),
         pieces[7][0, width:],
         pieces[8].reshape(experts, width).T,
     )

time: 585 us -> 441 us (0.75); the launches traced: 576 us -> 439 us
  Pallas kernels: 231 us -> 316 us
  waiting for transfers between devices: 98.1 us -> 17.1 us
  matrix products: 96.5 us -> 25 us
  other arithmetic: 46 us -> 26.2 us
  local copies, waits for them, and re-layouts: 55.6 us -> 39.9 us
  between operations: 15.6 us -> 1.47 us
  blocking collectives: 11.1 us -> 0 us
  starting transfers between devices: 21.6 us -> 13.2 us
    reduce_scatter x2 -> x0, waiting for transfers between devices: 59.9 us -> none  [to_tokens(): mine = lax.psum_scatter(partial, 'seq', scatter_dimension=0, tiled=True)]
    pallas_call x1 -> x4, Pallas kernels: 122 us -> 178 us  [the longest x1 94.4 us: finish(): pl.pallas_call(functools.partial(finish_kernel, planes, side), name='fini...]
    all_gather x2 -> x0, waiting for transfers between devices: 38.1 us -> none  [to_experts(): lax.all_gather(arrived.reshape(senders * capacity, width), 'seq', axis=0,...]
    dot_general x8 -> x2, matrix products: 32.7 us -> 5.13 us  [cols_dot(): lax.dot_general(left, right, (((1,), (1,)), ((), ())), precision=precisio...]
    dot_general x6 -> x4, matrix products: 32.3 us -> 9.54 us  [half_dot(): return jnp.dot(left, right, preferred_element_type=jnp.float32)]
    pallas_call x4, Pallas kernels: 65.2 us -> 85.1 us  [scan_call(): pl.pallas_call(kernel, name=name, grid=(sequences, width // GROUP), in_sp...]
    dot_general x10 -> x4, matrix products: 25.5 us -> 6.59 us  [rows_dot(): lax.dot_general(left, right, (((0,), (0,)), ((), ())), precision=precisio...]
    ppermute x0 -> x3, waiting for transfers between devices: none -> 17.1 us  [the longest x1 17.1 us: along_planes(): return lax.ppermute(values, 'seq', pairs)]
  transfers between devices with their start and end apart: 9 -> 5, of which waited for: 3 -> 1; matrix products, arithmetic and copies ran while one was open for 15% -> 7% of each run, Pallas kernels for 19% -> 18%
where the time goes in v2:
time: 441 us; the launch traced here: 439 us
  Pallas kernels  316 us (72%)
  local copies, waits for them, and re-layouts  39.9 us (9%)
  other arithmetic  26.2 us (6%)
  matrix products  25 us (6%)
  waiting for transfers between devices  17.1 us (4%)
  starting transfers between devices  13.2 us (3%)
    pallas_call x1, Pallas kernels, finish(): pl.pallas_call(functools.partial(finish_kernel, planes, side), name='fini...  94.4 us
    pallas_call x4, Pallas kernels, scan_call(): pl.pallas_call(kernel, name=name, grid=(sequences, width // GROUP), in_sp...  85.1 us
    pallas_call x2, Pallas kernels, exchange(): pl.pallas_call(functools.partial(exchange_kernel, reverse, planes, member...  53.1 us
    pallas_call x2, Pallas kernels, dispatch(): pl.pallas_call(functools.partial(dispatch_kernel, planes, members, return...  50.4 us
    pallas_call x1, Pallas kernels, expert_apply(): pl.pallas_call(expert_kernel, name='expert_apply', grid=(up.shape[2] // u...  33.1 us
    unnamed x138, local copies, waits for them, and re-layouts  23.6 us
    ppermute x1, waiting for transfers between devices, along_planes(): return lax.ppermute(values, 'seq', pairs)  17.1 us
    dot_general x4, matrix products, half_dot(): return jnp.dot(left, right, preferred_element_type=jnp.float32)  9.54 us
  transfers between devices with their start and end apart: 5, of which 1 were waited for; matrix products, arithmetic and copies ran while one was open for 7% of the time, Pallas kernels for 18%

profile of v2, /device:TPU:11, one launch (start us, length us, event | category | flops | bytes accessed | tf_op | source)
XLA Modules:
  0.0 439.0 jit_solution(4929545465982839941)
XLA Ops:
  0.7 1.3 multiply_reduce_fusion.4
  2.0 1.2 fusion.14.normed_ref
  3.2 3.9 fusion.40
  7.3 1.5 copy-done.32
  8.8 1.1 copy-done.23
  9.9 3.7 collective-permute-start
  13.7 1.1 convolution_convert_fusion.2
  14.8 4.0 all-to-all-start
  18.9 1.3 collective-permute-start.3
  21.7 3.4 slice.137.in_proj_ref
  26.8 2.1 divide_multiply_fusion
  29.0 1.0 fusion.41
  29.9 1.2 copy-done.2
  31.2 2.8 compare_select_fusion
  34.0 1.1 copy-done.28
  35.1 0.9 bitcast_reduce_fusion.sum_ref
  36.2 0.8 copy.45
  37.0 0.8 copy.43
  37.7 1.9 broadcast_in_dim.23.in_ref.refs_3_
  39.7 1.4 copy-done.7
  41.1 6.7 %first_pass.1.end_ref = f32[2,16,1536]{2,1,0:T(8,128)S(1)} custom-call(f32[256,1536]{1,0:T(8,128)S(1)} %copy-done.7, f32[256,1536]{1,0:T(8,128)S(1)} %bitcast.64, f32[256,16,128]{2,1,0:T(8,128)} %broadcast_in_dim.23.in_ref.refs_3_, f32[16,1536]{1,0:T(8,128)S(1)} %copy-done.20), custom_call_target="tpu_custom_call" | custom-call | flops 125829120 | bytes 6291456 | tf_op jit(solution)/shard_map/first_pass/pallas_call | solution.py:333
  47.8 32.4 %state_exchange.1.start_ref.refs_7_ = f32[2,16,1536]{2,1,0:T(8,128)S(1)} custom-call(f32[2,16,1536]{2,1,0:T(8,128)S(1)} %first_pass.1.end_ref, f32[2,1536]{1,0:T(2,128)S(1)} %bitcast_reduce_fusion.sum_ref, f32[4,1536]{1,0:T(4,128)S(1)} %constant_dynamic-slice_fusion.rates_ref), custom_call_target="tpu_custom_call" | custom-call | flops 1000000 | bytes 20000000 | tf_op jit(solution)/shard_map/state_exchange/pallas_call | solution.py:491
  80.4 15.4 %second_pass.1 = f32[256,1536]{1,0:T(8,128)S(1)} custom-call(f32[256,1536]{1,0:T(8,128)S(1)} %copy-done.8, f32[256,1536]{1,0:T(8,128)} %bitcast.61, f32[256,16,128]{2,1,0:T(8,128)} %broadcast_in_dim.23.in_ref.refs_3_, f32[16,1536]{1,0:T(8,128)S(1)} %copy-done.20, f32[2,16,1536]{2,1,0:T(8,128)S(1)} %state_exchange.1.start_ref.refs_7_, ...), custom_call_target="tpu_custom_call" | custom-call | flops 125829120 | bytes 6291456 | tf_op jit(solution)/shard_map/second_pass/pallas_call | solution.py:333
  97.0 0.9 copy-done.34
  97.9 2.2 multiply_reduce_fusion.3
  100.9 1.5 copy.46.delta_low_ref
  103.1 2.3 convolution_convert_fusion.3
  105.4 24.8 %send_rows.1 = bf16[2,8,40,768]{3,2,1,0:T(8,128)(2,1)} custom-call(bf16[8,40,768]{2,1,0:T(8,128)(2,1)} %bitcast.82), custom_call_target="tpu_custom_call" | custom-call | flops 1000000 | bytes 50000000 | tf_op jit(solution)/shard_map/send_rows/pallas_call | solution.py:1158
  130.2 4.1 collective-permute-start.1
  134.3 2.9 pad_maximum_fusion.1.extended_ref
  137.3 17.1 %collective-permute-done.1 = bf16[8,40,768]{2,1,0:T(8,128)(2,1)S(1)} collective-permute-done((bf16[8,40,768]{2,1,0:T(8,128)(2,1)S(1)}, bf16[8,40,768]{2,1,0:T(8,128)(2,1)S(1)}, u32[]{:S(2)}, u32[]{:S(2)}) %collective-permute-start.1) | collective-permute-done | bytes 491552 | tf_op jit(solution)/shard_map/ppermute | solution.py:1417
  154.5 33.1 %expert_apply.1 = (bf16[640,768]{1,0:T(8,128)(2,1)S(1)}, bf16[640,768]{1,0:T(8,128)(2,1)S(1)}, f32[1,768,768]{2,1,0:T(8,128)}, f32[1,768,768]{2,1,0:T(8,128)}, b...) custom-call(bf16[640,768]{1,0:T(8,128)(2,1)S(1)} %bitcast.66, ...), custom_call_target="tpu_custom_call" | custom-call | flops 9059696640 | bytes 30000000 | tf_op jit(solution)/shard_map/expert_apply/pallas_call | solution.py:1284
  187.6 0.9 copy-done.12
  188.5 1.0 copy-done.14
  190.1 25.6 %return_rows.1 = bf16[2,8,40,768]{3,2,1,0:T(8,128)(2,1)} custom-call(bf16[2,8,40,768]{3,2,1,0:T(8,128)(2,1)} %bitcast.68), custom_call_target="tpu_custom_call" | custom-call | flops 1000000 | bytes 50000000 | tf_op jit(solution)/shard_map/return_rows/pallas_call | solution.py:1158
  215.8 2.3 multiply_reduce_fusion.1
  218.4 1.1 copy-done.5
  219.5 3.4 multiply_reduce_fusion
  222.9 2.2 convolution_convert_fusion.1
  225.2 0.8 convolution_convert_fusion
  226.0 1.7 fusion.normed_gate_ref
  227.9 1.9 broadcast_in_dim.27.out_ref.refs_4_
  229.8 6.5 %back_summary.1.end_ref = f32[2,16,1536]{2,1,0:T(8,128)S(1)} custom-call(f32[256,1536]{1,0:T(8,128)S(1)} %copy-done.9, f32[256,1536]{1,0:T(8,128)S(1)} %get-tuple-element.74.grad_ref.refs_2_.grad_scan_ref, f32[256,16,128]{2,1,0:T(8,128)} %broadcast_in_dim.27.out_ref.refs_4_, f32[16,1536]{1,0:T(8,128)S(1)} %copy-done.20), custom_call_target="tpu_custom_call" | custom-call | flops 125829120 | bytes 6291456 | tf_op jit(solution)/shard_map/back_summary/pallas_call | solution.py:333
  236.4 20.8 %state_exchange_back.1.refs_8_ = f32[2,16,1536]{2,1,0:T(8,128)S(1)} custom-call(f32[2,16,1536]{2,1,0:T(8,128)S(1)} %back_summary.1.end_ref, f32[2,1536]{1,0:T(2,128)S(1)} %bitcast_reduce_fusion.sum_ref, f32[4,1536]{1,0:T(4,128)S(1)} %constant_dynamic-slice_fusion.rates_ref), custom_call_target="tpu_custom_call" | custom-call | flops 1000000 | bytes 20000000 | tf_op jit(solution)/shard_map/state_exchange_back/pallas_call | solution.py:491
  258.3 1.6 pad_maximum_fusion
  259.9 56.4 %backward_scan.1 = (f32[256,1536]{1,0:T(8,128)}, f32[256,1536]{1,0:T(8,128)}, f32[256,256]{1,0:T(8,128)S(1)}, f32[256,256]{1,0:T(8,128)S(1)}, f32[2,16,1536]{2,1...) custom-call(f32[256,1536]{1,0:T(8,128)} %get-tuple-element.93.delta_, ...), custom_call_target="tpu_custom_call" | custom-call | flops 125829120 | bytes 6291456 | tf_op jit(solution)/shard_map/backward_scan/pallas_call | solution.py:333
  316.3 0.7 copy-done.15
  317.0 0.7 copy-done.16
  317.8 0.7 copy-done.17
  318.5 0.7 copy-done.18
  319.8 94.4 %finish_gradients.1 = (f32[256,768]{1,0:T(8,128)}, bf16[2,2,2,4,48,768]{5,4,3,2,1,0:T(8,128)(2,1)}, bf16[2,2,2,4,48,768]{5,4,3,2,1,0:T(8,128)(2,1)}, bf16[2,2,2,...) custom-call(f32[256,1536]{1,0:T(8,128)} %get-tuple-element.41.grad_d, ...), custom_call_target="tpu_custom_call" | custom-call | flops 100000000 | bytes 200000000 | tf_op jit(solution)/shard_map/finish_gradients/pallas_call | solution.py:1052
  414.2 1.2 fusion.38
  416.4 0.8 slice_bitcast_fusion
  417.2 0.7 slice.173
  420.4 1.3 constant_dynamic-update-slice_fusion.1
  422.1 1.5 copy-done.37
  423.7 1.5 copy-done.36
  425.2 2.9 bitcast_convert_fusion
  428.1 1.3 fusion.12
  429.6 1.7 convert_add_fusion
  431.3 0.8 copy-done.38
  432.1 1.7 convert_add_fusion.1
  433.8 4.3 maximum_convert_fusion
  438.1 0.9 copy.52
  (166 shorter events, 13.5 us)
Async XLA Ops:
  0.6 97.3 %copy-start = (bf16[1536,768]{1,0:T(8,128)(2,1)S(1)}, bf16[1536,768]{1,0:T(8,128)(2,1)}, u32[]{:S(2)}) copy-start(bf16[1536,768]{1,0:T(8,128)(2,1)} %param.28) | copy-start | bytes 7077892
  3.2 4.0 copy-start.30
  7.1 1.7 copy-start.32
  7.1 6.5 %copy-start.62 = (s32[2,128]{1,0:T(2,128)S(1)}, s32[2,128]{1,0:T(2,128)}, u32[]{:S(2)}) copy-start(s32[2,128]{1,0:T(2,128)} %param.34) | copy-start | bytes 3076
  7.1 6.5 %copy-start.63 = (s32[2,128]{1,0:T(2,128)S(1)}, s32[2,128]{1,0:T(2,128)}, u32[]{:S(2)}) copy-start(s32[2,128]{1,0:T(2,128)} %param.33) | copy-start | bytes 3076
  7.2 6.5 %copy-start.40 = (bf16[2,128,768]{2,1,0:T(8,128)(2,1)S(1)}, bf16[2,128,768]{2,1,0:T(8,128)(2,1)}, u32[]{:S(2)}) copy-start(bf16[2,128,768]{2,1,0:T(8,128)(2,1)} %param.35) | copy-start | bytes 1179652
  8.8 1.1 copy-start.23
  8.8 12.7 %copy-start.53 = (f32[4,1536]{1,0:T(4,128)S(1)}, f32[4,1536]{1,0:T(4,128)}, u32[]{:S(2)}) copy-start(f32[4,1536]{1,0:T(4,128)} %conv_weight_ref.1) | copy-start | bytes 73732
  8.8 12.8 %copy-start.20 = (f32[16,1536]{1,0:T(8,128)S(1)}, f32[16,1536]{1,0:T(8,128)}, u32[]{:S(2)}) copy-start(f32[16,1536]{1,0:T(8,128)} %refs_6_.1) | copy-start | bytes 294916
  9.9 16.9 %collective-permute-start = (f32[2,3,1536]{2,1,0:T(4,128)S(1)}, f32[2,3,1536]{2,1,0:T(4,128)S(1)}, u32[]{:S(2)}, u32[]{:S(2)}) collective-permute-start(f32[2,3,1536]{2,1,0:T(4,128)S(1)} %slice.159), channel_id=1, source_target_pairs={{0,1},{1,2},{2,3},{3,4},{4,5},{5,6},{6,7},{7,8},{8,9},{9,10},{10,1... | collective-permute-start | bytes 110600 | tf_op jit(solution)/shard_map/ppermute | solution.py:25
  13.7 7.9 %copy-start.57 = (s32[256]{0:T(256)}, s32[256]{0:T(256)S(1)}, u32[]{:S(2)}) copy-start(s32[256]{0:T(256)S(1)} %fusion.29) | copy-start | bytes 3076
  14.8 115.5 %all-to-all-start = ((bf16[8,40,768]{2,1,0:T(8,128)(2,1)}), bf16[8,40,768]{2,1,0:T(8,128)(2,1)S(1)}, u32[]{:S(2)}, u32[]{:S(2)}) async-start(bf16[8,40,768]{2,1,0:T(8,128)(2,1)} %bitcast.11), calls=%async_computation | async-start | bytes 983040 | tf_op jit(solution)/shard_map/all_to_all | solution.py:1424
  18.8 135.7 %collective-permute-start.2 = (bf16[1,768,768]{2,1,0:T(8,128)(2,1)}, bf16[1,768,768]{2,1,0:T(8,128)(2,1)}, u32[]{:S(2)}, u32[]{:S(2)}) collective-permute-start(bf16[1,768,768]{2,1,0:T(8,128)(2,1)} %up_ref.1), channel_id=1, source_target_pairs={{0,8},{8,0},{16,24},{24,16},{1,9},{9,1},{17,25},{25,17},{2,10},{10... | collective-permute-start | bytes 3538952 | tf_op jit(solution)/shard_map/ppermute | solution.py:1421
  18.9 135.5 %collective-permute-start.3 = (bf16[1,768,768]{2,1,0:T(8,128)(2,1)}, bf16[1,768,768]{2,1,0:T(8,128)(2,1)}, u32[]{:S(2)}, u32[]{:S(2)}) collective-permute-start(bf16[1,768,768]{2,1,0:T(8,128)(2,1)} %down_ref.1), channel_id=1, source_target_pairs={{0,8},{8,0},{16,24},{24,16},{1,9},{9,1},{17,25},{25,17},{2,10},{10... | collective-permute-start | bytes 3538952 | tf_op jit(solution)/shard_map/ppermute | solution.py:1421
  21.6 3.4 copy-start.56
  21.6 4.0 copy-start.54
  21.7 5.1 %copy-start.24 = (f32[256,1536]{1,0:T(8,128)S(1)}, f32[256,1536]{1,0:T(8,128)}, u32[]{:S(2)}) copy-start(f32[256,1536]{1,0:T(8,128)} %copy-done.23) | copy-start | bytes 4718596
  21.7 5.1 %copy-start.58 = (f32[1536]{0:T(1024)S(1)}, f32[1536]{0:T(1024)}, u32[]{:S(2)}) copy-start(f32[1536]{0:T(1024)} %param.22) | copy-start | bytes 18436
  26.8 2.2 copy-start.50
  26.8 2.2 copy-start.44
  29.0 2.2 copy-start.52
  29.0 2.3 copy-start.64
  29.9 1.2 copy-start.2
  34.0 1.2 copy-start.28
  37.7 1.9 copy-start.3
  39.7 1.4 copy-start.7
  41.1 39.1 %copy-start.47 = (bf16[256,256]{1,0:T(8,128)(2,1)S(1)}, bf16[256,256]{1,0:T(8,128)(2,1)}, u32[]{:S(2)}) copy-start(bf16[256,256]{1,0:T(8,128)(2,1)} %copy.45) | copy-start | bytes 393220
  41.1 39.1 %copy-start.48 = (bf16[256,256]{1,0:T(8,128)(2,1)S(1)}, bf16[256,256]{1,0:T(8,128)(2,1)}, u32[]{:S(2)}) copy-start(bf16[256,256]{1,0:T(8,128)(2,1)} %copy.43) | copy-start | bytes 393220
  41.1 39.1 %copy-start.59 = (s32[256]{0:T(256)S(1)}, s32[256]{0:T(256)}, u32[]{:S(2)}) copy-start(s32[256]{0:T(256)} %get-tuple-element.98) | copy-start | bytes 3076
  41.1 39.2 %copy-start.60 = (s32[256]{0:T(256)S(1)}, s32[256]{0:T(256)}, u32[]{:S(2)}) copy-start(s32[256]{0:T(256)} %get-tuple-element.99) | copy-start | bytes 3076
  41.1 39.3 %copy-start.8 = (f32[256,1536]{1,0:T(8,128)S(1)}, f32[256,1536]{1,0:T(8,128)}, u32[]{:S(2)}) copy-start(f32[256,1536]{1,0:T(8,128)} %get-tuple-element.93.delta_ref.refs_0_) | copy-start | bytes 4718596
  80.4 15.5 %copy-start.4 = (f32[2,128,1536]{2,1,0:T(8,128)S(1)}, f32[2,128,1536]{2,1,0:T(8,128)}, u32[]{:S(2)}) copy-start(f32[2,128,1536]{2,1,0:T(8,128)} %copy-done.2) | copy-start | bytes 4718596
  80.4 15.5 %copy-start.33 = (f32[256,3072]{1,0:T(8,128)S(1)}, f32[256,3072]{1,0:T(8,128)}, u32[]{:S(2)}) copy-start(f32[256,3072]{1,0:T(8,128)} %copy-done.32) | copy-start | bytes 9437188
  95.9 1.1 copy-start.10
  95.9 2.0 copy-start.29
  100.3 34.1 %copy-start.61 = (f32[136]{0:T(256)S(1)}, f32[136]{0:T(256)}, u32[]{:S(2)}) copy-start(f32[136]{0:T(256)} %pad.6.clone) | copy-start | bytes 1636
  100.9 33.4 %copy-start.51 = (f32[2,3,1536]{2,1,0:T(4,128)S(1)}, f32[2,3,1536]{2,1,0:T(4,128)}, u32[]{:S(2)}) copy-start(f32[2,3,1536]{2,1,0:T(4,128)} %copy-done.50) | copy-start | bytes 110596
  130.2 24.1 %collective-permute-start.1 = (bf16[8,40,768]{2,1,0:T(8,128)(2,1)S(1)}, bf16[8,40,768]{2,1,0:T(8,128)(2,1)S(1)}, u32[]{:S(2)}, u32[]{:S(2)}) collective-permute-start(bf16[8,40,768]{2,1,0:T(8,128)(2,1)S(1)} %all-to-all-done), channel_id=1, source_target_pairs={{0,16},{8,24},{16,0},{24,8},{1,17},{9,25},{17,1},{25,9},{2,18},{10... | collective-permute-start | bytes 1474568 | tf_op jit(solution)/shard_map/ppermute | solution.py:1417
  137.3 17.2 %copy-start.13 = (bf16[2,8,40,768]{3,2,1,0:T(8,128)(2,1)S(1)}, bf16[2,8,40,768]{3,2,1,0:T(8,128)(2,1)}, u32[]{:S(2)}) copy-start(bf16[2,8,40,768]{3,2,1,0:T(8,128)(2,1)} %send_rows.1) | copy-start | bytes 2949124
  137.3 17.2 %copy-start.22 = (f32[768,8]{0,1:T(8,128)S(1)}, f32[768,8]{0,1:T(8,128)}, u32[]{:S(2)}) copy-start(f32[768,8]{0,1:T(8,128)} %param.30) | copy-start | bytes 73732
  188.5 1.0 copy-start.14
  190.1 25.7 %copy-start.49 = (pred[320,256]{1,0:T(32,128)(4,1)S(1)}, pred[320,256]{1,0:T(32,128)(4,1)}, u32[]{:S(2)}) copy-start(pred[320,256]{1,0:T(32,128)(4,1)} %iota_compare_fusion) | copy-start | bytes 245764
  190.1 25.7 %copy-start.55 = (f32[768]{0:T(1024)S(1)}, f32[768]{0:T(1024)}, u32[]{:S(2)}) copy-start(f32[768]{0:T(1024)} %param.29) | copy-start | bytes 9220
  215.7 2.3 copy-start.26
  215.8 2.3 copy-start.41
  215.8 2.6 copy-start.11
  218.1 1.4 copy-start.5
  218.1 7.9 %slice-start = ((s8[4718592]{0:T(1024)(128)(4,1)}), s8[4194304]{0:T(1024)(128)(4,1)S(1)}, s32[]{:S(2)}) async-start(s8[4718592]{0:T(1024)(128)(4,1)} %bitcast.85), calls=%async_computation.1 | async-start | bytes 8388608
  219.5 3.4 copy-start.25
  219.5 3.4 copy-start.35
  219.5 6.5 %slice-start.1 = ((s8[4718592]{0:T(1024)(128)(4,1)}), s8[524288]{0:T(1024)(128)(4,1)S(1)}, s32[]{:S(2)}) async-start(s8[4718592]{0:T(1024)(128)(4,1)} %bitcast.85), calls=%async_computation.2 | async-start | bytes 1048576
  222.9 6.9 %copy-start.6 = (f32[256,1536]{1,0:T(8,128)}, f32[256,1536]{1,0:T(8,128)S(1)}, u32[]{:S(2)}) copy-start(f32[256,1536]{1,0:T(8,128)S(1)} %get-tuple-element.74.grad_ref.refs_2_.grad_scan_ref) | copy-start | bytes 4718596
  222.9 2.3 copy-start.31
  227.9 2.0 copy-start.9
  419.8 2.0 copy-start.42
  421.9 1.7 copy-start.37
  423.5 1.7 copy-start.36
  425.2 2.9 copy-start.27
  425.2 2.9 copy-start.45
  425.2 4.2 copy-start.39
  428.1 1.5 copy-start.43
  429.6 2.5 copy-start.38
  433.8 4.3 copy-start.46
  433.8 5.2 %copy-start.1 = (bf16[1536,768]{1,0:T(8,128)(2,1)S(1)}, bf16[1536,768]{1,0:T(8,128)(2,1)}, u32[]{:S(2)}) copy-start(bf16[1536,768]{1,0:T(8,128)(2,1)} %param.28) | copy-start | bytes 7077892
  (8 other events, 6.0 us)

commit v3 on v2

v3 whole, which is shorter than its diff:
```python
import functools
import math

import jax
import jax.numpy as jnp
from jax import lax
from jax.experimental import pallas as pl
from jax.experimental.pallas import tpu as pltpu
from jax.sharding import PartitionSpec as P

BLK = 16
LANES = 128
GROUP = 512
LOG2E = 1.4426950408889634
LN2 = 0.6931471805599453
VMEM_BYTES = 50 * 1024 * 1024


EPSILON = 1e-05


def half_dot(left, right):
    return jnp.dot(left, right, preferred_element_type=jnp.float32)


def rows_dot(left, right, precision=None):
    return lax.dot_general(
        left,
        right,
        (((0,), (0,)), ((), ())),
        precision=precision,
        preferred_element_type=jnp.float32,
    )


def cols_dot(left, right, precision=None):
    return lax.dot_general(
        left,
        right,
        (((1,), (1,)), ((), ())),
        precision=precision,
        preferred_element_type=jnp.float32,
    )


def norm_backward(values, scaling, gain_vec, incoming):
    normal = values * scaling
    weighted = incoming * gain_vec
    grad_gain = jnp.sum(incoming * normal, axis=0, keepdims=True)
    grad_values = scaling * (
        weighted - normal * jnp.mean(weighted * normal, axis=-1, keepdims=True)
    )
    return (grad_values, grad_gain)


def silu_slope(values):
    sigma = jax.nn.sigmoid(values)
    return sigma * (1.0 + values * (1.0 - sigma))


def lane_parts(ref, k, states):
    width = ref.shape[-1]
    return [
        jnp.broadcast_to(ref[k : k + 1, at : at + LANES], (states, LANES))
        for at in range(0, width, LANES)
    ]


def block_of(ref, i):
    return ref.at[pl.ds(pl.multiple_of(i * BLK, BLK), BLK), :]


def rates_of(log_ref):
    rates = -jnp.exp(log_ref[...]) * LOG2E
    return [rates[:, at : at + LANES] for at in range(0, rates.shape[1], LANES)]


def first_pass_kernel(delta_ref, conv_ref, in_ref, log_ref, end_ref, drive):
    steps, width = delta_ref.shape
    states = log_ref.shape[0]
    rates = rates_of(log_ref)
    drive[...] = delta_ref[...] * conv_ref[...]

    def block(i, state):
        state = list(state)
        inwards = in_ref[i]
        for k in range(BLK):
            inward = jnp.broadcast_to(inwards[:, k : k + 1], (states, LANES))
            deltas = lane_parts(block_of(delta_ref, i), k, states)
            drives = lane_parts(block_of(drive, i), k, states)
            for j in range(width // LANES):
                state[j] = jnp.exp2(deltas[j] * rates[j]) * state[j] + inward * drives[j]
        return tuple(state)

    zero = tuple(jnp.zeros((states, LANES), jnp.float32) for _ in range(width // LANES))
    last = lax.fori_loop(0, steps // BLK, block, zero)
    for j in range(width // LANES):
        end_ref[0, :, j * LANES : (j + 1) * LANES] = last[j]


def second_pass_kernel(
    delta_ref, conv_ref, in_ref, log_ref, start_ref, out_ref, rest_ref, scanned_ref, drive, stack
):
    steps, width = delta_ref.shape
    states = log_ref.shape[0]
    rates = rates_of(log_ref)
    drive[...] = delta_ref[...] * conv_ref[...]

    def block(i, state):
        state = list(state)
        inwards = in_ref[i]
        for k in range(BLK):
            inward = jnp.broadcast_to(inwards[:, k : k + 1], (states, LANES))
            deltas = lane_parts(block_of(delta_ref, i), k, states)
            drives = lane_parts(block_of(drive, i), k, states)
            for j in range(width // LANES):
                state[j] = jnp.exp2(deltas[j] * rates[j]) * state[j] + inward * drives[j]
                stack[k * states : (k + 1) * states, j * LANES : (j + 1) * LANES] = state[j].astype(
                    jnp.bfloat16
                )
        rows = pl.ds(pl.multiple_of(i * BLK, BLK), BLK)
        both = jnp.concatenate([out_ref[rows, :], rest_ref[rows, :]], axis=0)
        product = jnp.dot(both, stack[...], preferred_element_type=jnp.float32)
        scanned_ref[rows, :] = product[:BLK] + product[BLK:]
        return tuple(state)

    begin = tuple(start_ref[0, :, j * LANES : (j + 1) * LANES] for j in range(width // LANES))
    lax.fori_loop(0, steps // BLK, block, begin)


def back_summary_kernel(delta_ref, grad_ref, out_ref, log_ref, end_ref):
    steps, width = delta_ref.shape
    states = log_ref.shape[0]
    rates = rates_of(log_ref)
    blocks = steps // BLK

    def block(i, state):
        state = list(state)
        outwards = out_ref[blocks - 1 - i]
        for k in reversed(range(BLK)):
            outward = jnp.broadcast_to(outwards[:, k : k + 1], (states, LANES))
            deltas = lane_parts(block_of(delta_ref, blocks - 1 - i), k, states)
            grads = lane_parts(block_of(grad_ref, blocks - 1 - i), k, states)
            for j in range(width // LANES):
                state[j] = jnp.exp2(deltas[j] * rates[j]) * (state[j] + outward * grads[j])
        return tuple(state)

    zero = tuple(jnp.zeros((states, LANES), jnp.float32) for _ in range(width // LANES))
    last = lax.fori_loop(0, blocks, block, zero)
    for j in range(width // LANES):
        end_ref[0, :, j * LANES : (j + 1) * LANES] = last[j]


def backward_body(
    middle,
    first,
    delta_ref,
    conv_ref,
    grad_ref,
    in_ref,
    out_ref,
    in_diag_ref,
    log_ref,
    start_ref,
    finish_ref,
    grad_delta_ref,
    grad_conv_ref,
    grad_in_ref,
    grad_out_ref,
    grad_log_ref,
    drive,
    carried,
    stack,
    slope,
):
    steps, width = delta_ref.shape
    states = log_ref.shape[0]
    parts = width // LANES
    rates = rates_of(log_ref)
    blocks = steps // BLK
    drive[...] = delta_ref[...] * conv_ref[...]

    def forward(i, state):
        state = list(state)
        inwards = in_ref[i]
        for k in range(BLK):
            t = i * BLK + k
            inward = jnp.broadcast_to(inwards[:, k : k + 1], (states, LANES))
            deltas = lane_parts(block_of(delta_ref, i), k, states)
            drives = lane_parts(block_of(drive, i), k, states)
            for j in range(parts):
                at = slice(j * LANES, (j + 1) * LANES)
                decay = jnp.exp2(deltas[j] * rates[j])
                kept = decay * state[j]
                carried[t, :, at] = kept
                state[j] = kept + inward * drives[j]
                stack[k * states : (k + 1) * states, at] = state[j].astype(jnp.bfloat16)
        rows = pl.ds(pl.multiple_of(i * BLK, BLK), BLK)
        partial = cols_dot(grad_ref[rows, :].astype(jnp.bfloat16), stack[...])

        @pl.when(first)
        def _():
            grad_out_ref[rows, :] = partial

        @pl.when(jnp.logical_not(first))
        def _():
            grad_out_ref[rows, :] += partial

        return tuple(state)

    begin = tuple(start_ref[0, :, j * LANES : (j + 1) * LANES] for j in range(parts))
    lax.fori_loop(0, blocks, forward, begin)
    middle()
    column = lax.broadcasted_iota(jnp.int32, (BLK, BLK * states), 1) // states
    row = lax.broadcasted_iota(jnp.int32, (BLK, BLK * states), 0)
    ones = jnp.where(column == row, 1.0, 0.0).astype(jnp.bfloat16)

    def backward(i, state):
        adjoint, gathered = list(state[:parts]), list(state[parts:])
        outwards = out_ref[blocks - 1 - i]
        for k in reversed(range(BLK)):
            t = (blocks - 1 - i) * BLK + k
            outward = jnp.broadcast_to(outwards[:, k : k + 1], (states, LANES))
            deltas = lane_parts(block_of(delta_ref, blocks - 1 - i), k, states)
            grads = lane_parts(block_of(grad_ref, blocks - 1 - i), k, states)
            for j in range(parts):
                at = slice(j * LANES, (j + 1) * LANES)
                whole = adjoint[j] + outward * grads[j]
                exponent = whole * carried[t, :, at]
                gathered[j] = gathered[j] + exponent * deltas[j]
                slope[k * states : (k + 1) * states, at] = (exponent * rates[j]).astype(
                    jnp.bfloat16
                )
                stack[k * states : (k + 1) * states, at] = whole.astype(jnp.bfloat16)
                adjoint[j] = jnp.exp2(deltas[j] * rates[j]) * whole
        rows = pl.ds(pl.multiple_of((blocks - 1 - i) * BLK, BLK), BLK)
        driven = jnp.dot(in_diag_ref[rows, :], stack[...], preferred_element_type=jnp.float32)
        summed = jnp.dot(ones, slope[...], preferred_element_type=jnp.float32) * LN2
        grad_delta_ref[rows, :] = summed + driven * conv_ref[rows, :]
        grad_conv_ref[rows, :] = driven * delta_ref[rows, :]
        partial = cols_dot(drive[rows, :].astype(jnp.bfloat16), stack[...])

        @pl.when(first)
        def _():
            grad_in_ref[rows, :] = partial

        @pl.when(jnp.logical_not(first))
        def _():
            grad_in_ref[rows, :] += partial

        return tuple(adjoint + gathered)

    ends = tuple(finish_ref[0, :, j * LANES : (j + 1) * LANES] for j in range(parts))
    zero = tuple(jnp.zeros((states, LANES), jnp.float32) for _ in range(parts))
    last = lax.fori_loop(0, blocks, backward, ends + zero)
    for j in range(parts):
        grad_log_ref[0, :, j * LANES : (j + 1) * LANES] = last[parts + j] * rates[j] * LN2


def scan_call(kernel, name, sequences, states, operands, results, scratch):
    tokens, width = next(value.shape for kind, value in operands if kind == "wide")
    steps = tokens // sequences
    specs = {
        "wide": pl.BlockSpec((steps, GROUP), lambda q, j: (q, j)),
        "cols": pl.BlockSpec((steps // BLK, states, BLK), lambda q, j: (q, 0, 0)),
        "narrow": pl.BlockSpec((steps, BLK * states), lambda q, j: (q, 0)),
        "rates": pl.BlockSpec((states, GROUP), lambda q, j: (0, j)),
        "state": pl.BlockSpec((1, states, GROUP), lambda q, j: (q, 0, j)),
    }
    shapes = {
        "wide": (tokens, width),
        "narrow": (tokens, BLK * states),
        "state": (sequences, states, width),
    }
    in_specs = [specs[kind] for kind, _ in operands]
    out_specs = [specs[kind] for kind in results]
    out_shape = [jax.ShapeDtypeStruct(shapes[kind], jnp.float32) for kind in results]
    return pl.pallas_call(
        kernel,
        name=name,
        grid=(sequences, width // GROUP),
        in_specs=in_specs,
        out_specs=out_specs,
        out_shape=out_shape,
        scratch_shapes=scratch,
        compiler_params=pltpu.CompilerParams(
            dimension_semantics=("arbitrary", "arbitrary"),
            vmem_limit_bytes=VMEM_BYTES,
        ),
        cost_estimate=pl.CostEstimate(
            flops=20 * tokens * states * width,
            transcendentals=tokens * states * width,
            bytes_accessed=16 * tokens * width,
        ),
    )(*(value for _, value in operands))


MESH = pl.DeviceIdType.MESH


def remote(src, dst, send, arrive, axis, peer):
    return pltpu.make_async_remote_copy(
        src_ref=src,
        dst_ref=dst,
        send_sem=send,
        recv_sem=arrive,
        device_id={axis: peer},
        device_id_type=MESH,
    )


def greet(axes):
    barrier = pltpu.get_barrier_semaphore()
    total = 0
    for axis, size in axes:
        mine = lax.axis_index(axis)
        for k in range(1, size):
            pl.semaphore_signal(
                barrier, inc=1, device_id={axis: lax.rem(mine + k, size)}, device_id_type=MESH
            )
        total += size - 1
    pl.semaphore_wait(barrier, total)


def exchange_body(
    reverse,
    planes,
    members,
    end_ref,
    sum_ref,
    rates_ref,
    carry_ref,
    packed,
    landed,
    summary,
    totals,
    starts,
    carries,
    send_one,
    recv_one,
    send_two,
    recv_two,
    send_three,
    recv_three,
):
    sequences, states, width = end_ref.shape
    rows = sequences * states // members
    plane, member = lax.axis_index("seq"), lax.axis_index("exp")
    rates = -jnp.exp(rates_ref[...])
    for i in range(members):
        q, n = (i * rows) // states, (i * rows) % states
        packed[i, :rows] = end_ref[q, n : n + rows]
        packed[i, rows:] = sum_ref[q : q + 1]
    for k in range(1, members):
        other = lax.rem(member + k, members)
        remote(
            packed.at[other],
            landed.at[member],
            send_one.at[k],
            recv_one.at[member],
            "exp",
            other,
        ).start()
    landed[member] = packed[member]
    for k in range(1, members):
        other = lax.rem(member + k, members)
        remote(
            packed.at[other], landed.at[other], send_one.at[k], recv_one.at[other], "exp", other
        ).wait()
    order = range(members)[::-1] if reverse else range(members)
    plane_order = range(planes)[::-1] if reverse else range(planes)

    def through(piece, before):
        return jnp.exp(piece[rows:] * rates) * before + piece[:rows]

    state = jnp.zeros((rows, width), jnp.float32)
    total = jnp.zeros((1, width), jnp.float32)
    for i in order:
        piece = landed[i]
        state = through(piece, state)
        total = total + piece[rows:]
    summary[:rows] = state
    summary[rows:] = total
    for k in range(1, planes):
        other = lax.rem(plane + k, planes)
        remote(
            summary, totals.at[plane], send_two.at[k], recv_two.at[plane], "seq", other
        ).start()
    totals[plane] = summary[...]
    for k in range(1, planes):
        other = lax.rem(plane + k, planes)
        remote(summary, totals.at[other], send_two.at[k], recv_two.at[other], "seq", other).wait()
    state = jnp.zeros((rows, width), jnp.float32)
    for s in plane_order:
        reached = plane < s if reverse else plane > s
        state = jnp.where(reached, through(totals[s], state), state)
    for i in order:
        starts[i] = state
        state = through(landed[i], state)
    for k in range(1, members):
        other = lax.rem(member + k, members)
        remote(
            starts.at[other],
            carries.at[member],
            send_three.at[k],
            recv_three.at[member],
            "exp",
            other,
        ).start()
    carries[member] = starts[member]
    for k in range(1, members):
        other = lax.rem(member + k, members)
        remote(
            starts.at[other],
            carries.at[other],
            send_three.at[k],
            recv_three.at[other],
            "exp",
            other,
        ).wait()
    for i in range(members):
        q, n = (i * rows) // states, (i * rows) % states
        carry_ref[q, n : n + rows] = carries[i]


def exchange_kernel(reverse, planes, members, *refs):
    greet((("seq", planes), ("exp", members)))
    exchange_body(reverse, planes, members, *refs)


def exchange_scratch(planes, members, rows, width):
    piece = (rows + 1, width)
    return [
        pltpu.VMEM((members,) + piece, jnp.float32),
        pltpu.VMEM((members,) + piece, jnp.float32),
        pltpu.VMEM(piece, jnp.float32),
        pltpu.VMEM((planes,) + piece, jnp.float32),
        pltpu.VMEM((members, rows, width), jnp.float32),
        pltpu.VMEM((members, rows, width), jnp.float32),
        pltpu.SemaphoreType.DMA((members,)),
        pltpu.SemaphoreType.DMA((members,)),
        pltpu.SemaphoreType.DMA((planes,)),
        pltpu.SemaphoreType.DMA((planes,)),
        pltpu.SemaphoreType.DMA((members,)),
        pltpu.SemaphoreType.DMA((members,)),
    ]


def exchange(local_end, delta_sum, own_log):
    planes, members = lax.axis_size("seq"), lax.axis_size("exp")
    rows, width = own_log.shape
    vmem = pl.BlockSpec(memory_space=pltpu.VMEM)
    return pl.pallas_call(
        functools.partial(exchange_kernel, True, planes, members),
        name="state_exchange_back",
        in_specs=[vmem] * 3,
        out_specs=vmem,
        out_shape=jax.ShapeDtypeStruct(local_end.shape, jnp.float32),
        scratch_shapes=exchange_scratch(planes, members, rows, width),
        compiler_params=pltpu.CompilerParams(
            collective_id=2, has_side_effects=True, vmem_limit_bytes=VMEM_BYTES
        ),
        cost_estimate=pl.CostEstimate(flops=10**6, transcendentals=10**5, bytes_accessed=2 * 10**7),
    )(local_end, delta_sum, own_log)


class Sums:
    def __init__(self, planes, side, sends, arrivals):
        self.planes, self.side = planes, side
        self.plane, self.member = lax.axis_index("seq"), lax.axis_index("exp")
        chip, self.core = self.member // 2, lax.rem(self.member, 2)
        high, low = chip // side, lax.rem(chip, side)
        self.first = low + (high - low) * self.core
        self.second = high + (low - high) * self.core
        self.partner = self.member + 1 - 2 * self.core
        self.sends, self.arrivals = sends, arrivals

    def chip_at(self, first, second):
        low = first + (second - first) * self.core
        high = second + (first - second) * self.core
        return (high * self.side + low) * 2 + self.core

    def first_peer(self, k):
        other = lax.rem(self.first + k, self.side)
        return other, self.chip_at(other, self.second)

    def second_peer(self, k):
        other = lax.rem(self.second + k, self.side)
        return other, self.chip_at(self.first, other)

    def plane_peer(self, k):
        return lax.rem(self.plane + k, self.planes)

    def signal_peers(self, barrier):
        peers = [{"exp": self.partner}]
        peers += [{"exp": self.first_peer(k)[1]} for k in range(1, self.side)]
        peers += [{"exp": self.second_peer(k)[1]} for k in range(1, self.side)]
        peers += [{"seq": self.plane_peer(k)} for k in range(1, self.planes)]
        for peer in peers:
            pl.semaphore_signal(barrier, inc=1, device_id=peer, device_id_type=MESH)
        return len(peers)

    def move(self, stage, at, slot, src, dst, axis, peer):
        return remote(
            src, dst, self.sends[stage].at[at], self.arrivals[stage].at[slot], axis, peer
        )

    def pair_half(self, i, given, half):
        return self.move(0, i, i, given.at[1 - self.core], half, "exp", self.partner)

    def scatter_first(self, i, k, half, slots, arriving):
        other, device = self.first_peer(k)
        slot = other if arriving else self.first
        return self.move(1, (i, k), (i, slot), half.at[other], slots.at[slot], "exp", device)

    def scatter_second(self, i, k, quarter, slots, arriving):
        other, device = self.second_peer(k)
        slot = other if arriving else self.second
        return self.move(2, (i, k), (i, slot), quarter.at[other], slots.at[slot], "exp", device)

    def scatter_plane(self, i, k, eighth, slots, arriving):
        other = self.plane_peer(k)
        slot = other if arriving else self.plane
        return self.move(3, (i, k), (i, slot), eighth.at[other], slots.at[slot], "seq", other)

    def gather_plane(self, i, k, block, arriving):
        other = self.plane_peer(k)
        slot = other if arriving else self.plane
        return self.move(
            4, (i, k), (i, slot), block.at[self.plane], block.at[slot], "seq", other
        )

    def gather_second(self, i, k, result, arriving):
        other, device = self.second_peer(k)
        slot = other if arriving else self.second
        row = result.at[self.core, self.first]
        return self.move(5, (i, k), (i, slot), row.at[self.second], row.at[slot], "exp", device)

    def gather_first(self, i, k, result, arriving):
        other, device = self.first_peer(k)
        slot = other if arriving else self.first
        own = result.at[self.core]
        return self.move(6, (i, k), (i, slot), own.at[self.first], own.at[slot], "exp", device)

    def pair_gather(self, i, k, result, arriving):
        other = lax.rem(self.first + k, self.side)
        low = lax.rem(self.partner // 2, self.side)
        theirs = low + (self.partner // (2 * self.side) - low) * (1 - self.core)
        other = lax.rem(theirs + k, self.side) if arriving else other
        half = 1 - self.core if arriving else self.core
        mine = result.at[self.core, lax.rem(self.first + k, self.side)]
        return self.move(7, (i, k), (i, k), mine, result.at[half, other], "exp", self.partner)

    def after_pair(self, i, given, half, slots):
        self.pair_half(i, given, half).wait()
        own = self.core
        for at in range(self.side):
            for to in range(self.side):
                both = given[own, at, to].astype(jnp.float32) + half[at, to].astype(jnp.float32)
                half[at, to] = both.astype(jnp.bfloat16)
        for k in range(1, self.side):
            self.scatter_first(i, k, half, slots, False).start()
        slots[self.first] = half[self.first]

    def after_first(self, i, half, slots, quarter, slots_two):
        for k in range(1, self.side):
            self.scatter_first(i, k, half, slots, True).wait_recv()
        for at in range(self.side):
            added = slots[0, at].astype(jnp.float32)
            for k in range(1, self.side):
                added = added + slots[k, at].astype(jnp.float32)
            quarter[at] = added.astype(jnp.bfloat16)
        for k in range(1, self.side):
            self.scatter_second(i, k, quarter, slots_two, False).start()
        slots_two[self.second] = quarter[self.second]

    def after_second(self, i, quarter, slots_two, eighth, slots_three):
        for k in range(1, self.side):
            self.scatter_second(i, k, quarter, slots_two, True).wait_recv()
        added = slots_two[0].astype(jnp.float32)
        for k in range(1, self.side):
            added = added + slots_two[k].astype(jnp.float32)
        eighth[...] = added.astype(jnp.bfloat16)
        for k in range(1, self.planes):
            self.scatter_plane(i, k, eighth, slots_three, False).start()
        slots_three[self.plane] = eighth[self.plane]

    def after_planes(self, i, eighth, slots_three, block):
        for k in range(1, self.planes):
            self.scatter_plane(i, k, eighth, slots_three, True).wait_recv()
        added = slots_three[0].astype(jnp.float32)
        for k in range(1, self.planes):
            added = added + slots_three[k].astype(jnp.float32)
        block[self.plane] = added.astype(jnp.bfloat16)
        for k in range(1, self.planes):
            self.gather_plane(i, k, block, False).start()

    def planes_gathered(self, i, block):
        for k in range(1, self.planes):
            self.gather_plane(i, k, block, True).wait_recv()

    def scatter_sent(self, i, half, slots, quarter, slots_two, eighth, slots_three, block):
        for k in range(1, self.side):
            self.scatter_first(i, k, half, slots, False).wait_send()
            self.scatter_second(i, k, quarter, slots_two, False).wait_send()
        for k in range(1, self.planes):
            self.scatter_plane(i, k, eighth, slots_three, False).wait_send()
            self.gather_plane(i, k, block, False).wait_send()

    def gather_second_start(self, i, result):
        for k in range(1, self.side):
            self.gather_second(i, k, result, False).start()

    def gather_across(self, i, result):
        for k in range(1, self.side):
            self.gather_second(i, k, result, True).wait_recv()
        for k in range(1, self.side):
            self.gather_first(i, k, result, False).start()
        self.pair_gather(i, 0, result, False).start()

    def gather_pass(self, i, result):
        for k in range(1, self.side):
            self.gather_first(i, k, result, True).wait_recv()
            self.pair_gather(i, k, result, False).start()

    def gather_end(self, i, result):
        for k in range(self.side):
            self.pair_gather(i, k, result, True).wait_recv()
            self.pair_gather(i, k, result, False).wait_send()
        for k in range(1, self.side):
            self.gather_first(i, k, result, False).wait_send()
            self.gather_second(i, k, result, False).wait_send()


def stage_semaphores(count, planes, side):
    each = [(count,)] + [(count, size) for size in (side, side, planes, planes, side, side, side)]
    return [pltpu.SemaphoreType.DMA(shape) for shape in each]


def scatter_buffers(tails, planes, side):
    leads = [(side, side, planes), (side, side, planes), (side, planes), (side, planes)]
    leads += [(planes,), (planes,)]
    return [pltpu.VMEM(lead + tail, jnp.bfloat16) for lead in leads for tail in tails]


def neighbour_plane():
    plane = lax.axis_index("seq")
    return {"seq": plane + 1 - 2 * lax.rem(plane, 2)}


def swapped(src, dst, send, arrive):
    return pltpu.make_async_remote_copy(
        src_ref=src,
        dst_ref=dst,
        send_sem=send,
        recv_sem=arrive,
        device_id=neighbour_plane(),
        device_id_type=MESH,
    )


class Routes:
    def __init__(self, planes, members, sends, arrivals, local):
        self.planes, self.members = planes, members
        self.plane, self.member = lax.axis_index("seq"), lax.axis_index("exp")
        self.hops = planes // 2
        self.sends, self.arrivals, self.local = sends, arrivals, local
        self.pairs = [
            (hop, k) for hop in reversed(range(self.hops)) for k in range(members) if hop or k
        ]

    def device(self, hop, k):
        return {
            "seq": lax.rem(self.plane + 2 * hop, self.planes),
            "exp": lax.rem(self.member + k, self.members),
        }

    def signal_peers(self, barrier):
        for hop, k in self.pairs:
            pl.semaphore_signal(
                barrier, inc=1, device_id=self.device(hop, k), device_id_type=MESH
            )
        return len(self.pairs)

    def moved(self, given, landed, returning, hop, k, arriving):
        device = self.device(hop, k)
        other = device["exp"]
        slot = hop if arriving else (-hop) % self.hops
        sender = other if arriving else self.member
        return pltpu.make_async_remote_copy(
            src_ref=given.at[hop, other] if returning else given.at[other],
            dst_ref=landed.at[slot, sender],
            send_sem=self.sends.at[hop, k],
            recv_sem=self.arrivals.at[slot, sender],
            device_id=device,
            device_id_type=MESH,
        )

    def own(self, given, landed, returning):
        src = given.at[0, self.member] if returning else given.at[self.member]
        return pltpu.make_async_copy(src, landed.at[0, self.member], self.local)

    def start(self, given, landed, returning):
        for hop, k in self.pairs:
            self.moved(given, landed, returning, hop, k, False).start()
        self.own(given, landed, returning).start()

    def wait_group(self, given, landed, hop):
        for at, k in self.pairs:
            if at == hop:
                self.moved(given, landed, False, hop, k, True).wait_recv()
        if hop == 0:
            self.own(given, landed, False).wait()

    def wait_sent(self, given, landed):
        for hop, k in self.pairs:
            self.moved(given, landed, False, hop, k, False).wait_send()

    def wait(self, given, landed, returning):
        for hop, k in self.pairs:
            self.moved(given, landed, returning, hop, k, True).wait_recv()
        self.own(given, landed, returning).wait()
        for hop, k in self.pairs:
            self.moved(given, landed, returning, hop, k, False).wait_send()


def route_semaphores(planes, members):
    shape = (planes // 2, members)
    return [
        pltpu.SemaphoreType.DMA(shape),
        pltpu.SemaphoreType.DMA(shape),
        pltpu.SemaphoreType.DMA,
    ]


def two_part(left, right, dims):
    high = left.astype(jnp.bfloat16)
    rest = (left - high.astype(jnp.float32)).astype(jnp.bfloat16)
    numbers = (dims, ((), ()))
    wide = jnp.float32
    return lax.dot_general(high, right, numbers, preferred_element_type=wide) + lax.dot_general(
        rest, right, numbers, preferred_element_type=wide
    )


LANE_UNIT = 256


def lane_unit(j):
    return pl.ds(pl.multiple_of(j * LANE_UNIT, LANE_UNIT), LANE_UNIT)


def normalized(values, gain):
    return values * lax.rsqrt(jnp.mean(values * values, axis=-1, keepdims=True) + EPSILON) * gain


def chain_device(at, members):
    return {"seq": at // members, "exp": lax.rem(at, members)}


def forward_kernel(
    planes,
    members,
    capacity,
    layer_ref,
    out_grad_ref,
    target_ref,
    vectors_ref,
    in_proj_ref,
    conv_weight_ref,
    state_proj_ref,
    delta_proj_ref,
    decay_log_ref,
    own_log_ref,
    out_proj_ref,
    up_ref,
    down_ref,
    normed_ref,
    extended_ref,
    gate_ref,
    conv_pre_ref,
    conv_ref,
    delta_pre_ref,
    delta_ref,
    delta_low_ref,
    in_cols_ref,
    out_cols_ref,
    in_diag_ref,
    delta_sum_ref,
    carried_ref,
    mixer_pre_ref,
    mixed_ref,
    resid_ref,
    row_slots_ref,
    grad_rows_ref,
    near_up_ref,
    near_half_ref,
    rim_in_ref,
    grad_slots_ref,
    drive_ref,
    stack_ref,
    low_sum_ref,
    wide_sum_ref,
    out_diag_ref,
    out_rest_ref,
    local_end_ref,
    rim_out_ref,
    rim_sent_ref,
    rim_landed_ref,
    up_sent_ref,
    up_landed_ref,
    down_sent_ref,
    down_landed_ref,
    *rest,
):
    exchange_refs, grad_semaphores = rest[:12], rest[12:15]
    wide, half = jnp.float32, jnp.bfloat16
    tokens, width = layer_ref.shape
    own_tokens = slice(0, tokens)
    inner_width = conv_ref.shape[1]
    sequences = extended_ref.shape[0]
    piece = tokens // sequences
    states, taps = decay_log_ref.shape[0], conv_weight_ref.shape[0]
    low_rank = delta_low_ref.shape[1]
    experts = row_slots_ref.shape[0]
    conv_bias_ref, delta_bias_ref, skip_ref = (vectors_ref.at[i : i + 1] for i in range(3))
    mixer_gain_ref, expert_norm_ref = vectors_ref.at[3:4, :width], vectors_ref.at[3:4, width:]
    devices = planes * members
    place = lax.axis_index("seq") * members + lax.axis_index("exp")
    before, after = lax.rem(place + devices - 1, devices), lax.rem(place + 1, devices)
    grad_routes = Routes(planes, members, *grad_semaphores)
    barrier = pltpu.get_barrier_semaphore()
    for peer in (before, after):
        device = chain_device(peer, members)
        pl.semaphore_signal(barrier, inc=1, device_id=device, device_id_type=MESH)
    greeted = 2 + grad_routes.signal_peers(barrier)
    for axis, size in (("seq", planes), ("exp", members)):
        mine = lax.axis_index(axis)
        for k in range(1, size):
            other = {axis: lax.rem(mine + k, size)}
            pl.semaphore_signal(barrier, inc=1, device_id=other, device_id_type=MESH)
        greeted += size - 1
    for q in range(sequences):
        rim_out_ref[q] = layer_ref[(q + 1) * piece - 8 : (q + 1) * piece]
    pl.semaphore_wait(barrier, greeted)
    rim_copy = pltpu.make_async_remote_copy(
        src_ref=rim_out_ref,
        dst_ref=rim_in_ref,
        send_sem=rim_sent_ref,
        recv_sem=rim_landed_ref,
        device_id=chain_device(after, members),
        device_id_type=MESH,
    )
    rim_copy.start()
    up_swap = swapped(up_ref, near_up_ref, up_sent_ref, up_landed_ref)
    up_swap.start()
    cut = down_ref.shape[1] // 2
    down_swap = swapped(down_ref.at[:, pl.ds(0, cut)], near_half_ref, down_sent_ref, down_landed_ref)

    count = inner_width // LANE_UNIT
    normed_ref[own_tokens, :] = normalized(layer_ref[...].astype(wide), mixer_gain_ref[...]).astype(half)

    def project(j, carry):
        at = lane_unit(j)
        product = half_dot(normed_ref[own_tokens, :], in_proj_ref[:, at])
        for q in range(sequences):
            extended_ref[q, 8:, at] = product[q * piece : (q + 1) * piece]
        gate_at = pl.ds(pl.multiple_of(inner_width + j * LANE_UNIT, LANE_UNIT), LANE_UNIT)
        gate_ref[:, at] = half_dot(normed_ref[own_tokens, :], in_proj_ref[:, gate_at])
        return carry

    lax.fori_loop(0, count, project, 0)
    rim_copy.wait()
    keep = jnp.where(place > 0, 1.0, 0.0)
    rims = [normalized(rim_in_ref[q].astype(wide), mixer_gain_ref[...]) for q in range(sequences)]
    rim_normed = jnp.concatenate(rims, axis=0).astype(half)
    normed_ref[tokens:, :] = rim_normed
    low_sum_ref[...] = jnp.zeros(low_sum_ref.shape, wide)
    wide_sum_ref[...] = jnp.zeros(wide_sum_ref.shape, wide)

    def convolve(j, carry):
        at = lane_unit(j)
        rim = half_dot(rim_normed, in_proj_ref[:, at]) * keep
        for q in range(sequences):
            extended_ref[q, :8, at] = rim[q * 8 : (q + 1) * 8]
            start = 8 - (taps - 1)
            pre = conv_bias_ref[:, at] + conv_weight_ref[:1, at] * extended_ref[q, start : start + piece, at]
            for tap in range(1, taps):
                moved = extended_ref[q, start + tap : start + tap + piece, at]
                pre = pre + conv_weight_ref[tap : tap + 1, at] * moved
            conv_pre_ref[q * piece : (q + 1) * piece, at] = pre
            conv_ref[q * piece : (q + 1) * piece, at] = pre * jax.nn.sigmoid(pre)
        act = conv_ref[:, at]
        high = act.astype(half)
        low = (act - high.astype(wide)).astype(half)
        weight = state_proj_ref[:, at]
        low_sum_ref[...] += cols_dot(high, weight) + cols_dot(low, weight)
        tail = weight[low_rank:]
        wide_sum_ref[...] += cols_dot(tail, high) + cols_dot(tail, low)
        return carry

    lax.fori_loop(0, count, convolve, 0)
    delta_low_ref[...] = low_sum_ref[:, :low_rank]
    for i in range(tokens // BLK):
        block = wide_sum_ref[:, i * BLK : (i + 1) * BLK]
        in_cols_ref[i] = block[:states]
        out_cols_ref[i] = block[states:]
    shape = (tokens, BLK * states)
    column = lax.broadcasted_iota(jnp.int32, shape, 1)
    row = lax.rem(lax.broadcasted_iota(jnp.int32, shape, 0), BLK)
    own = column // states == row
    tile = jnp.where(
        lax.rem(lax.broadcasted_iota(jnp.int32, (states, BLK * states), 1), states)
        == lax.broadcasted_iota(jnp.int32, (states, BLK * states), 0),
        1.0,
        0.0,
    ).astype(half)

    def spread_out(values):
        return jnp.where(own, half_dot(values, tile), 0.0).astype(half)

    outward = low_sum_ref[:, low_rank + states :]
    out_high = outward.astype(half)
    in_diag_ref[...] = spread_out(low_sum_ref[:, low_rank : low_rank + states].astype(half))
    out_diag_ref[...] = spread_out(out_high)
    out_rest_ref[...] = spread_out((outward - out_high.astype(wide)).astype(half))

    def time_steps(j, carry):
        at = lane_unit(j)
        pre = two_part(delta_low_ref[...], delta_proj_ref[:, at], ((1,), (0,))) + delta_bias_ref[:, at]
        delta = jnp.maximum(pre, 0.0) + jnp.log1p(jnp.exp(-jnp.abs(pre)))
        delta_pre_ref[:, at] = pre
        delta_ref[:, at] = delta
        for q in range(sequences):
            part = delta[q * piece : (q + 1) * piece]
            delta_sum_ref[q : q + 1, at] = jnp.sum(part, axis=0, keepdims=True)
        return carry

    lax.fori_loop(0, count, time_steps, 0)
    groups = inner_width // GROUP
    blocks = piece // BLK

    def views(i):
        q, j = i // groups, lax.rem(i, groups)
        rows = pl.ds(pl.multiple_of(q * piece, piece), piece)
        lanes = pl.ds(pl.multiple_of(j * GROUP, GROUP), GROUP)
        cols = pl.ds(q * blocks, blocks)
        return q, rows, lanes, cols

    def first(i, carry):
        q, rows, lanes, cols = views(i)
        first_pass_kernel(
            delta_ref.at[rows, lanes],
            conv_ref.at[rows, lanes],
            in_cols_ref.at[cols],
            decay_log_ref.at[:, lanes],
            local_end_ref.at[pl.ds(q, 1), :, lanes],
            drive_ref,
        )
        return carry

    lax.fori_loop(0, sequences * groups, first, 0)
    exchange_body(
        False, planes, members, local_end_ref, delta_sum_ref, own_log_ref, carried_ref, *exchange_refs
    )
    up_swap.wait()
    slot = lax.broadcasted_iota(jnp.int32, (experts * capacity, tokens), 0)
    picks = jnp.where(slot == target_ref[...], 1.0, 0.0).astype(half)

    def fill(slots, values):
        product = half_dot(picks, values).astype(half)
        for e in range(experts):
            slots[e] = product[e * capacity : (e + 1) * capacity]

    fill(grad_slots_ref, out_grad_ref[...])
    grad_routes.start(grad_slots_ref, grad_rows_ref, False)
    down_swap.start()

    def second(i, carry):
        q, rows, lanes, cols = views(i)
        second_pass_kernel(
            delta_ref.at[rows, lanes],
            conv_ref.at[rows, lanes],
            in_cols_ref.at[cols],
            decay_log_ref.at[:, lanes],
            carried_ref.at[pl.ds(q, 1), :, lanes],
            out_diag_ref.at[rows],
            out_rest_ref.at[rows],
            mixer_pre_ref.at[rows, lanes],
            drive_ref,
            stack_ref,
        )
        return carry

    lax.fori_loop(0, sequences * groups, second, 0)

    def mix(j, carry):
        at = lane_unit(j)
        pre = mixer_pre_ref[:, at] + skip_ref[:, at] * conv_ref[:, at]
        gate = gate_ref[:, at]
        mixer_pre_ref[:, at] = pre
        mixed_ref[:, at] = (pre * (gate * jax.nn.sigmoid(gate))).astype(half)
        return carry

    lax.fori_loop(0, count, mix, 0)
    resid_ref[...] = layer_ref[...].astype(wide) + half_dot(mixed_ref[...], out_proj_ref[...])
    fill(row_slots_ref, normalized(resid_ref[...], expert_norm_ref[...]).astype(half))
    grad_routes.wait(grad_slots_ref, grad_rows_ref, False)
    down_swap.wait()


def forward(operands, capacity, states, sequences, low_rank, experts):
    planes, members = lax.axis_size("seq"), lax.axis_size("exp")
    tokens, width = operands[0].shape
    inner_width = operands[3].shape[1]
    up, down = operands[11:13]
    half, wide = jnp.bfloat16, jnp.float32
    piece = tokens // sequences
    token_wide = jax.ShapeDtypeStruct((tokens, inner_width), wide)
    cols = jax.ShapeDtypeStruct((tokens // BLK, states, BLK), wide)
    diag = (tokens, BLK * states)
    routed = jax.ShapeDtypeStruct((planes // 2, members, capacity, width), half)
    state = (sequences, states, inner_width)
    vmem, anywhere = (pl.BlockSpec(memory_space=space) for space in (pltpu.VMEM, pl.ANY))
    scratch = [
        pltpu.VMEM((experts, capacity, width), half),
        pltpu.VMEM((piece, GROUP), wide),
        pltpu.VMEM((BLK * states, GROUP), half),
        pltpu.VMEM((tokens, low_rank + 2 * states), wide),
        pltpu.VMEM((2 * states, tokens), wide),
        pltpu.VMEM(diag, half),
        pltpu.VMEM(diag, half),
        pltpu.VMEM(state, wide),
        pltpu.VMEM((sequences, 8, width), half),
    ]
    scratch += [pltpu.SemaphoreType.DMA] * 6
    scratch += exchange_scratch(planes, members, sequences * states // members, inner_width)
    scratch += route_semaphores(planes, members)
    return pl.pallas_call(
        functools.partial(forward_kernel, planes, members, capacity),
        name="forward_to_experts",
        in_specs=[vmem] * 11 + [anywhere] * 2,
        out_specs=[vmem] * 17 + [anywhere] * 3 + [vmem],
        out_shape=[
            jax.ShapeDtypeStruct((tokens + 8 * sequences, width), half),
            jax.ShapeDtypeStruct((sequences, piece + 8, inner_width), wide),
            token_wide,
            token_wide,
            token_wide,
            token_wide,
            token_wide,
            jax.ShapeDtypeStruct((tokens, low_rank), wide),
            cols,
            cols,
            jax.ShapeDtypeStruct(diag, half),
            jax.ShapeDtypeStruct((sequences, inner_width), wide),
            jax.ShapeDtypeStruct(state, wide),
            token_wide,
            jax.ShapeDtypeStruct((tokens, inner_width), half),
            jax.ShapeDtypeStruct((tokens, width), wide),
            jax.ShapeDtypeStruct((experts, capacity, width), half),
            routed,
            jax.ShapeDtypeStruct(up.shape, half),
            jax.ShapeDtypeStruct((1, down.shape[1] // 2, width), half),
            jax.ShapeDtypeStruct((sequences, 8, width), half),
        ],
        scratch_shapes=scratch,
        compiler_params=pltpu.CompilerParams(
            collective_id=1, has_side_effects=True, vmem_limit_bytes=60 * 1024 * 1024
        ),
        cost_estimate=pl.CostEstimate(flops=10**8, transcendentals=0, bytes_accessed=2 * 10**8),
    )(*operands)


def expert_kernel(
    planes,
    members,
    row_slots_ref,
    grad_rows_ref,
    up_ref,
    down_ref,
    near_up_ref,
    near_half_ref,
    router_ref,
    chosen_ref,
    outs_ref,
    back_ref,
    grad_up_ref,
    grad_down_ref,
    far_up_ref,
    far_down_ref,
    grad_router_ref,
    landed_ref,
    rows_ref,
    grads_ref,
    sent_ref,
    near_down_ref,
    out_sum_ref,
    row_sum_ref,
    hidden_own_ref,
    hidden_near_ref,
    pre_own_ref,
    pre_near_ref,
    shares_ref,
    far_up_sum_ref,
    far_down_sum_ref,
    returns_ref,
    down_sent_ref,
    down_landed_ref,
    back_sent_ref,
    back_landed_ref,
    *rest,
):
    routes = Routes(planes, members, *rest)
    wide, half = jnp.float32, jnp.bfloat16
    plane, member, hops = routes.plane, routes.member, routes.hops
    capacity, width = row_slots_ref.shape[1:]
    batch = members // 2
    chunk = batch * capacity
    group = members * capacity
    units = up_ref.shape[2]
    cut = units // 2
    barrier = pltpu.get_barrier_semaphore()
    pl.semaphore_signal(barrier, inc=1, device_id=neighbour_plane(), device_id_type=MESH)
    pl.semaphore_wait(barrier, routes.signal_peers(barrier) + 1)
    routes.start(row_slots_ref, landed_ref, False)
    down_swap = swapped(
        down_ref.at[0, pl.ds(cut, cut)], near_down_ref.at[pl.ds(cut, cut)], down_sent_ref, down_landed_ref
    )
    down_swap.start()
    near_down_ref[:cut] = near_half_ref[0]
    grad_router_ref[...] = jnp.zeros(grad_router_ref.shape, wide)
    for hop in range(hops):
        for e in range(members):
            grads_ref[hop * group + e * capacity : hop * group + (e + 1) * capacity] = grad_rows_ref[
                hop, e
            ]

    def gather(hop):
        routes.wait_group(row_slots_ref, landed_ref, hop)
        for e in range(members):
            rows_ref[hop * group + e * capacity : hop * group + (e + 1) * capacity] = landed_ref[hop, e]

    def through(at, up, down, hidden, back, where):
        pre = half_dot(rows_ref[at, :], up)
        phi = 0.5 * (1.0 + lax.erf(pre * 0.7071067811865476))
        slope = phi + pre * (jnp.exp(-0.5 * pre * pre) * 0.3989422804014327)
        active = (pre * phi).astype(half)
        hidden[at, where] = active
        arrived = (slope * cols_dot(sent_ref[at, :], down)).astype(half)
        back[at, where] = arrived
        return half_dot(active, down), cols_dot(arrived, up)

    def place(hop, c):
        return pl.ds(pl.multiple_of(hop * group + c * chunk, chunk), chunk)

    def own_part(hop, c):
        at = place(hop, c)
        logits = cols_dot(rows_ref[at, :].astype(wide), router_ref[...], lax.Precision.HIGHEST)
        raised = jnp.exp(logits - jnp.max(logits, axis=-1, keepdims=True))
        shares = raised / jnp.sum(raised, axis=-1, keepdims=True)
        gate = jnp.sum(shares * chosen_ref[...], axis=-1, keepdims=True)
        shares_ref[at, :] = shares
        sent_ref[at, :] = (gate * grads_ref[at, :].astype(wide)).astype(half)
        every = slice(0, units)
        out, row = through(at, up_ref[0], down_ref[0], hidden_own_ref, pre_own_ref, every)
        early = slice(0, cut)
        near_out, near_row = through(
            at, near_up_ref[0, :, :cut], near_down_ref[:cut], hidden_near_ref, pre_near_ref, early
        )
        out_sum_ref[at, :] = out + near_out
        row_sum_ref[at, :] = row + near_row

    def late_part(hop, c):
        at = place(hop, c)
        near_out, near_row = through(
            at,
            near_up_ref[0, :, cut:],
            near_down_ref[cut:],
            hidden_near_ref,
            pre_near_ref,
            slice(cut, units),
        )
        out = out_sum_ref[at, :] + near_out
        shares, chosen = shares_ref[at, :], chosen_ref[...]
        gate = jnp.sum(shares * chosen, axis=-1, keepdims=True)
        grad_gate = jnp.sum(grads_ref[at, :].astype(wide) * out, axis=-1, keepdims=True)
        grad_logits = grad_gate * gate * (chosen - shares)
        outs = (gate * out).astype(half)
        row = row_sum_ref[at, :] + near_row
        row = row + jnp.dot(
            grad_logits,
            router_ref[...],
            precision=lax.Precision.HIGHEST,
            preferred_element_type=wide,
        )
        row = row.astype(half)
        grad_router_ref[...] += rows_dot(
            grad_logits, rows_ref[at, :].astype(wide), lax.Precision.HIGHEST
        )
        for k in range(batch):
            part = slice(k * capacity, (k + 1) * capacity)
            outs_ref[hop, c * batch + k] = outs[part]
            returns_ref[hop, c * batch + k] = row[part]

    def returned(hop, e, arriving):
        slot = hop if arriving else (-hop) % hops
        sender = e if arriving else member
        return pltpu.make_async_remote_copy(
            src_ref=returns_ref.at[hop, e],
            dst_ref=back_ref.at[slot, sender],
            send_sem=back_sent_ref.at[hop, e],
            recv_sem=back_landed_ref.at[slot, sender],
            device_id={"seq": lax.rem(plane + 2 * hop, planes), "exp": e},
            device_id_type=MESH,
        )

    def give_back(hop, c):
        for k in range(batch):
            e = c * batch + k
            if hop:
                returned(hop, e, False).start()
            else:

                @pl.when(e != member)
                def _():
                    returned(0, e, False).start()

    def loop(body):
        def run(c, carry):
            body(c)
            return carry

        lax.fori_loop(0, 2, run, 0)

    def weight_grads(hop):
        at = slice(hop * group, (hop + 1) * group)
        rows, sent = rows_ref[at, :], sent_ref[at, :]
        products = [
            (grad_up_ref.at[0], rows, pre_own_ref[at, :]),
            (grad_down_ref.at[0], hidden_own_ref[at, :], sent),
            (far_up_sum_ref, rows, pre_near_ref[at, :]),
            (far_down_sum_ref, hidden_near_ref[at, :], sent),
        ]
        for total, left, right in products:
            if hop:
                total[...] += rows_dot(left, right)
            else:
                total[...] = rows_dot(left, right)

    gather(0)
    loop(functools.partial(own_part, 0))
    down_swap.wait()

    def near_end(c):
        late_part(0, c)
        give_back(0, c)

    loop(near_end)
    weight_grads(0)
    for hop in range(1, hops):
        gather(hop)

        def far_end(c):
            own_part(hop, c)
            late_part(hop, c)
            give_back(hop, c)

        loop(far_end)
        weight_grads(hop)
    far_up_ref[0] = far_up_sum_ref[...].astype(half)
    far_down_ref[0] = far_down_sum_ref[...].astype(half)
    back_ref[0, member] = returns_ref[0, member]
    for hop in range(hops):
        for k in range(members):
            if hop or k:
                e = lax.rem(member + k, members)
                returned(hop, e, True).wait_recv()
                returned(hop, e, False).wait_send()
    routes.wait_sent(row_slots_ref, landed_ref)


def expert_apply(row_slots, grad_rows, weights, router, chosen):
    planes, members = lax.axis_size("seq"), lax.axis_size("exp")
    experts, capacity, width = row_slots.shape
    up, down, near_up, near_half = weights
    units = up.shape[2]
    hops = planes // 2
    count = hops * members * capacity
    half, wide = jnp.bfloat16, jnp.float32
    vmem = pl.BlockSpec(memory_space=pltpu.VMEM)
    slotted = (hops, members, capacity, width)
    every = (hops, members)
    return pl.pallas_call(
        functools.partial(expert_kernel, planes, members),
        name="expert_apply",
        in_specs=[vmem] * 8,
        out_specs=[vmem] * 7,
        out_shape=[
            jax.ShapeDtypeStruct(slotted, half),
            jax.ShapeDtypeStruct(slotted, half),
            jax.ShapeDtypeStruct(up.shape, wide),
            jax.ShapeDtypeStruct(down.shape, wide),
            jax.ShapeDtypeStruct(up.shape, half),
            jax.ShapeDtypeStruct(down.shape, half),
            jax.ShapeDtypeStruct(router.shape, wide),
        ],
        scratch_shapes=[
            pltpu.VMEM(slotted, half),
            pltpu.VMEM((count, width), half),
            pltpu.VMEM((count, width), half),
            pltpu.VMEM((count, width), half),
            pltpu.VMEM(down.shape[1:], half),
            pltpu.VMEM((count, width), wide),
            pltpu.VMEM((count, width), wide),
            pltpu.VMEM((count, units), half),
            pltpu.VMEM((count, units), half),
            pltpu.VMEM((count, units), half),
            pltpu.VMEM((count, units), half),
            pltpu.VMEM((count, experts), wide),
            pltpu.VMEM(up.shape[1:], wide),
            pltpu.VMEM(down.shape[1:], wide),
            pltpu.VMEM(slotted, half),
            pltpu.SemaphoreType.DMA,
            pltpu.SemaphoreType.DMA,
            pltpu.SemaphoreType.DMA(every),
            pltpu.SemaphoreType.DMA(every),
        ]
        + route_semaphores(planes, members),
        compiler_params=pltpu.CompilerParams(
            collective_id=4, has_side_effects=True, vmem_limit_bytes=60 * 1024 * 1024
        ),
        cost_estimate=pl.CostEstimate(
            flops=24 * count * width * units,
            transcendentals=4 * count * units,
            bytes_accessed=3 * 10**7,
        ),
    )(row_slots, grad_rows, *weights, router, chosen)


def gradient_kernel(
    planes,
    side,
    delta_ref,
    conv_ref,
    grad_scan_ref,
    in_cols_ref,
    out_cols_ref,
    in_diag_ref,
    decay_log_ref,
    carried_ref,
    carried_back_ref,
    delta_pre_ref,
    delta_low_ref,
    conv_pre_ref,
    extended_ref,
    normed_ref,
    normed_gate_ref,
    layer_ref,
    rim_layer_ref,
    grad_resid_ref,
    delta_proj_ref,
    state_proj_ref,
    in_proj_ref,
    conv_weight_ref,
    vectors_ref,
    skip_grad_ref,
    norm_grad_ref,
    router_grad_ref,
    early_out_ref,
    early_gate_ref,
    returned_ref,
    far_up_ref,
    far_down_ref,
    in_grad_ref,
    total_out_ref,
    total_gate_ref,
    total_inner_ref,
    total_small_ref,
    landed_ref,
    near_up_ref,
    near_down_ref,
    grad_delta,
    grad_conv,
    grad_in,
    grad_out,
    grad_log,
    drive,
    kept,
    stack,
    slope_stack,
    low_grads,
    padded,
    slopes,
    small,
    rim_out,
    rim_in,
    rim_sent,
    rim_landed,
    in_part,
    part_loaded,
    given_inner,
    given_small,
    *rest,
):
    early_buffers, tail_buffers, small_buffers = rest[:12], rest[12:18], rest[18:24]
    swap_sent, swap_landed, rest = rest[24], rest[25], rest[26:]
    sums = Sums(planes, side, rest[:8], rest[8:16])
    routes = Routes(planes, 2 * side * side, *rest[16:19])
    tokens, inner_width = conv_ref.shape
    width = layer_ref.shape[1]
    low_rank = delta_low_ref.shape[1]
    states, taps = decay_log_ref.shape[0], conv_weight_ref.shape[0]
    sequences = extended_ref.shape[0]
    piece = tokens // sequences
    chips = side * side
    wide, half = jnp.float32, jnp.bfloat16
    skip_ref, mixer_gain_ref = vectors_ref.at[2:3], vectors_ref.at[3:4, :width]
    devices = 2 * chips * planes
    place = sums.plane * (2 * chips) + sums.member
    before, after = lax.rem(place + devices - 1, devices), lax.rem(place + 1, devices)
    barrier = pltpu.get_barrier_semaphore()
    for peer in (before, after):
        device = chain_device(peer, 2 * chips)
        pl.semaphore_signal(barrier, inc=1, device_id=device, device_id_type=MESH)
    pl.semaphore_signal(barrier, inc=1, device_id=neighbour_plane(), device_id_type=MESH)
    greeted = 3 + sums.signal_peers(barrier) + routes.signal_peers(barrier)
    pl.semaphore_wait(barrier, greeted)

    in_load = pltpu.make_async_copy(in_proj_ref.at[:, pl.ds(0, inner_width)], in_part, part_loaded)
    in_load.start()
    pair = range(2)
    given = (early_out_ref, early_gate_ref)
    results = (total_out_ref, total_gate_ref)
    stages = [tuple(early_buffers[2 * stage + i] for stage in range(6)) for i in pair]
    blocks = [result.at[sums.core, sums.first, sums.second] for result in results]
    swaps = [
        swapped(src, dst, swap_sent.at[i], swap_landed.at[i])
        for i, (src, dst) in enumerate([(far_up_ref, near_up_ref), (far_down_ref, near_down_ref)])
    ]
    for i in pair:
        sums.pair_half(i, given[i], stages[i][0]).start()
    routes.start(returned_ref, landed_ref, True)
    swaps[0].start()
    groups = inner_width // GROUP
    count = sequences * groups
    cols_each = piece // BLK

    def scan_group(g, carry):
        q, j = g // groups, lax.rem(g, groups)
        rows = pl.ds(pl.multiple_of(q * piece, piece), piece)
        lanes = pl.ds(pl.multiple_of(j * GROUP, GROUP), GROUP)
        cols = pl.ds(q * cols_each, cols_each)

        def middle():
            @pl.when(g == 0)
            def _():
                for i in pair:
                    sums.after_pair(i, given[i], *stages[i][:2])

            @pl.when(g == count // 2)
            def _():
                for i in pair:
                    sums.after_first(i, *stages[i][:4])

            @pl.when(g == count - 2)
            def _():
                for i in pair:
                    sums.after_second(i, *stages[i][2:6])

            @pl.when(g == count - 1)
            def _():
                for i in pair:
                    sums.after_planes(i, *stages[i][4:6], blocks[i])
                swaps[1].start()

        one = pl.ds(q, 1)
        backward_body(
            middle,
            j == 0,
            delta_ref.at[rows, lanes],
            conv_ref.at[rows, lanes],
            grad_scan_ref.at[rows, lanes],
            in_cols_ref.at[cols],
            out_cols_ref.at[cols],
            in_diag_ref.at[rows],
            decay_log_ref.at[:, lanes],
            carried_ref.at[one, :, lanes],
            carried_back_ref.at[one, :, lanes],
            grad_delta.at[rows, lanes],
            grad_conv.at[rows, lanes],
            grad_in.at[rows],
            grad_out.at[rows],
            grad_log.at[one, :, lanes],
            drive,
            kept,
            stack,
            slope_stack,
        )
        return carry

    lax.fori_loop(0, count, scan_group, 0)
    unit = LANE_UNIT
    low_grads[...] = jnp.zeros(low_grads.shape, wide)
    small[...] = jnp.zeros(small.shape, wide)
    at_delta = low_rank + 2 * states
    at_log = at_delta + low_rank
    at_conv = at_log + states
    at_end = at_conv + taps + 2

    def first(j, carry):
        at = lane_unit(j)
        slope = grad_delta[:, at] * jax.nn.sigmoid(delta_pre_ref[:, at])
        small[at_conv + taps + 1 : at_conv + taps + 2, at] = jnp.sum(slope, axis=0, keepdims=True)
        small[at_delta:at_log, at] = rows_dot(delta_low_ref[...], slope, lax.Precision.HIGHEST)
        low_grads[...] += two_part(slope, delta_proj_ref[:, at], ((1,), (1,)))
        return carry

    lax.fori_loop(0, inner_width // unit, first, 0)
    for i in pair:
        sums.planes_gathered(i, blocks[i])
        sums.gather_second_start(i, results[i])
    column = lax.broadcasted_iota(jnp.int32, grad_in.shape, 1) // states
    row = lax.rem(lax.broadcasted_iota(jnp.int32, grad_in.shape, 0), BLK)
    fold = jnp.where(
        lax.rem(lax.broadcasted_iota(jnp.int32, (grad_in.shape[1], states), 0), states)
        == lax.broadcasted_iota(jnp.int32, (grad_in.shape[1], states), 1),
        1.0,
        0.0,
    ).astype(half)

    def folded(ref):
        return two_part(jnp.where(column == row, ref[...], 0.0), fold, ((1,), (0,)))

    coefs = jnp.concatenate([low_grads[...], folded(grad_in), folded(grad_out)], axis=1)
    keep = jnp.where(place > 0, 1.0, 0.0)
    rim_out[...] = jnp.zeros(rim_out.shape, half)

    def dense(at):
        small[:at_delta, at] = rows_dot(coefs, conv_ref[:, at], lax.Precision.HIGHEST)
        through = two_part(coefs, state_proj_ref[:, at], ((1,), (0,)))
        through = through + grad_scan_ref[:, at] * skip_ref[:, at] + grad_conv[:, at]
        pre = conv_pre_ref[:, at]
        sigma = jax.nn.sigmoid(pre)
        through = through * (sigma * (1.0 + pre * (1.0 - sigma)))
        small[at_conv + taps : at_conv + taps + 1, at] = jnp.sum(through, axis=0, keepdims=True)
        for q in range(sequences):
            padded[q, :8] = jnp.zeros((8, unit), wide)
            padded[q, 8 + piece :] = jnp.zeros((8, unit), wide)
            padded[q, 8 : 8 + piece] = through[q * piece : (q + 1) * piece]
            result = jnp.zeros((piece, unit), wide)
            rim = jnp.zeros((8, unit), wide)
            for tap in range(taps):
                weight = conv_weight_ref[tap : tap + 1, at]
                shift = taps - 1 - tap
                result = result + weight * padded[q, 8 + shift : 8 + shift + piece]
                rim = rim + weight * padded[q, 8 - tap : 16 - tap]
            slopes[q * piece : (q + 1) * piece, at] = result.astype(half)
            rim_out[q, 8 - (taps - 1) :, at] = (rim[: taps - 1] * keep).astype(half)
            slopes[tokens + q * 8 : tokens + (q + 1) * 8, at] = rim_out[q, :, at]
        for tap in range(taps):
            start = 8 - (taps - 1) + tap
            product = jnp.zeros((1, unit), wide)
            for q in range(sequences):
                product = product + jnp.sum(
                    padded[q, 8 : 8 + piece] * extended_ref[q, start : start + piece, at],
                    axis=0,
                    keepdims=True,
                )
            small[at_conv + tap : at_conv + tap + 1, at] = product

    slabs = given_inner.shape[0]
    tall = width // chips
    size = tall // planes

    def tail_of(s):
        return [buffer.at[s] for buffer in tail_buffers]

    def after_tail_pair(s):
        sums.after_pair(2 + s, given_inner.at[s], *tail_of(s)[:2])

    def slab(s, carry):
        for c in range(2):
            at = lane_unit(c * slabs + s)
            dense(at)
            for m in range(chips):
                product = rows_dot(
                    normed_ref[:, m * tall : (m + 1) * tall], slopes[:, at]
                ).astype(half)
                for z in range(planes):
                    part = product[z * size : (z + 1) * size]
                    given_inner[s, c, m // side, m % side, z] = part
        sums.pair_half(2 + s, given_inner.at[s], tail_buffers[0].at[s]).start()

        @pl.when(s > 0)
        def _():
            after_tail_pair(s - 1)

        return carry

    lax.fori_loop(0, slabs, slab, 0)
    after_tail_pair(slabs - 1)
    rim_copy = pltpu.make_async_remote_copy(
        src_ref=rim_out,
        dst_ref=rim_in,
        send_sem=rim_sent,
        recv_sem=rim_landed,
        device_id=chain_device(before, 2 * chips),
        device_id_type=MESH,
    )
    rim_copy.start()
    sums.gather_across(0, results[0])
    in_load.wait()
    projected = cols_dot(slopes[...], in_part[...])
    normed_grad = normed_gate_ref[...] + projected[:tokens]

    def normal_of(values):
        scaling = lax.rsqrt(jnp.mean(values * values, axis=-1, keepdims=True) + EPSILON)
        return values * scaling, scaling

    normal, scaling = normal_of(layer_ref[...].astype(wide))
    gain_grad = jnp.sum(normed_grad * normal, axis=0, keepdims=True)
    for q in range(sequences):
        rim_normal, _ = normal_of(rim_layer_ref[q].astype(wide))
        rim_grad = projected[tokens + q * 8 : tokens + (q + 1) * 8]
        gain_grad = gain_grad + jnp.sum(rim_grad * rim_normal, axis=0, keepdims=True)
    log_total = grad_log[0]
    for q in range(1, sequences):
        log_total = log_total + grad_log[q]
    small[at_log:at_conv] = log_total
    small[at_end : at_end + 1] = skip_grad_ref[...]
    small[at_end + 1 : at_end + 2, :width] = gain_grad
    small[at_end + 1 : at_end + 2, width:] = norm_grad_ref[...]
    for k in range(router_grad_ref.shape[0]):
        line = at_end + 2 + k // 2
        small[line : line + 1, (k % 2) * width : (k % 2 + 1) * width] = router_grad_ref[k : k + 1]
    low = given_small.shape[4]
    for c in range(2):
        for m in range(chips):
            for z in range(planes):
                line = (m * planes + z) * low
                given_small[c, m // side, m % side, z] = small[
                    line : line + low, c * width : (c + 1) * width
                ].astype(half)
    last = 2 + slabs
    every = range(slabs)
    sums.pair_half(last, given_small, small_buffers[0]).start()
    for s in every:
        sums.after_first(2 + s, *tail_of(s)[:4])
    sums.after_pair(last, given_small, *small_buffers[:2])
    sums.gather_across(1, results[1])
    weighted = normed_grad * mixer_gain_ref[...]
    in_grad_ref[...] = grad_resid_ref[...] + scaling * (
        weighted - normal * jnp.mean(weighted * normal, axis=-1, keepdims=True)
    )
    for s in every:
        sums.after_second(2 + s, *tail_of(s)[2:6])
    sums.after_first(last, *small_buffers[:4])
    tails = [total_inner_ref.at[s] for s in every] + [total_small_ref]
    tail_blocks = [total.at[sums.core, sums.first, sums.second] for total in tails]
    for s in every:
        sums.after_planes(2 + s, *tail_of(s)[4:6], tail_blocks[s])
    sums.after_second(last, *small_buffers[2:6])
    sums.gather_pass(0, results[0])
    for s in every:
        sums.planes_gathered(2 + s, tail_blocks[s])
        sums.gather_second_start(2 + s, tails[s])
    sums.after_planes(last, *small_buffers[4:6], tail_blocks[slabs])
    for s in every:
        sums.gather_across(2 + s, tails[s])
    sums.planes_gathered(last, tail_blocks[slabs])
    sums.gather_second_start(last, total_small_ref)
    sums.gather_pass(1, results[1])
    rim_copy.wait()
    keep_last = jnp.where(place < devices - 1, 1.0, 0.0)
    for q in range(sequences):
        rows = slice((q + 1) * piece - 8, (q + 1) * piece)
        added = cols_dot(rim_in[q], in_part[...]) * keep_last
        fixed = (normed_grad[rows] + added) * mixer_gain_ref[...]
        mean = jnp.mean(fixed * normal[rows], axis=-1, keepdims=True)
        in_grad_ref[rows, :] = grad_resid_ref[rows, :] + scaling[rows] * (
            fixed - normal[rows] * mean
        )
    sums.gather_across(last, total_small_ref)
    for s in every:
        sums.gather_pass(2 + s, tails[s])
    sums.gather_pass(last, total_small_ref)
    routes.wait(returned_ref, landed_ref, True)
    for swap in swaps:
        swap.wait()
    ends = [(i, stages[i], blocks[i], results[i]) for i in pair]
    ends += [(2 + s, tail_of(s), tail_blocks[s], tails[s]) for s in every]
    ends += [(last, small_buffers, tail_blocks[slabs], total_small_ref)]
    for i, buffers, block, result in ends:
        sums.scatter_sent(i, *buffers, block)
        sums.gather_end(i, result)


def all_gradients(operands, small_height, side):
    planes = lax.axis_size("seq")
    tokens, inner_width = operands[1].shape
    width = operands[15].shape[1]
    states, low_rank = operands[6].shape[0], operands[10].shape[1]
    sequences = operands[7].shape[0]
    piece = tokens // sequences
    low = -(-small_height // (side * side * planes))
    lead = (2, side, side, planes)
    big = operands[26].shape
    slabs = width // LANE_UNIT
    inner = (slabs,) + lead + (big[4], LANE_UNIT)
    little = lead + (low, width)
    vmem, anywhere = (pl.BlockSpec(memory_space=space) for space in (pltpu.VMEM, pl.ANY))
    half, wide = jnp.bfloat16, jnp.float32
    token_wide = pltpu.VMEM((tokens, inner_width), wide)
    narrow = pltpu.VMEM((tokens, BLK * states), wide)
    steps = pltpu.VMEM((piece, states, GROUP), wide)
    stack = pltpu.VMEM((BLK * states, GROUP), half)
    rim = pltpu.VMEM((sequences, 8, inner_width), half)
    tail_shapes = [value.shape for value in scatter_buffers([inner[5:]], planes, side)]
    moved = [jax.ShapeDtypeStruct(value.shape, half) for value in operands[28:]]
    semaphores = stage_semaphores(3 + slabs, planes, side)
    return pl.pallas_call(
        functools.partial(gradient_kernel, planes, side),
        name="backward_gradients",
        in_specs=[vmem] * 20 + [anywhere] + [vmem] * 7 + [anywhere] * 3,
        out_specs=[vmem] * 5 + [anywhere] * 3,
        out_shape=[jax.ShapeDtypeStruct((tokens, width), wide)]
        + [jax.ShapeDtypeStruct(shape, half) for shape in (big, big, inner, little)]
        + moved,
        scratch_shapes=[
            token_wide,
            token_wide,
            narrow,
            narrow,
            pltpu.VMEM((sequences, states, inner_width), wide),
            pltpu.VMEM((piece, GROUP), wide),
            steps,
            stack,
            stack,
            pltpu.VMEM((tokens, low_rank), wide),
            pltpu.VMEM((sequences, piece + 16, LANE_UNIT), wide),
            pltpu.VMEM((tokens + 8 * sequences, inner_width), half),
            pltpu.VMEM((low * side * side * planes, inner_width), wide),
            rim,
            rim,
            pltpu.SemaphoreType.DMA,
            pltpu.SemaphoreType.DMA,
            pltpu.VMEM((width, inner_width), half),
            pltpu.SemaphoreType.DMA,
            pltpu.VMEM(inner, half),
            pltpu.VMEM(little, half),
        ]
        + scatter_buffers([big[4:], big[4:]], planes, side)
        + [pltpu.VMEM((slabs,) + shape, half) for shape in tail_shapes]
        + scatter_buffers([little[4:]], planes, side)
        + [pltpu.SemaphoreType.DMA((2,)), pltpu.SemaphoreType.DMA((2,))]
        + semaphores
        + semaphores
        + route_semaphores(planes, 2 * side * side),
        compiler_params=pltpu.CompilerParams(
            collective_id=3, has_side_effects=True, vmem_limit_bytes=63 * 1024 * 1024
        ),
        cost_estimate=pl.CostEstimate(flops=10**8, transcendentals=0, bytes_accessed=2 * 10**8),
    )(*operands)


def on_device(
    layer_in,
    mixer_gain,
    in_proj,
    conv_weight,
    conv_bias,
    state_proj,
    delta_proj,
    delta_bias,
    decay_log,
    skip_gain,
    out_proj,
    expert_norm,
    router_weight,
    expert_up,
    expert_down,
    expert_ids,
    capacity_slot,
    out_grad,
):
    sequences, piece_len, width = layer_in.shape
    tokens = sequences * piece_len
    taps, inner_width = conv_weight.shape
    low_rank = delta_proj.shape[0]
    states = decay_log.shape[0]
    experts = router_weight.shape[1]
    senders = lax.axis_size("exp")
    capacity = (5 * tokens + 4 * experts - 1) // (4 * experts)
    planes = lax.axis_size("seq")
    hops = planes // 2
    flat_ids = expert_ids.reshape(1, tokens)
    flat_slot = capacity_slot.reshape(1, tokens)
    target = jnp.where(flat_slot < capacity, flat_ids * capacity + flat_slot, experts * capacity)
    slot_rows = jnp.arange(experts * capacity, dtype=jnp.int32)
    picks = (slot_rows[:, None] == target).astype(jnp.bfloat16)
    state_rows = sequences * states // senders
    first_row = lax.rem(lax.axis_index("exp") * state_rows, states)
    own_log = lax.dynamic_slice(decay_log, (first_row, 0), (state_rows, inner_width))
    norms = jnp.concatenate([mixer_gain, expert_norm])
    vectors = jnp.stack([conv_bias, delta_bias, skip_gain, norms])
    (
        normed_half,
        extended,
        gate_half,
        conv_pre,
        conv_flat,
        delta_pre,
        delta,
        delta_low,
        in_cols,
        out_cols,
        in_diag,
        delta_sum,
        carried,
        mixer_pre,
        mixed,
        resid,
        row_slots,
        grad_rows,
        near_up,
        near_half,
        rim_layer,
    ) = forward(
        [
            layer_in.reshape(tokens, width),
            out_grad.reshape(tokens, width),
            target,
            vectors,
            in_proj,
            conv_weight,
            state_proj.T,
            delta_proj,
            decay_log,
            own_log,
            out_proj,
            expert_up,
            expert_down,
        ],
        capacity,
        states,
        sequences,
        low_rank,
        experts,
    )
    gate_act = jax.nn.silu(gate_half)
    scaling_two = lax.rsqrt(jnp.mean(resid * resid, axis=-1, keepdims=True) + EPSILON)
    weights = [expert_up, expert_down, near_up, near_half]
    chosen = (
        jnp.arange(experts, dtype=jnp.int32) == lax.axis_index("exp")
    ).astype(jnp.float32)[None, :]
    expert_out, back_rows, grad_up, grad_down, far_up, far_down, grad_router = expert_apply(
        row_slots, grad_rows, weights, router_weight.T, chosen
    )
    grad_routed = rows_dot(
        jnp.concatenate([picks] * hops, axis=0), back_rows.reshape(hops * senders * capacity, width)
    )
    grad_top = out_grad.reshape(tokens, width).astype(jnp.float32)
    grad_resid_norm, grad_expert_norm = norm_backward(resid, scaling_two, expert_norm, grad_routed)
    grad_resid = grad_top + grad_resid_norm
    grad_mixer = grad_resid.astype(jnp.bfloat16)
    grad_out_proj = rows_dot(mixed, grad_mixer)
    grad_mixed = cols_dot(grad_mixer, out_proj)
    grad_scan = grad_mixed * gate_act
    grad_gate_half = grad_mixed * mixer_pre * silu_slope(gate_half)
    grad_gate_half = grad_gate_half.astype(jnp.bfloat16)
    grad_in_gate = rows_dot(normed_half[:tokens], grad_gate_half)
    grad_normed_gate = cols_dot(grad_gate_half, in_proj[:, inner_width:])
    grad_skip_gain = jnp.sum(grad_scan * conv_flat, axis=0, keepdims=True)
    (gradient_first,) = scan_call(
        back_summary_kernel,
        "back_summary",
        sequences,
        states,
        [("wide", delta), ("wide", grad_scan), ("cols", out_cols), ("rates", decay_log)],
        ["state"],
        [],
    )
    carried_back = exchange(gradient_first, delta_sum, own_log)
    side = math.isqrt(senders // 2)
    big = (2, side, side, planes, inner_width // (senders * planes), width)

    def as_rows(values):
        blocks = values.shape[1] // width
        return jnp.concatenate(
            [values[:, at * width : (at + 1) * width] for at in range(blocks)], axis=0
        ).astype(jnp.bfloat16)

    early = [
        grad_out_proj.astype(jnp.bfloat16).reshape(big),
        as_rows(grad_in_gate).reshape(big),
    ]
    heights = [low_rank + 2 * states, low_rank, states, taps, 1, 1, 1, 1, experts // 2]
    in_grad, sum_out, sum_gate, sum_inner, sum_small, back_out, near_up, near_down = all_gradients(
        [
            delta,
            conv_flat,
            grad_scan,
            in_cols,
            out_cols,
            in_diag,
            decay_log,
            carried,
            carried_back,
            delta_pre,
            delta_low,
            conv_pre,
            extended,
            normed_half,
            grad_normed_gate,
            layer_in.reshape(tokens, width),
            rim_layer,
            grad_resid,
            delta_proj,
            state_proj.T,
            in_proj,
            conv_weight,
            vectors,
            grad_skip_gain,
            grad_expert_norm,
            grad_router,
        ]
        + early
        + [expert_out, far_up, far_down],
        sum(heights),
        side,
    )
    grad_up_own = grad_up + near_up.astype(jnp.float32)
    grad_down_own = grad_down + near_down.astype(jnp.float32)
    token_out = rows_dot(
        jnp.concatenate([picks] * hops, axis=0), back_out.reshape(hops * senders * capacity, width)
    )
    layer_out = (resid + token_out).astype(jnp.bfloat16).reshape(sequences, piece_len, width)
    in_grad = in_grad.reshape(sequences, piece_len, width)
    rows_of = (inner_width, width)
    slabs = width // LANE_UNIT
    by_slab = sum_inner.reshape(slabs, 2, width, LANE_UNIT)
    inner_parts = [by_slab[s, c] for c in range(2) for s in range(slabs)]
    grad_in_proj = jnp.concatenate(
        inner_parts + [sum_gate[c].reshape(width, width) for c in range(2)], axis=1
    ).astype(jnp.float32)
    small_halves = sum_small.reshape(2, -1, width)
    small_wide = jnp.concatenate([small_halves[0], small_halves[1]], axis=1).astype(jnp.float32)
    offsets = [sum(heights[:at]) for at in range(len(heights) + 1)]
    pieces = [small_wide[offsets[at] : offsets[at + 1]] for at in range(len(heights))]
    summed = (
        pieces[7][0, :width],
        grad_in_proj,
        pieces[3],
        pieces[4][0],
        pieces[0].T,
        pieces[1],
        pieces[5][0],
        pieces[2],
        pieces[6][0],
        sum_out.reshape(rows_of).astype(jnp.float32),
        pieces[7][0, width:],
        pieces[8].reshape(experts, width).T,
    )
    return (
        layer_out,
        in_grad,
        summed[0],
        summed[1],
        summed[2],
        summed[3],
        summed[4],
        summed[5],
        summed[6],
        summed[7],
        summed[8],
        summed[9],
        summed[10],
        summed[11],
        grad_up_own,
        grad_down_own,
    )


def solution(mesh):
    placed = (
        P(None, ("seq", "exp"), None),
        P(),
        P(),
        P(),
        P(),
        P(),
        P(),
        P(),
        P(),
        P(),
        P(),
        P(),
        P(),
        P("exp", None, "seq"),
        P("exp", "seq", None),
        P(None, ("seq", "exp")),
        P(None, ("seq", "exp")),
        P(None, ("seq", "exp"), None),
    )
    return jax.shard_map(
        on_device,
        mesh=mesh,
        in_specs=placed,
        out_specs=(
            P(None, ("seq", "exp"), None),
            P(None, ("seq", "exp"), None),
            P(),
            P(),
            P(),
            P(),
            P(),
            P(),
            P(),
            P(),
            P(),
            P(),
            P(),
            P(),
            P("exp", None, "seq"),
            P("exp", "seq", None),
        ),
        check_vma=False,
    )
```

time: 441 us -> 340 us (0.77)
  local copies, waits for them, and re-layouts: 39.9 us -> 9.64 us
  Pallas kernels: 316 us -> 293 us
  waiting for transfers between devices: 17.1 us -> 0 us
  matrix products: 25 us -> 11.3 us
  starting transfers between devices: 13.2 us -> 0 us
    pallas_call x4 -> x1, Pallas kernels: 85.1 us -> 6.7 us  [scan_call(): pl.pallas_call(kernel, name=name, grid=(sequences, width // GROUP), in_sp...]
    pallas_call x6 -> x4, Pallas kernels: 231 us -> 286 us  [the longest x1 125 us: all_gradients(): pl.pallas_call(functools.partial(gradient_kernel, planes, side), name='ba...]
    unnamed x138 -> x64, local copies, waits for them, and re-layouts: 23.6 us -> 3.37 us
    ppermute x4 -> x0, waiting for transfers between devices: 17.1 us -> none  [the longest x1 17.1 us: along_planes(): return lax.ppermute(values, 'seq', pairs)]
    dot_general x6 -> x0, matrix products: 13.3 us -> none  [the longest x4 9.54 us: half_dot(): return jnp.dot(left, right, preferred_element_type=jnp.float32)]
    ppermute x4 -> x0, starting transfers between devices: 9.23 us -> none  [the longest x1 4.09 us: along_planes(): return lax.ppermute(values, 'seq', pairs)]
    concatenate x2 -> x1, other arithmetic: 7.24 us -> 0.71 us  [on_device(): norms = jnp.concatenate([mixer_gain, expert_norm])]
    broadcast_in_dim x7 -> x2, local copies, waits for them, and re-layouts: 6.25 us -> 1.22 us  [the longest x1 0.64 us: on_device(): grad_skip_gain = jnp.sum(grad_scan * conv_flat, axis=0, keepdims=True)]
  transfers between devices with their start and end apart: 5 -> 0, of which waited for: 1 -> 0; matrix products, arithmetic and copies ran while one was open for 7% -> 0% of each run, Pallas kernels for 18% -> 0%
where the time goes in v3:
time: 340 us; the launch traced here: 337 us
  Pallas kernels  293 us (86%)
  other arithmetic  22.3 us (7%)
  matrix products  11.3 us (3%)
  local copies, waits for them, and re-layouts  9.64 us (3%)
    pallas_call x1, Pallas kernels, all_gradients(): pl.pallas_call(functools.partial(gradient_kernel, planes, side), name='ba...  125 us
    pallas_call x1, Pallas kernels, forward(): pl.pallas_call(functools.partial(forward_kernel, planes, members, capacit...  72.9 us
    pallas_call x1, Pallas kernels, expert_apply(): pl.pallas_call(functools.partial(expert_kernel, planes, members), name='e...  66.1 us
    pallas_call x1, Pallas kernels, exchange(): pl.pallas_call(functools.partial(exchange_kernel, True, planes, members),...  22.7 us

profile of v3, /device:TPU:11, one launch (start us, length us, event | category | flops | bytes accessed | tf_op | source)
XLA Modules:
  0.0 337.4 jit_solution(15994815175357194880)
XLA Ops:
  0.7 0.5 compare_convert_fusion.chosen_ref
  1.2 0.7 compare_select_fusion
  1.9 0.7 stack.15
  2.6 0.7 stack.16
  3.3 0.7 stack.17
  4.0 0.7 pad_maximum_fusion.2
  4.7 1.5 pad_maximum_fusion.1
  6.1 0.1 iota_compare_fusion
  6.2 0.0 copy-done.24
  6.2 72.9 %forward_to_experts.1 = (bf16[272,768]{1,0:T(8,128)(2,1)}, f32[2,136,1536]{2,1,0:T(8,128)}, f32[256,1536]{1,0:T(8,128)}, f32[256,1536]{1,0:T(8,128)}, f32[256,15...) custom-call(bf16[256,768]{1,0:T(8,128)(2,1)} %bitcast.65, ...), custom_call_target="tpu_custom_call" | custom-call | flops 100000000 | bytes 200000000 | tf_op jit(solution)/shard_map/forward_to_experts/pallas_call | solution.py:1039
  79.1 1.3 multiply_reduce_fusion.3
  80.4 0.0 copy-start.8
  80.4 0.0 copy-start.23
  80.4 0.0 copy-start.25
  80.4 66.1 %expert_apply.1 = (bf16[2,8,40,768]{3,2,1,0:T(8,128)(2,1)}, bf16[2,8,40,768]{3,2,1,0:T(8,128)(2,1)}, f32[1,768,768]{2,1,0:T(8,128)}, f32[1,768,768]{2,1,0:T(8,12...) custom-call(bf16[8,40,768]{2,1,0:T(8,128)(2,1)} %get-tuple-element.55.row_slots_ref, ...), custom_call_target="tpu_custom_call" | custom-call | flops 9059696640 | bytes 30000000 | tf_op jit(solution)/shard_map/expert_apply/pallas_call | solution.py:1294
  146.5 0.0 copy-start.16
  146.6 0.0 copy-start.13
  146.6 2.0 multiply_reduce_fusion.1
  148.6 0.6 broadcast_in_dim.17.norm_grad_ref
  149.2 0.0 copy-done.16
  149.2 0.3 multiply_add_fusion.grad_resid_ref
  149.5 0.0 copy-start.7
  149.5 0.0 copy-start.3
  149.6 0.0 copy-start.5
  149.6 0.0 slice-start.1
  149.6 3.2 multiply_reduce_fusion
  152.8 0.0 copy-start.1
  152.8 0.6 broadcast_in_dim.16.skip_grad_ref
  153.5 0.0 copy-done.3
  153.5 6.7 %back_summary.1.refs_0_ = f32[2,16,1536]{2,1,0:T(8,128)S(1)} custom-call(f32[256,1536]{1,0:T(8,128)S(1)} %copy-done, f32[256,1536]{1,0:T(8,128)S(1)} %get-tuple-element.96.grad_ref.grad_scan_ref, f32[16,16,16]{2,1,0:T(8,128)S(1)} %copy-done.5, f32[16,1536]{1,0:T(8,128)S(1)} %copy-done.3), custom_call_target="tpu_custom_call" | custom-call | flops 125829120 | bytes 6291456 | tf_op jit(solution)/shard_map/back_summary/pallas_call | solution.py:278
  160.2 22.7 %state_exchange_back.1.carried_back_ref = f32[2,16,1536]{2,1,0:T(8,128)S(1)} custom-call(f32[2,16,1536]{2,1,0:T(8,128)S(1)} %back_summary.1.refs_0_, f32[2,1536]{1,0:T(2,128)S(1)} %copy-done.6, f32[4,1536]{1,0:T(4,128)S(1)} %copy-done.4), custom_call_target="tpu_custom_call" | custom-call | flops 1000000 | bytes 20000000 | tf_op jit(solution)/shard_map/state_exchange_back/pallas_call | solution.py:453
  182.9 0.0 copy-start.2
  182.9 0.0 copy-start.15
  182.9 1.7 fusion.normed_gate_ref
  184.6 0.8 convolution_convert_fusion
  185.4 0.2 fusion.17
  185.6 1.6 pad_maximum_fusion
  187.2 0.0 copy-done.7
  187.2 2.2 convolution_convert_fusion.1
  189.4 124.7 %backward_gradients.1 = (f32[256,768]{1,0:T(8,128)}, bf16[2,2,2,4,48,768]{5,4,3,2,1,0:T(8,128)(2,1)}, bf16[2,2,2,4,48,768]{5,4,3,2,1,0:T(8,128)(2,1)}, bf16[3,2,...) custom-call(f32[256,1536]{1,0:T(8,128)} %get-tuple-element.53.delta_, ...), custom_call_target="tpu_custom_call" | custom-call | flops 100000000 | bytes 200000000 | tf_op jit(solution)/shard_map/backward_gradients/pallas_call | solution.py:1722
  314.1 3.8 %convert_add_fusion = f32[1,768,768]{2,1,0:T(8,128)} fusion(f32[1,768,768]{2,1,0:T(8,128)} %get-tuple-element.86, bf16[1,768,768]{2,1,0:T(8,128)(2,1)} %get-tuple-element.87), kind=kLoop, calls=%fused_computation.4 | loop fusion | flops 1179648 | bytes 5898240 | tf_op jit(solution)/shard_map/add | solution.py:1934
  317.9 1.6 convert_add_fusion.1
  319.6 0.0 copy-done.9
  319.6 0.5 copy-done.19
  320.0 1.3 fusion.2
  321.3 0.0 copy-done.21
  321.4 0.1 fusion.18
  321.4 0.1 squeeze.39
  321.5 0.1 squeeze.40
  321.6 0.6 convert_reduce_fusion.3
  322.2 0.7 convert_reduce_fusion
  322.9 0.6 maximum_convert_fusion.2
  323.5 0.6 reshape.162
  324.1 0.6 maximum_convert_fusion.1
  324.8 0.1 maximum_convert_fusion
  324.9 0.7 slice.112
  325.6 0.8 slice_bitcast_fusion
  326.4 0.2 fusion.16
  326.7 1.4 copy-done.11
  328.4 0.2 constant_dynamic-update-slice_fusion.1
  328.6 0.2 constant_dynamic-update-slice_fusion
  328.8 5.0 %convert_element_type.57 = f32[768,3072]{1,0:T(8,128)} convert(bf16[768,3072]{1,0:T(8,128)(2,1)S(1)} %constant_dynamic-update-slice_fusion) | non-fusion elementwise | flops 2359296 | bytes 14155776 | tf_op jit(solution)/shard_map/convert_element_type | solution.py:1946
  333.8 2.7 bitcast_convert_fusion
  336.5 0.9 copy.45
  (46 shorter events, 0.4 us)
Async XLA Ops:
  1.9 4.3 %copy-start.24 = (s32[2,128]{1,0:T(2,128)}, s32[2,128]{1,0:T(2,128)S(1)}, u32[]{:S(2)}) copy-start(s32[2,128]{1,0:T(2,128)S(1)} %compare_select_fusion) | copy-start | bytes 3076
  80.4 66.2 %copy-start.8 = (f32[256,768]{1,0:T(8,128)S(1)}, f32[256,768]{1,0:T(8,128)}, u32[]{:S(2)}) copy-start(f32[256,768]{1,0:T(8,128)} %get-tuple-element.52) | copy-start | bytes 2359300
  80.4 66.2 %copy-start.23 = (f32[768]{0:T(1024)S(1)}, f32[768]{0:T(1024)}, u32[]{:S(2)}) copy-start(f32[768]{0:T(1024)} %param.29) | copy-start | bytes 9220
  80.4 69.1 %copy-start.25 = (f32[256,1536]{1,0:T(8,128)S(1)}, f32[256,1536]{1,0:T(8,128)}, u32[]{:S(2)}) copy-start(f32[256,1536]{1,0:T(8,128)} %get-tuple-element.60) | copy-start | bytes 4718596
  146.5 2.7 copy-start.16
  146.6 2.9 copy-start.13
  146.6 2.9 copy-start.17
  149.2 33.7 %slice-start = ((s8[4718592]{0:T(1024)(128)(4,1)}), s8[4194304]{0:T(1024)(128)(4,1)S(1)}, s32[]{:S(2)}) async-start(s8[4718592]{0:T(1024)(128)(4,1)} %bitcast.52), calls=%async_computation | async-start | bytes 8388608
  149.5 37.6 %copy-start.7 = (f32[256,768]{1,0:T(8,128)}, f32[256,768]{1,0:T(8,128)S(1)}, u32[]{:S(2)}) copy-start(f32[256,768]{1,0:T(8,128)S(1)} %multiply_add_fusion.grad_resid_ref) | copy-start | bytes 2359300
  149.5 3.9 %copy-start = (f32[256,1536]{1,0:T(8,128)S(1)}, f32[256,1536]{1,0:T(8,128)}, u32[]{:S(2)}) copy-start(f32[256,1536]{1,0:T(8,128)} %get-tuple-element.53.delta_ref) | copy-start | bytes 4718596
  149.5 3.9 %copy-start.3 = (f32[16,1536]{1,0:T(8,128)S(1)}, f32[16,1536]{1,0:T(8,128)}, u32[]{:S(2)}) copy-start(f32[16,1536]{1,0:T(8,128)} %decay_log_ref.3) | copy-start | bytes 294916
  149.6 3.9 %copy-start.5 = (f32[16,16,16]{2,1,0:T(8,128)S(1)}, f32[16,16,16]{2,1,0:T(8,128)}, u32[]{:S(2)}) copy-start(f32[16,16,16]{2,1,0:T(8,128)} %get-tuple-element.62.out_ref.out_cols_ref) | copy-start | bytes 49156
  149.6 33.3 %slice-start.1 = ((s8[4718592]{0:T(1024)(128)(4,1)}), s8[524288]{0:T(1024)(128)(4,1)S(1)}, s32[]{:S(2)}) async-start(s8[4718592]{0:T(1024)(128)(4,1)} %bitcast.52), calls=%async_computation.1 | async-start | bytes 1048576
  152.8 7.4 %copy-start.1 = (f32[256,1536]{1,0:T(8,128)}, f32[256,1536]{1,0:T(8,128)S(1)}, u32[]{:S(2)}) copy-start(f32[256,1536]{1,0:T(8,128)S(1)} %get-tuple-element.96.grad_ref.grad_scan_ref) | copy-start | bytes 4718596
  153.5 6.7 %copy-start.4 = (f32[4,1536]{1,0:T(4,128)S(1)}, f32[4,1536]{1,0:T(4,128)}, u32[]{:S(2)}) copy-start(f32[4,1536]{1,0:T(4,128)} %get-tuple-element.108.own_log_ref.refs_2_) | copy-start | bytes 73732
  153.5 6.7 %copy-start.6 = (f32[2,1536]{1,0:T(2,128)S(1)}, f32[2,1536]{1,0:T(2,128)}, u32[]{:S(2)}) copy-start(f32[2,1536]{1,0:T(2,128)} %get-tuple-element.65.refs_1_) | copy-start | bytes 36868
  182.9 1.7 copy-start.2
  182.9 1.7 copy-start.15
  185.6 1.6 copy-start.22
  314.1 3.8 %copy-start.14 = (f32[1,768,768]{2,1,0:T(8,128)S(1)}, f32[1,768,768]{2,1,0:T(8,128)}, u32[]{:S(2)}) copy-start(f32[1,768,768]{2,1,0:T(8,128)} %get-tuple-element.84) | copy-start | bytes 7077892
  314.1 3.8 %copy-start.18 = (bf16[1,768,768]{2,1,0:T(8,128)(2,1)S(1)}, bf16[1,768,768]{2,1,0:T(8,128)(2,1)}, u32[]{:S(2)}) copy-start(bf16[1,768,768]{2,1,0:T(8,128)(2,1)} %get-tuple-element.85) | copy-start | bytes 3538948
  317.9 1.6 copy-start.9
  317.9 2.1 copy-start.19
  319.6 1.8 copy-start.21
  322.2 4.2 %copy-start.12 = (bf16[2,2,2,4,48,768]{5,4,3,2,1,0:T(8,128)(2,1)S(1)}, bf16[2,2,2,4,48,768]{5,4,3,2,1,0:T(8,128)(2,1)}, u32[]{:S(2)}) copy-start(bf16[2,2,2,4,48,768]{5,4,3,2,1,0:T(8,128)(2,1)} %get-tuple-element.82) | copy-start | bytes 7077892
  326.4 1.7 copy-start.11
  328.8 5.1 %copy-start.10 = (bf16[2,2,2,4,48,768]{5,4,3,2,1,0:T(8,128)(2,1)S(1)}, bf16[2,2,2,4,48,768]{5,4,3,2,1,0:T(8,128)(2,1)}, u32[]{:S(2)}) copy-start(bf16[2,2,2,4,48,768]{5,4,3,2,1,0:T(8,128)(2,1)} %get-tuple-element.83) | copy-start | bytes 7077892
  333.8 2.7 copy-start.20

commit v4 on v3

--- a/solution.py
+++ b/solution.py
@@ -68,6 +68,11 @@
 
 def block_of(ref, i):
     return ref.at[pl.ds(pl.multiple_of(i * BLK, BLK), BLK), :]
+
+
+def rows_of_block(ref, i, states):
+    size = BLK * states
+    return ref.at[pl.ds(pl.multiple_of(i * size, size), size), :]
 
 
 def rates_of(log_ref):
@@ -109,23 +114,24 @@
     def block(i, state):
         state = list(state)
         inwards = in_ref[i]
+        kept = rows_of_block(stack, i, states)
         for k in range(BLK):
             inward = jnp.broadcast_to(inwards[:, k : k + 1], (states, LANES))
             deltas = lane_parts(block_of(delta_ref, i), k, states)
             drives = lane_parts(block_of(drive, i), k, states)
             for j in range(width // LANES):
                 state[j] = jnp.exp2(deltas[j] * rates[j]) * state[j] + inward * drives[j]
-                stack[k * states : (k + 1) * states, j * LANES : (j + 1) * LANES] = state[j].astype(
-                    jnp.bfloat16
-                )
-        rows = pl.ds(pl.multiple_of(i * BLK, BLK), BLK)
-        both = jnp.concatenate([out_ref[rows, :], rest_ref[rows, :]], axis=0)
-        product = jnp.dot(both, stack[...], preferred_element_type=jnp.float32)
-        scanned_ref[rows, :] = product[:BLK] + product[BLK:]
+                at = slice(j * LANES, (j + 1) * LANES)
+                kept[k * states : (k + 1) * states, at] = state[j].astype(jnp.bfloat16)
         return tuple(state)
 
     begin = tuple(start_ref[0, :, j * LANES : (j + 1) * LANES] for j in range(width // LANES))
     lax.fori_loop(0, steps // BLK, block, begin)
+    for i in range(steps // BLK):
+        rows = slice(i * BLK, (i + 1) * BLK)
+        both = jnp.concatenate([out_ref[rows, :], rest_ref[rows, :]], axis=0)
+        product = half_dot(both, stack[i * BLK * states : (i + 1) * BLK * states, :])
+        scanned_ref[rows, :] = product[:BLK] + product[BLK:]
 
 
 def back_summary_kernel(delta_ref, grad_ref, out_ref, log_ref, end_ref):
@@ -323,6 +329,8 @@
 
 
 def exchange_body(
+    after_first,
+    after_second,
     reverse,
     planes,
     members,
@@ -361,6 +369,7 @@
             "exp",
             other,
         ).start()
+    after_first()
     landed[member] = packed[member]
     for k in range(1, members):
         other = lax.rem(member + k, members)
@@ -390,6 +399,7 @@
     for k in range(1, planes):
         other = lax.rem(plane + k, planes)
         remote(summary, totals.at[other], send_two.at[k], recv_two.at[other], "seq", other).wait()
+    after_second()
     state = jnp.zeros((rows, width), jnp.float32)
     for s in plane_order:
         reached = plane < s if reverse else plane > s
@@ -425,7 +435,7 @@
 
 def exchange_kernel(reverse, planes, members, *refs):
     greet((("seq", planes), ("exp", members)))
-    exchange_body(reverse, planes, members, *refs)
+    exchange_body(lambda: None, lambda: None, reverse, planes, members, *refs)
 
 
 def exchange_scratch(planes, members, rows, width):
@@ -666,7 +676,7 @@
         self.hops = planes // 2
         self.sends, self.arrivals, self.local = sends, arrivals, local
         self.pairs = [
-            (hop, k) for hop in reversed(range(self.hops)) for k in range(members) if hop or k
+            (hop, k) for hop in range(self.hops) for k in range(members) if hop or k
         ]
 
     def device(self, hop, k):
@@ -686,31 +696,29 @@
         device = self.device(hop, k)
         other = device["exp"]
         slot = hop if arriving else (-hop) % self.hops
-        sender = other if arriving else self.member
+        if returning:
+            index = other if arriving else self.member
+            src = given.at[hop, (self.members - k) % self.members]
+        else:
+            index, src = k, given.at[other]
         return pltpu.make_async_remote_copy(
-            src_ref=given.at[hop, other] if returning else given.at[other],
-            dst_ref=landed.at[slot, sender],
+            src_ref=src,
+            dst_ref=landed.at[slot, index],
             send_sem=self.sends.at[hop, k],
-            recv_sem=self.arrivals.at[slot, sender],
+            recv_sem=self.arrivals.at[slot, index],
             device_id=device,
             device_id_type=MESH,
         )
 
     def own(self, given, landed, returning):
-        src = given.at[0, self.member] if returning else given.at[self.member]
-        return pltpu.make_async_copy(src, landed.at[0, self.member], self.local)
+        src = given.at[0, 0] if returning else given.at[self.member]
+        index = self.member if returning else 0
+        return pltpu.make_async_copy(src, landed.at[0, index], self.local)
 
     def start(self, given, landed, returning):
         for hop, k in self.pairs:
             self.moved(given, landed, returning, hop, k, False).start()
         self.own(given, landed, returning).start()
-
-    def wait_group(self, given, landed, hop):
-        for at, k in self.pairs:
-            if at == hop:
-                self.moved(given, landed, False, hop, k, True).wait_recv()
-        if hop == 0:
-            self.own(given, landed, False).wait()
 
     def wait_sent(self, given, landed):
         for hop, k in self.pairs:
@@ -852,8 +860,24 @@
         device_id_type=MESH,
     )
     rim_copy.start()
-    up_swap = swapped(up_ref, near_up_ref, up_sent_ref, up_landed_ref)
-    up_swap.start()
+    up_rows = up_ref.shape[1]
+    marks = (0, up_rows // 2, up_rows * 11 // 16, up_rows)
+    up_swaps = []
+    for i, (low, high) in enumerate(zip(marks, marks[1:])):
+        at = pl.ds(low, high - low)
+        ends = (up_ref.at[:, at], near_up_ref.at[:, at])
+        up_swaps.append(swapped(*ends, up_sent_ref.at[i], up_landed_ref.at[i]))
+    slot = lax.broadcasted_iota(jnp.int32, (experts * capacity, tokens), 0)
+    picks = jnp.where(slot == target_ref[...], 1.0, 0.0).astype(half)
+
+    def fill(slots, values):
+        product = half_dot(picks, values).astype(half)
+        for e in range(experts):
+            slots[e] = product[e * capacity : (e + 1) * capacity]
+
+    fill(grad_slots_ref, out_grad_ref[...])
+    grad_routes.start(grad_slots_ref, grad_rows_ref, False)
+    up_swaps[0].start()
     cut = down_ref.shape[1] // 2
     down_swap = swapped(down_ref.at[:, pl.ds(0, cut)], near_half_ref, down_sent_ref, down_landed_ref)
 
@@ -960,21 +984,23 @@
         return carry
 
     lax.fori_loop(0, sequences * groups, first, 0)
+
+    def between_planes():
+        up_swaps[2].start()
+        down_swap.start()
+
     exchange_body(
-        False, planes, members, local_end_ref, delta_sum_ref, own_log_ref, carried_ref, *exchange_refs
+        up_swaps[1].start,
+        between_planes,
+        False,
+        planes,
+        members,
+        local_end_ref,
+        delta_sum_ref,
+        own_log_ref,
+        carried_ref,
+        *exchange_refs,
     )
-    up_swap.wait()
-    slot = lax.broadcasted_iota(jnp.int32, (experts * capacity, tokens), 0)
-    picks = jnp.where(slot == target_ref[...], 1.0, 0.0).astype(half)
-
-    def fill(slots, values):
-        product = half_dot(picks, values).astype(half)
-        for e in range(experts):
-            slots[e] = product[e * capacity : (e + 1) * capacity]
-
-    fill(grad_slots_ref, out_grad_ref[...])
-    grad_routes.start(grad_slots_ref, grad_rows_ref, False)
-    down_swap.start()
 
     def second(i, carry):
         q, rows, lanes, cols = views(i)
@@ -1007,6 +1033,8 @@
     fill(row_slots_ref, normalized(resid_ref[...], expert_norm_ref[...]).astype(half))
     grad_routes.wait(grad_slots_ref, grad_rows_ref, False)
     down_swap.wait()
+    for swap in up_swaps:
+        swap.wait()
 
 
 def forward(operands, capacity, states, sequences, low_rank, experts):
@@ -1025,7 +1053,7 @@
     scratch = [
         pltpu.VMEM((experts, capacity, width), half),
         pltpu.VMEM((piece, GROUP), wide),
-        pltpu.VMEM((BLK * states, GROUP), half),
+        pltpu.VMEM((piece * states, GROUP), half),
         pltpu.VMEM((tokens, low_rank + 2 * states), wide),
         pltpu.VMEM((2 * states, tokens), wide),
         pltpu.VMEM(diag, half),
@@ -1033,7 +1061,8 @@
         pltpu.VMEM(state, wide),
         pltpu.VMEM((sequences, 8, width), half),
     ]
-    scratch += [pltpu.SemaphoreType.DMA] * 6
+    scratch += [pltpu.SemaphoreType.DMA] * 2 + [pltpu.SemaphoreType.DMA((3,))] * 2
+    scratch += [pltpu.SemaphoreType.DMA] * 2
     scratch += exchange_scratch(planes, members, sequences * states // members, inner_width)
     scratch += route_semaphores(planes, members)
     return pl.pallas_call(
@@ -1136,10 +1165,19 @@
                 hop, e
             ]
 
-    def gather(hop):
-        routes.wait_group(row_slots_ref, landed_ref, hop)
-        for e in range(members):
-            rows_ref[hop * group + e * capacity : hop * group + (e + 1) * capacity] = landed_ref[hop, e]
+    def gather(hop, c):
+        rows = rows_ref.at[place(hop, c), :]
+        for k in range(batch):
+            r = c * batch + k
+            if hop:
+                routes.moved(row_slots_ref, landed_ref, False, hop, r, True).wait_recv()
+            else:
+
+                @pl.when(r > 0)
+                def _():
+                    routes.moved(row_slots_ref, landed_ref, False, 0, r, True).wait_recv()
+
+            rows[k * capacity : (k + 1) * capacity, :] = landed_ref[hop, r]
 
     def through(at, up, down, hidden, back, where):
         pre = half_dot(rows_ref[at, :], up)
@@ -1203,28 +1241,29 @@
             outs_ref[hop, c * batch + k] = outs[part]
             returns_ref[hop, c * batch + k] = row[part]
 
-    def returned(hop, e, arriving):
+    def returned(hop, r, arriving):
+        other = lax.rem(member + members - r, members)
         slot = hop if arriving else (-hop) % hops
-        sender = e if arriving else member
+        sender = other if arriving else member
         return pltpu.make_async_remote_copy(
-            src_ref=returns_ref.at[hop, e],
+            src_ref=returns_ref.at[hop, r],
             dst_ref=back_ref.at[slot, sender],
-            send_sem=back_sent_ref.at[hop, e],
+            send_sem=back_sent_ref.at[hop, r],
             recv_sem=back_landed_ref.at[slot, sender],
-            device_id={"seq": lax.rem(plane + 2 * hop, planes), "exp": e},
+            device_id={"seq": lax.rem(plane + 2 * hop, planes), "exp": other},
             device_id_type=MESH,
         )
 
     def give_back(hop, c):
         for k in range(batch):
-            e = c * batch + k
+            r = c * batch + k
             if hop:
-                returned(hop, e, False).start()
+                returned(hop, r, False).start()
             else:
 
-                @pl.when(e != member)
+                @pl.when(r > 0)
                 def _():
-                    returned(0, e, False).start()
+                    returned(0, r, False).start()
 
     def loop(body):
         def run(c, carry):
@@ -1248,35 +1287,44 @@
             else:
                 total[...] = rows_dot(left, right)
 
-    gather(0)
-    loop(functools.partial(own_part, 0))
-    down_swap.wait()
+    routes.own(row_slots_ref, landed_ref, False).wait()
+
+    def near_start(c):
+        gather(0, c)
+        own_part(0, c)
+
+    loop(near_start)
+    for hop in range(1, hops):
+
+        def far_end(c):
+            gather(hop, c)
+            own_part(hop, c)
+            if hop == 1:
+
+                @pl.when(c == 0)
+                def _():
+                    down_swap.wait()
+
+            late_part(hop, c)
+            give_back(hop, c)
+
+        loop(far_end)
 
     def near_end(c):
         late_part(0, c)
         give_back(0, c)
 
     loop(near_end)
-    weight_grads(0)
-    for hop in range(1, hops):
-        gather(hop)
-
-        def far_end(c):
-            own_part(hop, c)
-            late_part(hop, c)
-            give_back(hop, c)
-
-        loop(far_end)
+    for hop in range(hops):
         weight_grads(hop)
     far_up_ref[0] = far_up_sum_ref[...].astype(half)
     far_down_ref[0] = far_down_sum_ref[...].astype(half)
-    back_ref[0, member] = returns_ref[0, member]
+    back_ref[0, member] = returns_ref[0, 0]
     for hop in range(hops):
-        for k in range(members):
-            if hop or k:
-                e = lax.rem(member + k, members)
-                returned(hop, e, True).wait_recv()
-                returned(hop, e, False).wait_send()
+        for r in range(members):
+            if hop or r:
+                returned(hop, r, True).wait_recv()
+                returned(hop, r, False).wait_send()
     routes.wait_sent(row_slots_ref, landed_ref)
 
 

time: 340 us -> 324 us (0.953)
  Pallas kernels: 293 us -> 278 us
    pallas_call x1, Pallas kernels: 66.1 us -> 58.8 us  [expert_apply(): pl.pallas_call(functools.partial(expert_kernel, planes, members), name='e...]
    pallas_call x1, Pallas kernels: 72.9 us -> 67.1 us  [forward(): pl.pallas_call(functools.partial(forward_kernel, planes, members, capacit...]
where the time goes in v4:
time: 324 us; the launch traced here: 322 us
  Pallas kernels  278 us (86%)
  other arithmetic  22.3 us (7%)
  matrix products  11.3 us (3%)
  local copies, waits for them, and re-layouts  9.64 us (3%)
    pallas_call x1, Pallas kernels, all_gradients(): pl.pallas_call(functools.partial(gradient_kernel, planes, side), name='ba...  126 us
    pallas_call x1, Pallas kernels, forward(): pl.pallas_call(functools.partial(forward_kernel, planes, members, capacit...  67.1 us
    pallas_call x1, Pallas kernels, expert_apply(): pl.pallas_call(functools.partial(expert_kernel, planes, members), name='e...  58.8 us
    pallas_call x1, Pallas kernels, exchange(): pl.pallas_call(functools.partial(exchange_kernel, True, planes, members),...  19.7 us
    pallas_call x1, Pallas kernels, scan_call(): pl.pallas_call(kernel, name=name, grid=(sequences, width // GROUP), in_sp...  6.7 us

profile of v4, /device:TPU:11, one launch (start us, length us, event | category | flops | bytes accessed | tf_op | source)
XLA Modules:
  0.0 322.5 jit_solution(12226144816957978424)
XLA Ops:
  0.7 0.5 compare_convert_fusion.chosen_ref
  1.2 0.7 compare_select_fusion
  1.9 0.7 stack.15
  2.6 0.7 stack.16
  3.3 0.7 stack.17
  4.0 0.7 pad_maximum_fusion.2
  4.7 1.5 pad_maximum_fusion.1
  6.1 0.1 iota_compare_fusion
  6.2 0.0 copy-done.24
  6.2 67.1 %forward_to_experts.1 = (bf16[272,768]{1,0:T(8,128)(2,1)}, f32[2,136,1536]{2,1,0:T(8,128)}, f32[256,1536]{1,0:T(8,128)}, f32[256,1536]{1,0:T(8,128)}, f32[256,15...) custom-call(bf16[256,768]{1,0:T(8,128)(2,1)} %bitcast.65, ...), custom_call_target="tpu_custom_call" | custom-call | flops 100000000 | bytes 200000000 | tf_op jit(solution)/shard_map/forward_to_experts/pallas_call | solution.py:1068
  73.3 1.3 multiply_reduce_fusion.3
  74.6 0.0 copy-start.8
  74.6 0.0 copy-start.23
  74.6 58.8 %expert_apply.1 = (bf16[2,8,40,768]{3,2,1,0:T(8,128)(2,1)}, bf16[2,8,40,768]{3,2,1,0:T(8,128)(2,1)}, f32[1,768,768]{2,1,0:T(8,128)}, f32[1,768,768]{2,1,0:T(8,12...) custom-call(bf16[8,40,768]{2,1,0:T(8,128)(2,1)} %get-tuple-element.55.row_slots_ref, ...), custom_call_target="tpu_custom_call" | custom-call | flops 9059696640 | bytes 30000000 | tf_op jit(solution)/shard_map/expert_apply/pallas_call | solution.py:1342
  133.4 0.0 copy-start.16
  133.4 0.0 copy-done.8
  133.4 0.0 copy-done.23
  133.4 0.0 copy-start.13
  133.5 2.0 multiply_reduce_fusion.1
  135.5 0.6 broadcast_in_dim.17.norm_grad_ref
  136.1 0.3 multiply_add_fusion.grad_resid_ref
  136.4 0.0 copy-done.25
  136.4 0.0 copy-done.13
  136.4 0.0 copy-done.17
  136.4 0.0 copy-start.7
  136.4 0.0 copy-start.3
  136.4 0.0 slice-start.1
  136.4 3.2 multiply_reduce_fusion
  139.7 0.0 copy-start.1
  139.7 0.6 broadcast_in_dim.16.skip_grad_ref
  140.3 0.0 copy-done
  140.3 6.7 %back_summary.1.refs_0_ = f32[2,16,1536]{2,1,0:T(8,128)S(1)} custom-call(f32[256,1536]{1,0:T(8,128)S(1)} %copy-done, f32[256,1536]{1,0:T(8,128)S(1)} %get-tuple-element.96.grad_ref.grad_scan_ref, f32[16,16,16]{2,1,0:T(8,128)S(1)} %copy-done.5, f32[16,1536]{1,0:T(8,128)S(1)} %copy-done.3), custom_call_target="tpu_custom_call" | custom-call | flops 125829120 | bytes 6291456 | tf_op jit(solution)/shard_map/back_summary/pallas_call | solution.py:284
  147.1 19.7 %state_exchange_back.1.carried_back_ref = f32[2,16,1536]{2,1,0:T(8,128)S(1)} custom-call(f32[2,16,1536]{2,1,0:T(8,128)S(1)} %back_summary.1.refs_0_, f32[2,1536]{1,0:T(2,128)S(1)} %copy-done.6, f32[4,1536]{1,0:T(4,128)S(1)} %copy-done.4), custom_call_target="tpu_custom_call" | custom-call | flops 1000000 | bytes 20000000 | tf_op jit(solution)/shard_map/state_exchange_back/pallas_call | solution.py:463
  166.8 0.0 copy-start.2
  166.8 1.7 fusion.normed_gate_ref
  168.5 0.8 convolution_convert_fusion
  169.3 0.2 fusion.17
  169.5 1.6 pad_maximum_fusion
  171.0 0.0 copy-done.7
  171.0 2.2 convolution_convert_fusion.1
  173.3 125.9 %backward_gradients.1 = (f32[256,768]{1,0:T(8,128)}, bf16[2,2,2,4,48,768]{5,4,3,2,1,0:T(8,128)(2,1)}, bf16[2,2,2,4,48,768]{5,4,3,2,1,0:T(8,128)(2,1)}, bf16[3,2,...) custom-call(f32[256,1536]{1,0:T(8,128)} %get-tuple-element.53.delta_, ...), custom_call_target="tpu_custom_call" | custom-call | flops 100000000 | bytes 200000000 | tf_op jit(solution)/shard_map/backward_gradients/pallas_call | solution.py:1770
  299.2 3.8 %convert_add_fusion = f32[1,768,768]{2,1,0:T(8,128)} fusion(f32[1,768,768]{2,1,0:T(8,128)} %get-tuple-element.86, bf16[1,768,768]{2,1,0:T(8,128)(2,1)} %get-tuple-element.87), kind=kLoop, calls=%fused_computation.4 | loop fusion | flops 1179648 | bytes 5898240 | tf_op jit(solution)/shard_map/add | solution.py:1982
  303.0 0.0 copy-done.18
  303.0 1.6 convert_add_fusion.1
  304.6 0.5 copy-done.19
  305.1 1.3 fusion.2
  306.4 0.1 fusion.18
  306.5 0.1 squeeze.39
  306.6 0.1 squeeze.40
  306.7 0.6 convert_reduce_fusion.3
  307.3 0.7 convert_reduce_fusion
  308.0 0.6 maximum_convert_fusion.2
  308.6 0.6 reshape.162
  309.2 0.6 maximum_convert_fusion.1
  309.9 0.1 maximum_convert_fusion
  310.0 0.7 slice.112
  310.7 0.8 slice_bitcast_fusion
  311.5 0.2 fusion.16
  311.7 1.4 copy-done.11
  313.5 0.2 constant_dynamic-update-slice_fusion.1
  313.7 0.2 constant_dynamic-update-slice_fusion
  313.8 5.0 %convert_element_type.57 = f32[768,3072]{1,0:T(8,128)} convert(bf16[768,3072]{1,0:T(8,128)(2,1)S(1)} %constant_dynamic-update-slice_fusion) | non-fusion elementwise | flops 2359296 | bytes 14155776 | tf_op jit(solution)/shard_map/convert_element_type | solution.py:1994
  318.9 2.7 bitcast_convert_fusion
  321.6 0.9 copy.45
  (46 shorter events, 0.4 us)
Async XLA Ops:
  1.9 4.3 %copy-start.24 = (s32[2,128]{1,0:T(2,128)}, s32[2,128]{1,0:T(2,128)S(1)}, u32[]{:S(2)}) copy-start(s32[2,128]{1,0:T(2,128)S(1)} %compare_select_fusion) | copy-start | bytes 3076
  74.6 58.8 %copy-start.8 = (f32[256,768]{1,0:T(8,128)S(1)}, f32[256,768]{1,0:T(8,128)}, u32[]{:S(2)}) copy-start(f32[256,768]{1,0:T(8,128)} %get-tuple-element.52) | copy-start | bytes 2359300
  74.6 58.8 %copy-start.23 = (f32[768]{0:T(1024)S(1)}, f32[768]{0:T(1024)}, u32[]{:S(2)}) copy-start(f32[768]{0:T(1024)} %param.29) | copy-start | bytes 9220
  74.6 61.8 %copy-start.25 = (f32[256,1536]{1,0:T(8,128)S(1)}, f32[256,1536]{1,0:T(8,128)}, u32[]{:S(2)}) copy-start(f32[256,1536]{1,0:T(8,128)} %get-tuple-element.60) | copy-start | bytes 4718596
  133.4 2.7 copy-start.16
  133.4 2.9 copy-start.13
  133.5 2.9 copy-start.17
  136.1 30.6 %slice-start = ((s8[4718592]{0:T(1024)(128)(4,1)}), s8[4194304]{0:T(1024)(128)(4,1)S(1)}, s32[]{:S(2)}) async-start(s8[4718592]{0:T(1024)(128)(4,1)} %bitcast.52), calls=%async_computation | async-start | bytes 8388608
  136.4 34.6 %copy-start.7 = (f32[256,768]{1,0:T(8,128)}, f32[256,768]{1,0:T(8,128)S(1)}, u32[]{:S(2)}) copy-start(f32[256,768]{1,0:T(8,128)S(1)} %multiply_add_fusion.grad_resid_ref) | copy-start | bytes 2359300
  136.4 3.9 %copy-start = (f32[256,1536]{1,0:T(8,128)S(1)}, f32[256,1536]{1,0:T(8,128)}, u32[]{:S(2)}) copy-start(f32[256,1536]{1,0:T(8,128)} %get-tuple-element.53.delta_ref) | copy-start | bytes 4718596
  136.4 3.9 %copy-start.3 = (f32[16,1536]{1,0:T(8,128)S(1)}, f32[16,1536]{1,0:T(8,128)}, u32[]{:S(2)}) copy-start(f32[16,1536]{1,0:T(8,128)} %decay_log_ref.3) | copy-start | bytes 294916
  136.4 3.9 %copy-start.5 = (f32[16,16,16]{2,1,0:T(8,128)S(1)}, f32[16,16,16]{2,1,0:T(8,128)}, u32[]{:S(2)}) copy-start(f32[16,16,16]{2,1,0:T(8,128)} %get-tuple-element.62.out_ref.out_cols_ref) | copy-start | bytes 49156
  136.4 30.3 %slice-start.1 = ((s8[4718592]{0:T(1024)(128)(4,1)}), s8[524288]{0:T(1024)(128)(4,1)S(1)}, s32[]{:S(2)}) async-start(s8[4718592]{0:T(1024)(128)(4,1)} %bitcast.52), calls=%async_computation.1 | async-start | bytes 1048576
  139.7 7.4 %copy-start.1 = (f32[256,1536]{1,0:T(8,128)}, f32[256,1536]{1,0:T(8,128)S(1)}, u32[]{:S(2)}) copy-start(f32[256,1536]{1,0:T(8,128)S(1)} %get-tuple-element.96.grad_ref.grad_scan_ref) | copy-start | bytes 4718596
  140.3 6.7 %copy-start.4 = (f32[4,1536]{1,0:T(4,128)S(1)}, f32[4,1536]{1,0:T(4,128)}, u32[]{:S(2)}) copy-start(f32[4,1536]{1,0:T(4,128)} %get-tuple-element.108.own_log_ref.refs_2_) | copy-start | bytes 73732
  140.3 6.7 %copy-start.6 = (f32[2,1536]{1,0:T(2,128)S(1)}, f32[2,1536]{1,0:T(2,128)}, u32[]{:S(2)}) copy-start(f32[2,1536]{1,0:T(2,128)} %get-tuple-element.65.refs_1_) | copy-start | bytes 36868
  166.8 1.7 copy-start.2
  166.8 1.7 copy-start.15
  169.5 1.6 copy-start.22
  299.2 3.8 %copy-start.14 = (f32[1,768,768]{2,1,0:T(8,128)S(1)}, f32[1,768,768]{2,1,0:T(8,128)}, u32[]{:S(2)}) copy-start(f32[1,768,768]{2,1,0:T(8,128)} %get-tuple-element.84) | copy-start | bytes 7077892
  299.2 3.8 %copy-start.18 = (bf16[1,768,768]{2,1,0:T(8,128)(2,1)S(1)}, bf16[1,768,768]{2,1,0:T(8,128)(2,1)}, u32[]{:S(2)}) copy-start(bf16[1,768,768]{2,1,0:T(8,128)(2,1)} %get-tuple-element.85) | copy-start | bytes 3538948
  303.0 1.6 copy-start.9
  303.0 2.1 copy-start.19
  304.6 1.8 copy-start.21
  307.3 4.2 %copy-start.12 = (bf16[2,2,2,4,48,768]{5,4,3,2,1,0:T(8,128)(2,1)S(1)}, bf16[2,2,2,4,48,768]{5,4,3,2,1,0:T(8,128)(2,1)}, u32[]{:S(2)}) copy-start(bf16[2,2,2,4,48,768]{5,4,3,2,1,0:T(8,128)(2,1)} %get-tuple-element.82) | copy-start | bytes 7077892
  311.5 1.7 copy-start.11
  313.8 5.1 %copy-start.10 = (bf16[2,2,2,4,48,768]{5,4,3,2,1,0:T(8,128)(2,1)S(1)}, bf16[2,2,2,4,48,768]{5,4,3,2,1,0:T(8,128)(2,1)}, u32[]{:S(2)}) copy-start(bf16[2,2,2,4,48,768]{5,4,3,2,1,0:T(8,128)(2,1)} %get-tuple-element.83) | copy-start | bytes 7077892
  318.9 2.7 copy-start.20

commit v5 on v4

--- a/solution.py
+++ b/solution.py
@@ -336,7 +336,7 @@
     members,
     end_ref,
     sum_ref,
-    rates_ref,
+    log_ref,
     carry_ref,
     packed,
     landed,
@@ -354,7 +354,11 @@
     sequences, states, width = end_ref.shape
     rows = sequences * states // members
     plane, member = lax.axis_index("seq"), lax.axis_index("exp")
-    rates = -jnp.exp(rates_ref[...])
+    own = lax.rem(member, states // rows)
+    logs = jnp.zeros((rows, width), jnp.float32)
+    for i in range(states // rows):
+        logs = jnp.where(own == i, log_ref[i * rows : (i + 1) * rows], logs)
+    rates = -jnp.exp(logs)
     for i in range(members):
         q, n = (i * rows) // states, (i * rows) % states
         packed[i, :rows] = end_ref[q, n : n + rows]
@@ -456,9 +460,10 @@
     ]
 
 
-def exchange(local_end, delta_sum, own_log):
+def exchange(local_end, delta_sum, decay_log):
     planes, members = lax.axis_size("seq"), lax.axis_size("exp")
-    rows, width = own_log.shape
+    sequences, states, width = local_end.shape
+    rows = sequences * states // members
     vmem = pl.BlockSpec(memory_space=pltpu.VMEM)
     return pl.pallas_call(
         functools.partial(exchange_kernel, True, planes, members),
@@ -471,7 +476,7 @@
             collective_id=2, has_side_effects=True, vmem_limit_bytes=VMEM_BYTES
         ),
         cost_estimate=pl.CostEstimate(flops=10**6, transcendentals=10**5, bytes_accessed=2 * 10**7),
-    )(local_end, delta_sum, own_log)
+    )(local_end, delta_sum, decay_log)
 
 
 class Sums:
@@ -773,13 +778,16 @@
     layer_ref,
     out_grad_ref,
     target_ref,
-    vectors_ref,
+    mixer_gain_all_ref,
+    conv_bias_all_ref,
+    delta_bias_all_ref,
+    skip_all_ref,
+    expert_norm_all_ref,
     in_proj_ref,
     conv_weight_ref,
     state_proj_ref,
     delta_proj_ref,
     decay_log_ref,
-    own_log_ref,
     out_proj_ref,
     up_ref,
     down_ref,
@@ -804,6 +812,7 @@
     near_up_ref,
     near_half_ref,
     rim_in_ref,
+    vectors_ref,
     grad_slots_ref,
     drive_ref,
     stack_ref,
@@ -831,6 +840,10 @@
     states, taps = decay_log_ref.shape[0], conv_weight_ref.shape[0]
     low_rank = delta_low_ref.shape[1]
     experts = row_slots_ref.shape[0]
+    for i, source in enumerate((conv_bias_all_ref, delta_bias_all_ref, skip_all_ref)):
+        vectors_ref[i : i + 1, :] = source[...].reshape(1, inner_width)
+    vectors_ref[3:4, :width] = mixer_gain_all_ref[...].reshape(1, width)
+    vectors_ref[3:4, width:] = expert_norm_all_ref[...].reshape(1, width)
     conv_bias_ref, delta_bias_ref, skip_ref = (vectors_ref.at[i : i + 1] for i in range(3))
     mixer_gain_ref, expert_norm_ref = vectors_ref.at[3:4, :width], vectors_ref.at[3:4, width:]
     devices = planes * members
@@ -997,7 +1010,7 @@
         members,
         local_end_ref,
         delta_sum_ref,
-        own_log_ref,
+        decay_log_ref,
         carried_ref,
         *exchange_refs,
     )
@@ -1040,8 +1053,8 @@
 def forward(operands, capacity, states, sequences, low_rank, experts):
     planes, members = lax.axis_size("seq"), lax.axis_size("exp")
     tokens, width = operands[0].shape
-    inner_width = operands[3].shape[1]
-    up, down = operands[11:13]
+    inner_width = operands[9].shape[1]
+    up, down = operands[14:16]
     half, wide = jnp.bfloat16, jnp.float32
     piece = tokens // sequences
     token_wide = jax.ShapeDtypeStruct((tokens, inner_width), wide)
@@ -1068,8 +1081,8 @@
     return pl.pallas_call(
         functools.partial(forward_kernel, planes, members, capacity),
         name="forward_to_experts",
-        in_specs=[vmem] * 11 + [anywhere] * 2,
-        out_specs=[vmem] * 17 + [anywhere] * 3 + [vmem],
+        in_specs=[vmem] * 14 + [anywhere] * 2,
+        out_specs=[vmem] * 17 + [anywhere] * 3 + [vmem] * 2,
         out_shape=[
             jax.ShapeDtypeStruct((tokens + 8 * sequences, width), half),
             jax.ShapeDtypeStruct((sequences, piece + 8, inner_width), wide),
@@ -1092,6 +1105,7 @@
             jax.ShapeDtypeStruct(up.shape, half),
             jax.ShapeDtypeStruct((1, down.shape[1] // 2, width), half),
             jax.ShapeDtypeStruct((sequences, 8, width), half),
+            jax.ShapeDtypeStruct((4, inner_width), wide),
         ],
         scratch_shapes=scratch,
         compiler_params=pltpu.CompilerParams(
@@ -1111,7 +1125,6 @@
     near_up_ref,
     near_half_ref,
     router_ref,
-    chosen_ref,
     outs_ref,
     back_ref,
     grad_up_ref,
@@ -1149,6 +1162,10 @@
     group = members * capacity
     units = up_ref.shape[2]
     cut = units // 2
+    experts = router_ref.shape[0]
+    chosen_row = jnp.where(
+        lax.broadcasted_iota(jnp.int32, (1, experts), 1) == member, 1.0, 0.0
+    )
     barrier = pltpu.get_barrier_semaphore()
     pl.semaphore_signal(barrier, inc=1, device_id=neighbour_plane(), device_id_type=MESH)
     pl.semaphore_wait(barrier, routes.signal_peers(barrier) + 1)
@@ -1197,7 +1214,7 @@
         logits = cols_dot(rows_ref[at, :].astype(wide), router_ref[...], lax.Precision.HIGHEST)
         raised = jnp.exp(logits - jnp.max(logits, axis=-1, keepdims=True))
         shares = raised / jnp.sum(raised, axis=-1, keepdims=True)
-        gate = jnp.sum(shares * chosen_ref[...], axis=-1, keepdims=True)
+        gate = jnp.sum(shares * chosen_row, axis=-1, keepdims=True)
         shares_ref[at, :] = shares
         sent_ref[at, :] = (gate * grads_ref[at, :].astype(wide)).astype(half)
         every = slice(0, units)
@@ -1220,7 +1237,7 @@
             slice(cut, units),
         )
         out = out_sum_ref[at, :] + near_out
-        shares, chosen = shares_ref[at, :], chosen_ref[...]
+        shares, chosen = shares_ref[at, :], chosen_row
         gate = jnp.sum(shares * chosen, axis=-1, keepdims=True)
         grad_gate = jnp.sum(grads_ref[at, :].astype(wide) * out, axis=-1, keepdims=True)
         grad_logits = grad_gate * gate * (chosen - shares)
@@ -1328,7 +1345,7 @@
     routes.wait_sent(row_slots_ref, landed_ref)
 
 
-def expert_apply(row_slots, grad_rows, weights, router, chosen):
+def expert_apply(row_slots, grad_rows, weights, router):
     planes, members = lax.axis_size("seq"), lax.axis_size("exp")
     experts, capacity, width = row_slots.shape
     up, down, near_up, near_half = weights
@@ -1342,7 +1359,7 @@
     return pl.pallas_call(
         functools.partial(expert_kernel, planes, members),
         name="expert_apply",
-        in_specs=[vmem] * 8,
+        in_specs=[vmem] * 7,
         out_specs=[vmem] * 7,
         out_shape=[
             jax.ShapeDtypeStruct(slotted, half),
@@ -1383,7 +1400,7 @@
             transcendentals=4 * count * units,
             bytes_accessed=3 * 10**7,
         ),
-    )(row_slots, grad_rows, *weights, router, chosen)
+    )(row_slots, grad_rows, *weights, router)
 
 
 def gradient_kernel(
@@ -1657,7 +1674,6 @@
         device_id_type=MESH,
     )
     rim_copy.start()
-    sums.gather_across(0, results[0])
     in_load.wait()
     projected = cols_dot(slopes[...], in_part[...])
     normed_grad = normed_gate_ref[...] + projected[:tokens]
@@ -1696,20 +1712,20 @@
     for s in every:
         sums.after_first(2 + s, *tail_of(s)[:4])
     sums.after_pair(last, given_small, *small_buffers[:2])
-    sums.gather_across(1, results[1])
+    for s in every:
+        sums.after_second(2 + s, *tail_of(s)[2:6])
+    for i in pair:
+        sums.gather_across(i, results[i])
     weighted = normed_grad * mixer_gain_ref[...]
     in_grad_ref[...] = grad_resid_ref[...] + scaling * (
         weighted - normal * jnp.mean(weighted * normal, axis=-1, keepdims=True)
     )
-    for s in every:
-        sums.after_second(2 + s, *tail_of(s)[2:6])
     sums.after_first(last, *small_buffers[:4])
     tails = [total_inner_ref.at[s] for s in every] + [total_small_ref]
     tail_blocks = [total.at[sums.core, sums.first, sums.second] for total in tails]
     for s in every:
         sums.after_planes(2 + s, *tail_of(s)[4:6], tail_blocks[s])
     sums.after_second(last, *small_buffers[2:6])
-    sums.gather_pass(0, results[0])
     for s in every:
         sums.planes_gathered(2 + s, tail_blocks[s])
         sums.gather_second_start(2 + s, tails[s])
@@ -1718,7 +1734,8 @@
         sums.gather_across(2 + s, tails[s])
     sums.planes_gathered(last, tail_blocks[slabs])
     sums.gather_second_start(last, total_small_ref)
-    sums.gather_pass(1, results[1])
+    for i in pair:
+        sums.gather_pass(i, results[i])
     rim_copy.wait()
     keep_last = jnp.where(place < devices - 1, 1.0, 0.0)
     for q in range(sequences):
@@ -1847,11 +1864,6 @@
     target = jnp.where(flat_slot < capacity, flat_ids * capacity + flat_slot, experts * capacity)
     slot_rows = jnp.arange(experts * capacity, dtype=jnp.int32)
     picks = (slot_rows[:, None] == target).astype(jnp.bfloat16)
-    state_rows = sequences * states // senders
-    first_row = lax.rem(lax.axis_index("exp") * state_rows, states)
-    own_log = lax.dynamic_slice(decay_log, (first_row, 0), (state_rows, inner_width))
-    norms = jnp.concatenate([mixer_gain, expert_norm])
-    vectors = jnp.stack([conv_bias, delta_bias, skip_gain, norms])
     (
         normed_half,
         extended,
@@ -1874,18 +1886,22 @@
         near_up,
         near_half,
         rim_layer,
+        vectors,
     ) = forward(
         [
             layer_in.reshape(tokens, width),
             out_grad.reshape(tokens, width),
             target,
-            vectors,
+            mixer_gain,
+            conv_bias,
+            delta_bias,
+            skip_gain,
+            expert_norm,
             in_proj,
             conv_weight,
             state_proj.T,
             delta_proj,
             decay_log,
-            own_log,
             out_proj,
             expert_up,
             expert_down,
@@ -1899,11 +1915,8 @@
     gate_act = jax.nn.silu(gate_half)
     scaling_two = lax.rsqrt(jnp.mean(resid * resid, axis=-1, keepdims=True) + EPSILON)
     weights = [expert_up, expert_down, near_up, near_half]
-    chosen = (
-        jnp.arange(experts, dtype=jnp.int32) == lax.axis_index("exp")
-    ).astype(jnp.float32)[None, :]
     expert_out, back_rows, grad_up, grad_down, far_up, far_down, grad_router = expert_apply(
-        row_slots, grad_rows, weights, router_weight.T, chosen
+        row_slots, grad_rows, weights, router_weight.T
     )
     grad_routed = rows_dot(
         jnp.concatenate([picks] * hops, axis=0), back_rows.reshape(hops * senders * capacity, width)
@@ -1929,7 +1942,7 @@
         ["state"],
         [],
     )
-    carried_back = exchange(gradient_first, delta_sum, own_log)
+    carried_back = exchange(gradient_first, delta_sum, decay_log)
     side = math.isqrt(senders // 2)
     big = (2, side, side, planes, inner_width // (senders * planes), width)
 

time: 324 us -> 320 us (0.988)
  no operation moved by 1% of the time
where the time goes in v5:
time: 320 us; the launch traced here: 319 us
  Pallas kernels  278 us (87%)
  other arithmetic  19.8 us (6%)
  matrix products  12.6 us (4%)
  local copies, waits for them, and re-layouts  7.54 us (2%)
    pallas_call x1, Pallas kernels, all_gradients(): pl.pallas_call(functools.partial(gradient_kernel, planes, side), name='ba...  126 us
    pallas_call x1, Pallas kernels, forward(): pl.pallas_call(functools.partial(forward_kernel, planes, members, capacit...  67.1 us
    pallas_call x1, Pallas kernels, expert_apply(): pl.pallas_call(functools.partial(expert_kernel, planes, members), name='e...  58.8 us
    pallas_call x1, Pallas kernels, exchange(): pl.pallas_call(functools.partial(exchange_kernel, True, planes, members),...  19.7 us
    dot_general x4, matrix products, rows_dot(): lax.dot_general(left, right, (((0,), (0,)), ((), ())), precision=precisio...  7.65 us
    pallas_call x1, Pallas kernels, scan_call(): pl.pallas_call(kernel, name=name, grid=(sequences, width // GROUP), in_sp...  6.7 us

profile of v5, /device:TPU:11, one launch (start us, length us, event | category | flops | bytes accessed | tf_op | source)
XLA Modules:
  0.0 319.2 jit_solution(17130984772648175920)
XLA Ops:
  0.6 0.7 compare_select_fusion
  1.3 0.1 iota_compare_fusion
  1.4 0.5 copy-done.21
  1.9 67.1 %forward_to_experts.1 = (bf16[272,768]{1,0:T(8,128)(2,1)}, f32[2,136,1536]{2,1,0:T(8,128)}, f32[256,1536]{1,0:T(8,128)}, f32[256,1536]{1,0:T(8,128)}, f32[256,15...) custom-call(bf16[256,768]{1,0:T(8,128)(2,1)} %bitcast.65, ...), custom_call_target="tpu_custom_call" | custom-call | flops 100000000 | bytes 200000000 | tf_op jit(solution)/shard_map/forward_to_experts/pallas_call | solution.py:1081
  69.0 1.3 multiply_reduce_fusion.3
  70.3 0.0 copy-start.7
  70.3 0.0 copy-start.20
  70.3 0.0 copy-start.22
  70.3 58.8 %expert_apply.1 = (bf16[2,8,40,768]{3,2,1,0:T(8,128)(2,1)}, bf16[2,8,40,768]{3,2,1,0:T(8,128)(2,1)}, f32[1,768,768]{2,1,0:T(8,128)}, f32[1,768,768]{2,1,0:T(8,12...) custom-call(bf16[8,40,768]{2,1,0:T(8,128)(2,1)} %get-tuple-element.56.row_slots_ref, ...), custom_call_target="tpu_custom_call" | custom-call | flops 9059696640 | bytes 30000000 | tf_op jit(solution)/shard_map/expert_apply/pallas_call | solution.py:1359
  129.1 0.0 copy-start.14
  129.1 0.0 copy-done.7
  129.1 0.0 copy-done.20
  129.1 0.0 copy-start.12
  129.1 0.0 copy-start.15
  129.2 2.0 multiply_reduce_fusion.1
  131.2 0.6 broadcast_in_dim.16.norm_grad_ref
  131.8 0.0 copy-done.14
  131.8 0.3 multiply_add_fusion.grad_resid_ref
  132.0 0.0 copy-done.22
  132.1 0.0 copy-done.12
  132.1 0.0 copy-done.15
  132.1 0.0 copy-start.6
  132.1 0.0 copy-start
  132.1 0.0 copy-start.2
  132.1 0.0 copy-start.4
  132.1 0.0 slice-start.1
  132.1 3.2 %multiply_reduce_fusion = (f32[1536]{0:T(1024)S(1)}, f32[256,1536]{1,0:T(8,128)S(1)}, bf16[256,1536]{1,0:T(8,128)(2,1)S(1)}) fusion(f32[256,1536]{1,0:T(8,128)S(1)} %copy-done.15, f32[256,1536]{1,0:T(8,128)S(1)} %copy-done.22, f32[256,1536]{1,0:T(8,128)} %get-tuple-element.72, bf16[1536,768]{1,0:T(8,128)(2,1)S(1)} %copy-done.12, ...), kind=kOutput, calls=%fused_computation.8 | convolution fusion | flops 609679872 | bytes 10229760 | tf_op jit(solution)/shard_map/dot_general | solution.py:37
  135.4 0.0 copy-start.1
  135.4 0.6 broadcast_in_dim.15.skip_grad_ref
  136.0 0.0 copy-done.2
  136.0 6.7 %back_summary.1.refs_0_ = f32[2,16,1536]{2,1,0:T(8,128)S(1)} custom-call(f32[256,1536]{1,0:T(8,128)S(1)} %copy-done, f32[256,1536]{1,0:T(8,128)S(1)} %get-tuple-element.98.grad_ref.grad_scan_ref, f32[16,16,16]{2,1,0:T(8,128)S(1)} %copy-done.4, f32[16,1536]{1,0:T(8,128)S(1)} %copy-done.2), custom_call_target="tpu_custom_call" | custom-call | flops 125829120 | bytes 6291456 | tf_op jit(solution)/shard_map/back_summary/pallas_call | solution.py:284
  142.7 19.7 %state_exchange_back.1.carried_back_ref = f32[2,16,1536]{2,1,0:T(8,128)S(1)} custom-call(f32[2,16,1536]{2,1,0:T(8,128)S(1)} %back_summary.1.refs_0_, f32[2,1536]{1,0:T(2,128)S(1)} %copy-done.5, f32[16,1536]{1,0:T(8,128)S(1)} %copy-done.2), custom_call_target="tpu_custom_call" | custom-call | flops 1000000 | bytes 20000000 | tf_op jit(solution)/shard_map/state_exchange_back/pallas_call | solution.py:468
  162.5 0.0 copy-start.3
  162.5 1.7 fusion.normed_gate_ref
  164.2 0.8 convolution_convert_fusion
  165.0 0.2 fusion.17
  165.2 0.0 copy-start.19
  165.2 1.6 pad_maximum_fusion
  166.8 0.0 copy-done.19
  166.8 2.2 convolution_convert_fusion.1
  169.0 126.0 %backward_gradients.1 = (f32[256,768]{1,0:T(8,128)}, bf16[2,2,2,4,48,768]{5,4,3,2,1,0:T(8,128)(2,1)}, bf16[2,2,2,4,48,768]{5,4,3,2,1,0:T(8,128)(2,1)}, bf16[3,2,...) custom-call(f32[256,1536]{1,0:T(8,128)} %get-tuple-element.54.delta_, ...), custom_call_target="tpu_custom_call" | custom-call | flops 100000000 | bytes 200000000 | tf_op jit(solution)/shard_map/backward_gradients/pallas_call | solution.py:1787
  295.0 2.6 fusion.2
  297.6 0.0 copy-done.16
  297.6 5.6 %convert_add_fusion = (f32[1,768,768]{2,1,0:T(8,128)}, f32[1,768,768]{2,1,0:T(8,128)}) fusion(f32[1,768,768]{2,1,0:T(8,128)} %get-tuple-element.88, bf16[1,768,768]{2,1,0:T(8,128)(2,1)} %get-tuple-element.89, f32[1,768,768]{2,1,0:T(8,128)} %get-tuple-element.86, bf16[1,768,768]{2,1,0:T(8,128)(2,1)S(1)} %copy-done.16), kind=kLoop, calls=%fused_computation.4 | loop fusion | flops 2359296 | bytes 11796480 | tf_op jit(solution)/shard_map/add | solution.py:1995
  303.2 0.1 fusion.18
  303.2 0.1 squeeze.39
  303.3 0.1 squeeze.40
  303.4 0.6 convert_reduce_fusion.3
  304.1 0.7 convert_reduce_fusion
  304.7 0.6 maximum_convert_fusion.2
  305.3 0.6 reshape.152
  305.9 0.6 maximum_convert_fusion.1
  306.6 0.1 maximum_convert_fusion
  306.7 0.7 slice.112
  307.4 0.8 slice_bitcast_fusion
  308.2 0.0 copy-done.11
  308.2 0.2 fusion.16
  308.5 1.4 copy-done.10
  310.2 0.2 constant_dynamic-update-slice_fusion.1
  310.4 0.2 constant_dynamic-update-slice_fusion
  310.6 0.0 copy-start.9
  310.6 5.0 %convert_element_type.46 = f32[768,3072]{1,0:T(8,128)} convert(bf16[768,3072]{1,0:T(8,128)(2,1)S(1)} %constant_dynamic-update-slice_fusion) | non-fusion elementwise | flops 2359296 | bytes 14155776 | tf_op jit(solution)/shard_map/convert_element_type | solution.py:2007
  315.6 2.7 bitcast_convert_fusion
  318.3 0.9 copy.45
  (32 shorter events, 0.3 us)
Async XLA Ops:
  1.3 0.6 copy-start.21
  70.3 58.9 %copy-start.7 = (f32[256,768]{1,0:T(8,128)S(1)}, f32[256,768]{1,0:T(8,128)}, u32[]{:S(2)}) copy-start(f32[256,768]{1,0:T(8,128)} %get-tuple-element.53) | copy-start | bytes 2359300
  70.3 58.9 %copy-start.20 = (f32[768]{0:T(1024)S(1)}, f32[768]{0:T(1024)}, u32[]{:S(2)}) copy-start(f32[768]{0:T(1024)} %expert_norm_all_ref.1) | copy-start | bytes 9220
  70.3 61.8 %copy-start.22 = (f32[256,1536]{1,0:T(8,128)S(1)}, f32[256,1536]{1,0:T(8,128)}, u32[]{:S(2)}) copy-start(f32[256,1536]{1,0:T(8,128)} %get-tuple-element.61) | copy-start | bytes 4718596
  129.1 2.7 copy-start.14
  129.1 2.9 copy-start.12
  129.1 2.9 copy-start.15
  131.8 30.7 %slice-start = ((s8[4718592]{0:T(1024)(128)(4,1)}), s8[4194304]{0:T(1024)(128)(4,1)S(1)}, s32[]{:S(2)}) async-start(s8[4718592]{0:T(1024)(128)(4,1)} %bitcast.52), calls=%async_computation | async-start | bytes 8388608
  132.1 34.7 %copy-start.6 = (f32[256,768]{1,0:T(8,128)}, f32[256,768]{1,0:T(8,128)S(1)}, u32[]{:S(2)}) copy-start(f32[256,768]{1,0:T(8,128)S(1)} %multiply_add_fusion.grad_resid_ref) | copy-start | bytes 2359300
  132.1 3.9 %copy-start = (f32[256,1536]{1,0:T(8,128)S(1)}, f32[256,1536]{1,0:T(8,128)}, u32[]{:S(2)}) copy-start(f32[256,1536]{1,0:T(8,128)} %get-tuple-element.54.delta_ref) | copy-start | bytes 4718596
  132.1 3.9 %copy-start.2 = (f32[16,1536]{1,0:T(8,128)S(1)}, f32[16,1536]{1,0:T(8,128)}, u32[]{:S(2)}) copy-start(f32[16,1536]{1,0:T(8,128)} %decay_log_ref.3) | copy-start | bytes 294916
  132.1 3.9 %copy-start.4 = (f32[16,16,16]{2,1,0:T(8,128)S(1)}, f32[16,16,16]{2,1,0:T(8,128)}, u32[]{:S(2)}) copy-start(f32[16,16,16]{2,1,0:T(8,128)} %get-tuple-element.63.out_ref.out_cols_ref) | copy-start | bytes 49156
  132.1 30.4 %slice-start.1 = ((s8[4718592]{0:T(1024)(128)(4,1)}), s8[524288]{0:T(1024)(128)(4,1)S(1)}, s32[]{:S(2)}) async-start(s8[4718592]{0:T(1024)(128)(4,1)} %bitcast.52), calls=%async_computation.1 | async-start | bytes 1048576
  135.4 7.4 %copy-start.1 = (f32[256,1536]{1,0:T(8,128)}, f32[256,1536]{1,0:T(8,128)S(1)}, u32[]{:S(2)}) copy-start(f32[256,1536]{1,0:T(8,128)S(1)} %get-tuple-element.98.grad_ref.grad_scan_ref) | copy-start | bytes 4718596
  136.0 6.7 %copy-start.5 = (f32[2,1536]{1,0:T(2,128)S(1)}, f32[2,1536]{1,0:T(2,128)}, u32[]{:S(2)}) copy-start(f32[2,1536]{1,0:T(2,128)} %get-tuple-element.66.refs_1_) | copy-start | bytes 36868
  162.5 1.7 copy-start.3
  162.5 1.7 copy-start.13
  165.2 1.6 copy-start.19
  169.0 126.0 %copy-start.8 = (f32[256,768]{1,0:T(8,128)S(1)}, f32[256,768]{1,0:T(8,128)}, u32[]{:S(2)}) copy-start(f32[256,768]{1,0:T(8,128)} %get-tuple-element.53) | copy-start | bytes 2359300
  295.0 2.6 copy-start.16
  297.6 5.6 %copy-start.18 = (bf16[2,2,2,4,10,768]{5,4,3,2,1,0:T(8,128)(2,1)S(1)}, bf16[2,2,2,4,10,768]{5,4,3,2,1,0:T(8,128)(2,1)}, u32[]{:S(2)}) copy-start(bf16[2,2,2,4,10,768]{5,4,3,2,1,0:T(8,128)(2,1)} %get-tuple-element.82) | copy-start | bytes 1474564
  304.0 4.2 %copy-start.11 = (bf16[2,2,2,4,48,768]{5,4,3,2,1,0:T(8,128)(2,1)S(1)}, bf16[2,2,2,4,48,768]{5,4,3,2,1,0:T(8,128)(2,1)}, u32[]{:S(2)}) copy-start(bf16[2,2,2,4,48,768]{5,4,3,2,1,0:T(8,128)(2,1)} %get-tuple-element.84) | copy-start | bytes 7077892
  308.2 1.7 copy-start.10
  310.6 5.1 %copy-start.9 = (bf16[2,2,2,4,48,768]{5,4,3,2,1,0:T(8,128)(2,1)S(1)}, bf16[2,2,2,4,48,768]{5,4,3,2,1,0:T(8,128)(2,1)}, u32[]{:S(2)}) copy-start(bf16[2,2,2,4,48,768]{5,4,3,2,1,0:T(8,128)(2,1)} %get-tuple-element.85) | copy-start | bytes 7077892
  315.6 2.7 copy-start.17

commit v6 on v5

--- a/solution.py
+++ b/solution.py
@@ -1433,7 +1433,7 @@
     norm_grad_ref,
     router_grad_ref,
     early_out_ref,
-    early_gate_ref,
+    gate_slope_ref,
     returned_ref,
     far_up_ref,
     far_down_ref,
@@ -1466,6 +1466,7 @@
     part_loaded,
     given_inner,
     given_small,
+    early_gate_ref,
     *rest,
 ):
     early_buffers, tail_buffers, small_buffers = rest[:12], rest[12:18], rest[18:24]
@@ -1490,6 +1491,15 @@
         pl.semaphore_signal(barrier, inc=1, device_id=device, device_id_type=MESH)
     pl.semaphore_signal(barrier, inc=1, device_id=neighbour_plane(), device_id_type=MESH)
     greeted = 3 + sums.signal_peers(barrier) + routes.signal_peers(barrier)
+    tall = width // chips
+    size = tall // planes
+    for c in range(2):
+        gate_part = gate_slope_ref[:, c * width : (c + 1) * width]
+        for m in range(chips):
+            part = normed_ref[:tokens, m * tall : (m + 1) * tall]
+            product = rows_dot(part, gate_part).astype(half)
+            for z in range(planes):
+                early_gate_ref[c, m // side, m % side, z] = product[z * size : (z + 1) * size]
     pl.semaphore_wait(barrier, greeted)
 
     in_load = pltpu.make_async_copy(in_proj_ref.at[:, pl.ds(0, inner_width)], in_part, part_loaded)
@@ -1635,8 +1645,6 @@
             small[at_conv + tap : at_conv + tap + 1, at] = product
 
     slabs = given_inner.shape[0]
-    tall = width // chips
-    size = tall // planes
 
     def tail_of(s):
         return [buffer.at[s] for buffer in tail_buffers]
@@ -1814,6 +1822,7 @@
             pltpu.SemaphoreType.DMA,
             pltpu.VMEM(inner, half),
             pltpu.VMEM(little, half),
+            pltpu.VMEM(big, half),
         ]
         + scatter_buffers([big[4:], big[4:]], planes, side)
         + [pltpu.VMEM((slabs,) + shape, half) for shape in tail_shapes]
@@ -1930,7 +1939,6 @@
     grad_scan = grad_mixed * gate_act
     grad_gate_half = grad_mixed * mixer_pre * silu_slope(gate_half)
     grad_gate_half = grad_gate_half.astype(jnp.bfloat16)
-    grad_in_gate = rows_dot(normed_half[:tokens], grad_gate_half)
     grad_normed_gate = cols_dot(grad_gate_half, in_proj[:, inner_width:])
     grad_skip_gain = jnp.sum(grad_scan * conv_flat, axis=0, keepdims=True)
     (gradient_first,) = scan_call(
@@ -1946,15 +1954,9 @@
     side = math.isqrt(senders // 2)
     big = (2, side, side, planes, inner_width // (senders * planes), width)
 
-    def as_rows(values):
-        blocks = values.shape[1] // width
-        return jnp.concatenate(
-            [values[:, at * width : (at + 1) * width] for at in range(blocks)], axis=0
-        ).astype(jnp.bfloat16)
-
     early = [
         grad_out_proj.astype(jnp.bfloat16).reshape(big),
-        as_rows(grad_in_gate).reshape(big),
+        grad_gate_half,
     ]
     heights = [low_rank + 2 * states, low_rank, states, taps, 1, 1, 1, 1, experts // 2]
     in_grad, sum_out, sum_gate, sum_inner, sum_small, back_out, near_up, near_down = all_gradients(

time: 320 us -> 318 us (level)
    dot_general x4 -> x3, matrix products: 7.65 us -> 6.84 us  [rows_dot(): lax.dot_general(left, right, (((0,), (0,)), ((), ())), precision=precisio...]
where the time goes in v6:
time: 318 us; the launch traced here: 316 us
  Pallas kernels  278 us (87%)
  other arithmetic  18.2 us (6%)
  matrix products  12.1 us (4%)
  local copies, waits for them, and re-layouts  7.41 us (2%)
    pallas_call x1, Pallas kernels, all_gradients(): pl.pallas_call(functools.partial(gradient_kernel, planes, side), name='ba...  125 us
    pallas_call x1, Pallas kernels, forward(): pl.pallas_call(functools.partial(forward_kernel, planes, members, capacit...  67.1 us
    pallas_call x1, Pallas kernels, expert_apply(): pl.pallas_call(functools.partial(expert_kernel, planes, members), name='e...  58.7 us
    pallas_call x1, Pallas kernels, exchange(): pl.pallas_call(functools.partial(exchange_kernel, True, planes, members),...  19.7 us
    dot_general x3, matrix products, rows_dot(): lax.dot_general(left, right, (((0,), (0,)), ((), ())), precision=precisio...  6.84 us
    pallas_call x1, Pallas kernels, scan_call(): pl.pallas_call(kernel, name=name, grid=(sequences, width // GROUP), in_sp...  6.7 us

profile of v6, /device:TPU:11, one launch (start us, length us, event | category | flops | bytes accessed | tf_op | source)
XLA Modules:
  0.0 316.4 jit_solution(13520635318550284880)
XLA Ops:
  0.6 0.7 compare_select_fusion
  1.3 0.1 iota_compare_fusion
  1.4 0.5 copy-done.21
  1.9 67.1 %forward_to_experts.1 = (bf16[272,768]{1,0:T(8,128)(2,1)}, f32[2,136,1536]{2,1,0:T(8,128)}, f32[256,1536]{1,0:T(8,128)}, f32[256,1536]{1,0:T(8,128)}, f32[256,15...) custom-call(bf16[256,768]{1,0:T(8,128)(2,1)} %bitcast.62, ...), custom_call_target="tpu_custom_call" | custom-call | flops 100000000 | bytes 200000000 | tf_op jit(solution)/shard_map/forward_to_experts/pallas_call | solution.py:1081
  69.0 1.3 multiply_reduce_fusion.3
  70.3 0.0 copy-start.7
  70.3 0.0 copy-start.20
  70.3 58.7 %expert_apply.1 = (bf16[2,8,40,768]{3,2,1,0:T(8,128)(2,1)}, bf16[2,8,40,768]{3,2,1,0:T(8,128)(2,1)}, f32[1,768,768]{2,1,0:T(8,128)}, f32[1,768,768]{2,1,0:T(8,12...) custom-call(bf16[8,40,768]{2,1,0:T(8,128)(2,1)} %get-tuple-element.56.row_slots_ref, ...), custom_call_target="tpu_custom_call" | custom-call | flops 9059696640 | bytes 30000000 | tf_op jit(solution)/shard_map/expert_apply/pallas_call | solution.py:1359
  129.0 0.0 copy-start.13
  129.0 0.0 copy-done.7
  129.0 0.0 copy-done.20
  129.1 0.0 copy-start.12
  129.1 0.0 copy-start.14
  129.1 2.0 multiply_reduce_fusion.1
  131.1 0.6 broadcast_in_dim.16.norm_grad_ref
  131.7 0.0 copy-done.13
  131.7 0.2 multiply_add_fusion.grad_resid_ref
  131.9 0.0 copy-done.12
  131.9 0.0 copy-done.14
  132.0 0.0 copy-start.6
  132.0 0.0 copy-start
  132.0 0.0 copy-start.2
  132.0 0.0 copy-start.4
  132.0 0.0 slice-start.1
  132.0 3.6 %multiply_reduce_fusion = (f32[1536]{0:T(1024)S(1)}, f32[256,1536]{1,0:T(8,128)S(1)}, bf16[256,1536]{1,0:T(8,128)(2,1)S(1)}) fusion(f32[256,1536]{1,0:T(8,128)S(1)} %copy-done.14, f32[256,1536]{1,0:T(8,128)} %get-tuple-element.61, f32[256,1536]{1,0:T(8,128)} %get-tuple-element.72, bf16[1536,768]{1,0:T(8,128)(2,1)S(1)} %copy-done.12, ...), kind=kOutput, calls=%fused_computation.6 | convolution fusion | flops 609679872 | bytes 10229760 | tf_op jit(solution)/shard_map/dot_general | solution.py:37
  135.6 0.0 copy-start.1
  135.6 0.0 copy-start.16
  135.7 0.7 broadcast_in_dim.15.skip_grad_ref
  136.3 0.0 copy-done
  136.3 0.0 copy-done.2
  136.3 0.0 copy-done.4
  136.3 6.7 %back_summary.1.refs_0_ = f32[2,16,1536]{2,1,0:T(8,128)S(1)} custom-call(f32[256,1536]{1,0:T(8,128)S(1)} %copy-done, f32[256,1536]{1,0:T(8,128)S(1)} %get-tuple-element.98.grad_ref.grad_scan_ref, f32[16,16,16]{2,1,0:T(8,128)S(1)} %copy-done.4, f32[16,1536]{1,0:T(8,128)S(1)} %copy-done.2), custom_call_target="tpu_custom_call" | custom-call | flops 125829120 | bytes 6291456 | tf_op jit(solution)/shard_map/back_summary/pallas_call | solution.py:284
  143.0 0.0 copy-done.1
  143.0 0.0 copy-done.5
  143.1 19.7 %state_exchange_back.1.carried_back_ref = f32[2,16,1536]{2,1,0:T(8,128)S(1)} custom-call(f32[2,16,1536]{2,1,0:T(8,128)S(1)} %back_summary.1.refs_0_, f32[2,1536]{1,0:T(2,128)S(1)} %copy-done.5, f32[16,1536]{1,0:T(8,128)S(1)} %copy-done.2), custom_call_target="tpu_custom_call" | custom-call | flops 1000000 | bytes 20000000 | tf_op jit(solution)/shard_map/state_exchange_back/pallas_call | solution.py:468
  162.8 0.0 copy-done.16
  162.8 0.0 slice-done
  162.8 0.0 slice-done.1
  162.8 0.0 copy-start.3
  162.8 0.0 copy-start.19
  162.8 1.7 fusion.normed_gate_ref
  164.5 0.0 copy-done.19
  164.5 2.2 convolution_convert_fusion
  166.8 125.4 %backward_gradients.1 = (f32[256,768]{1,0:T(8,128)}, bf16[2,2,2,4,48,768]{5,4,3,2,1,0:T(8,128)(2,1)}, bf16[2,2,2,4,48,768]{5,4,3,2,1,0:T(8,128)(2,1)}, bf16[3,2,...) custom-call(f32[256,1536]{1,0:T(8,128)} %get-tuple-element.54.delta_, ...), custom_call_target="tpu_custom_call" | custom-call | flops 100000000 | bytes 200000000 | tf_op jit(solution)/shard_map/backward_gradients/pallas_call | solution.py:1795
  292.2 2.6 fusion.2
  294.8 5.6 %convert_add_fusion = (f32[1,768,768]{2,1,0:T(8,128)}, f32[1,768,768]{2,1,0:T(8,128)}) fusion(f32[1,768,768]{2,1,0:T(8,128)} %get-tuple-element.88, bf16[1,768,768]{2,1,0:T(8,128)(2,1)} %get-tuple-element.89, f32[1,768,768]{2,1,0:T(8,128)} %get-tuple-element.86, bf16[1,768,768]{2,1,0:T(8,128)(2,1)S(1)} %copy-done.15), kind=kLoop, calls=%fused_computation.2 | loop fusion | flops 2359296 | bytes 11796480 | tf_op jit(solution)/shard_map/add | solution.py:1997
  300.3 0.1 fusion.16
  300.4 0.1 squeeze.39
  300.5 0.1 squeeze.40
  300.6 0.6 convert_reduce_fusion.3
  301.2 0.7 convert_reduce_fusion
  301.9 0.6 maximum_convert_fusion.2
  302.5 0.6 reshape.149
  303.1 0.6 maximum_convert_fusion.1
  303.8 0.1 maximum_convert_fusion
  303.9 0.7 slice.96
  304.6 0.8 slice_bitcast_fusion
  305.4 0.2 fusion.15
  305.6 1.4 copy-done.10
  307.4 0.2 constant_dynamic-update-slice_fusion.1
  307.6 0.2 constant_dynamic-update-slice_fusion
  307.7 5.0 %convert_element_type.40 = f32[768,3072]{1,0:T(8,128)} convert(bf16[768,3072]{1,0:T(8,128)(2,1)S(1)} %constant_dynamic-update-slice_fusion) | non-fusion elementwise | flops 2359296 | bytes 14155776 | tf_op jit(solution)/shard_map/convert_element_type | solution.py:2009
  312.8 2.7 bitcast_convert_fusion
  315.5 0.9 copy.45
  (27 shorter events, 0.3 us)
Async XLA Ops:
  1.3 0.6 copy-start.21
  70.3 58.8 %copy-start.7 = (f32[256,768]{1,0:T(8,128)S(1)}, f32[256,768]{1,0:T(8,128)}, u32[]{:S(2)}) copy-start(f32[256,768]{1,0:T(8,128)} %get-tuple-element.53) | copy-start | bytes 2359300
  70.3 58.8 %copy-start.20 = (f32[768]{0:T(1024)S(1)}, f32[768]{0:T(1024)}, u32[]{:S(2)}) copy-start(f32[768]{0:T(1024)} %expert_norm_all_ref.1) | copy-start | bytes 9220
  129.0 2.7 copy-start.13
  129.1 2.9 copy-start.12
  129.1 2.9 copy-start.14
  131.7 31.1 %slice-start = ((s8[4718592]{0:T(1024)(128)(4,1)}), s8[4194304]{0:T(1024)(128)(4,1)S(1)}, s32[]{:S(2)}) async-start(s8[4718592]{0:T(1024)(128)(4,1)} %bitcast.50), calls=%async_computation | async-start | bytes 8388608
  132.0 32.6 %copy-start.6 = (f32[256,768]{1,0:T(8,128)}, f32[256,768]{1,0:T(8,128)S(1)}, u32[]{:S(2)}) copy-start(f32[256,768]{1,0:T(8,128)S(1)} %multiply_add_fusion.grad_resid_ref) | copy-start | bytes 2359300
  132.0 4.4 %copy-start = (f32[256,1536]{1,0:T(8,128)S(1)}, f32[256,1536]{1,0:T(8,128)}, u32[]{:S(2)}) copy-start(f32[256,1536]{1,0:T(8,128)} %get-tuple-element.54.delta_ref) | copy-start | bytes 4718596
  132.0 4.3 %copy-start.2 = (f32[16,1536]{1,0:T(8,128)S(1)}, f32[16,1536]{1,0:T(8,128)}, u32[]{:S(2)}) copy-start(f32[16,1536]{1,0:T(8,128)} %decay_log_ref.3) | copy-start | bytes 294916
  132.0 4.3 %copy-start.4 = (f32[16,16,16]{2,1,0:T(8,128)S(1)}, f32[16,16,16]{2,1,0:T(8,128)}, u32[]{:S(2)}) copy-start(f32[16,16,16]{2,1,0:T(8,128)} %get-tuple-element.63.out_ref.out_cols_ref) | copy-start | bytes 49156
  132.0 30.8 %slice-start.1 = ((s8[4718592]{0:T(1024)(128)(4,1)}), s8[524288]{0:T(1024)(128)(4,1)S(1)}, s32[]{:S(2)}) async-start(s8[4718592]{0:T(1024)(128)(4,1)} %bitcast.50), calls=%async_computation.1 | async-start | bytes 1048576
  135.6 7.4 %copy-start.1 = (f32[256,1536]{1,0:T(8,128)}, f32[256,1536]{1,0:T(8,128)S(1)}, u32[]{:S(2)}) copy-start(f32[256,1536]{1,0:T(8,128)S(1)} %get-tuple-element.98.grad_ref.grad_scan_ref) | copy-start | bytes 4718596
  135.6 27.1 %copy-start.16 = (bf16[256,1536]{1,0:T(8,128)(2,1)}, bf16[256,1536]{1,0:T(8,128)(2,1)S(1)}, u32[]{:S(2)}) copy-start(bf16[256,1536]{1,0:T(8,128)(2,1)S(1)} %get-tuple-element.99.gate_slope_ref) | copy-start | bytes 2359300
  136.3 6.7 %copy-start.5 = (f32[2,1536]{1,0:T(2,128)S(1)}, f32[2,1536]{1,0:T(2,128)}, u32[]{:S(2)}) copy-start(f32[2,1536]{1,0:T(2,128)} %get-tuple-element.66.refs_1_) | copy-start | bytes 36868
  162.8 1.7 copy-start.3
  162.8 1.7 copy-start.19
  166.8 125.4 %copy-start.8 = (f32[256,768]{1,0:T(8,128)S(1)}, f32[256,768]{1,0:T(8,128)}, u32[]{:S(2)}) copy-start(f32[256,768]{1,0:T(8,128)} %get-tuple-element.53) | copy-start | bytes 2359300
  292.1 2.6 copy-start.15
  294.8 5.6 %copy-start.18 = (bf16[2,2,2,4,10,768]{5,4,3,2,1,0:T(8,128)(2,1)S(1)}, bf16[2,2,2,4,10,768]{5,4,3,2,1,0:T(8,128)(2,1)}, u32[]{:S(2)}) copy-start(bf16[2,2,2,4,10,768]{5,4,3,2,1,0:T(8,128)(2,1)} %get-tuple-element.82) | copy-start | bytes 1474564
  301.2 4.2 %copy-start.11 = (bf16[2,2,2,4,48,768]{5,4,3,2,1,0:T(8,128)(2,1)S(1)}, bf16[2,2,2,4,48,768]{5,4,3,2,1,0:T(8,128)(2,1)}, u32[]{:S(2)}) copy-start(bf16[2,2,2,4,48,768]{5,4,3,2,1,0:T(8,128)(2,1)} %get-tuple-element.84) | copy-start | bytes 7077892
  305.4 1.7 copy-start.10
  307.7 5.1 %copy-start.9 = (bf16[2,2,2,4,48,768]{5,4,3,2,1,0:T(8,128)(2,1)S(1)}, bf16[2,2,2,4,48,768]{5,4,3,2,1,0:T(8,128)(2,1)}, u32[]{:S(2)}) copy-start(bf16[2,2,2,4,48,768]{5,4,3,2,1,0:T(8,128)(2,1)} %get-tuple-element.85) | copy-start | bytes 7077892
  312.8 2.7 copy-start.17
